TPU v7x, 128 devices: a whole 4x4x4 slice. The times are simulated.
128 devices in a mesh: rep: 8 (over y, x_lo), seq: 16 (over z, x_hi, core).
Axes of the slice: x: 4 (x_hi: 2, x_lo: 2; x = x_hi * 2 + x_lo), y: 4, z: 4, core: 2. Of those that a mesh axis runs over, the one named last changes fastest.
Arguments:
- features: float32 [8, 3, 64, 65536], P('rep', None, None, 'seq'), may hold values from -6 to 6
- short_filter: float32 [3, 3, 64], replicated, may hold values from -3 to 3
- long_filter: float32 [64, 65536], P('seq', 'rep'), may hold values from -4 to 4
- skip_gain: float32 [64], P('seq'), may hold values from -4 to 4
- lengths: int32 [8], P('rep'), may hold values from 1 to 65536, as said below
Outputs:
- mixed: float32 [8, 64, 65536], P('rep', None, 'seq')
Inputs may be any that keep to these rules, and one draw needn't show every extreme that they name: `lengths`: one replica's length is exactly 65536.
All inputs are finite; a program needn't handle non-finite values.
Results may differ from a plain program's by a relative error of at most 0.00012.
Values sent between devices are 32-bit elements; how exact they have to be, the bound alone decides.
No kernel may reach another device: no remote copies, remote signals or barrier semaphores. Data moves between devices by JAX's collectives and lax.ppermute only.
A program may use at most 320 MiB of HBM per device.

v0:
```python
import math

import jax
import jax.numpy as jnp
from jax import lax
from jax.sharding import PartitionSpec as P

FFT_ROWS = 256


HIGH = lax.Precision.HIGHEST


def from_behind(block, axis, distance):
    devices = range(lax.axis_size(axis))
    route = [(i - distance, i) for i in devices if i - distance in devices]
    return lax.ppermute(block, axis, route)


def angle_table(row_index, col_count, modulus):
    cols = lax.iota(jnp.int32, col_count)
    product = row_index[:, None] * cols[None, :] % modulus
    return product.astype(jnp.float32) * (2.0 * math.pi / modulus)


def padded_to(signal, length):
    return jnp.pad(signal, ((0, 0), (0, length - signal.shape[1])))


def forward(signal, rows_count, cols_count, freq_rows):
    blocks = signal.reshape(signal.shape[0], rows_count, cols_count)
    first_angle = angle_table(freq_rows, rows_count, rows_count)
    section_real = jnp.einsum("kn,cnm->ckm", jnp.cos(first_angle), blocks, precision=HIGH)
    section_imag = -jnp.einsum("kn,cnm->ckm", jnp.sin(first_angle), blocks, precision=HIGH)
    twist = angle_table(freq_rows, cols_count, rows_count * cols_count)
    twist_real = jnp.cos(twist)
    twist_imag = -jnp.sin(twist)
    turned_real = section_real * twist_real - section_imag * twist_imag
    turned_imag = section_real * twist_imag + section_imag * twist_real
    last_angle = angle_table(lax.iota(jnp.int32, cols_count), cols_count, cols_count)
    last_real = jnp.cos(last_angle)
    last_imag = -jnp.sin(last_angle)
    spec_real = jnp.einsum("ckn,nm->ckm", turned_real, last_real, precision=HIGH) - jnp.einsum(
        "ckn,nm->ckm", turned_imag, last_imag, precision=HIGH
    )
    spec_imag = jnp.einsum("ckn,nm->ckm", turned_real, last_imag, precision=HIGH) + jnp.einsum(
        "ckn,nm->ckm", turned_imag, last_real, precision=HIGH
    )
    return (spec_real, spec_imag)


def inverse(spec_real, spec_imag, rows_count, cols_count):
    last_angle = angle_table(lax.iota(jnp.int32, cols_count), cols_count, cols_count)
    back_real = jnp.cos(last_angle)
    back_imag = jnp.sin(last_angle)
    mid_real = jnp.einsum("ckn,nm->ckm", spec_real, back_real, precision=HIGH) - jnp.einsum(
        "ckn,nm->ckm", spec_imag, back_imag, precision=HIGH
    )
    mid_imag = jnp.einsum("ckn,nm->ckm", spec_real, back_imag, precision=HIGH) + jnp.einsum(
        "ckn,nm->ckm", spec_imag, back_real, precision=HIGH
    )
    twist = angle_table(lax.iota(jnp.int32, rows_count), cols_count, rows_count * cols_count)
    twist_real = jnp.cos(twist)
    twist_imag = jnp.sin(twist)
    turned_real = mid_real * twist_real - mid_imag * twist_imag
    turned_imag = mid_real * twist_imag + mid_imag * twist_real
    first_angle = angle_table(lax.iota(jnp.int32, rows_count), rows_count, rows_count)
    result = jnp.einsum(
        "nk,ckm->cnm", jnp.cos(first_angle), turned_real, precision=HIGH
    ) - jnp.einsum("nk,ckm->cnm", jnp.sin(first_angle), turned_imag, precision=HIGH)
    result = result / (rows_count * cols_count)
    return result.reshape(result.shape[0], rows_count * cols_count)


def spectral_product(left_real, left_imag, right_real, right_imag):
    return (
        left_real * right_real - left_imag * right_imag,
        left_real * right_imag + left_imag * right_real,
    )


def body(features, short_filter, long_filter, skip_gain, lengths):
    seq_dev = features.shape[3]
    n_seq = lax.axis_size("seq")
    longest = seq_dev * n_seq
    half_len = longest // 2
    full_cols = 2 * longest // FFT_ROWS
    half_cols = full_cols // 2
    every_row = lax.iota(jnp.int32, FFT_ROWS)
    tail = features[..., seq_dev - 2 :]
    before = from_behind(tail, "seq", 1)
    extended = jnp.concatenate([before, features], axis=3)
    featured = sum(
        (
            short_filter[:, lag_index, :][None, :, :, None]
            * extended[..., 2 - lag_index : 2 - lag_index + seq_dev]
            for lag_index in range(3)
        )
    )
    places = lax.axis_index("seq") * seq_dev + lax.iota(jnp.int32, seq_dev)
    valid_mask = (places < lengths[0]).astype(jnp.float32)
    gated = featured[:, 1] * featured[:, 2] * valid_mask
    channel_rows = lax.all_to_all(gated, "seq", split_axis=1, concat_axis=2, tiled=True)[0]
    filter_full = lax.all_gather(long_filter, "rep", axis=1, tiled=True)
    filter_long = padded_to(filter_full, 2 * longest)
    filter_short = padded_to(filter_full[:, :half_len], longest)
    long_real, long_imag = forward(filter_long, FFT_ROWS, full_cols, every_row)
    short_real, short_imag = forward(filter_short, FFT_ROWS, half_cols, every_row)

    def long_conv(rows, kernel_real, kernel_imag):
        signal_real, signal_imag = forward(
            padded_to(rows, 2 * longest), FFT_ROWS, full_cols, every_row
        )
        prod_real, prod_imag = spectral_product(signal_real, signal_imag, kernel_real, kernel_imag)
        return inverse(prod_real, prod_imag, FFT_ROWS, full_cols)[:, :longest]

    def short_conv(rows):
        signal_real, signal_imag = forward(
            padded_to(rows[:, :half_len], longest), FFT_ROWS, half_cols, every_row
        )
        prod_real, prod_imag = spectral_product(signal_real, signal_imag, short_real, short_imag)
        return padded_to(inverse(prod_real, prod_imag, FFT_ROWS, half_cols)[:, :half_len], longest)

    def long_branch():
        return long_conv(channel_rows, long_real, long_imag)

    def short_branch():
        return short_conv(channel_rows)

    convolved = lax.cond(lengths[0] <= half_len, short_branch, long_branch)
    convolved = convolved + skip_gain[:, None] * channel_rows
    returned = lax.all_to_all(convolved[None], "seq", split_axis=2, concat_axis=1, tiled=True)
    return featured[:, 0] * returned * valid_mask


def solution(mesh):
    return jax.shard_map(
        body,
        mesh=mesh,
        in_specs=(P("rep", None, None, "seq"), P(), P("seq", "rep"), P("seq"), P("rep")),
        out_specs=P("rep", None, "seq"),
        check_vma=False,
    )
```

profile of v0, /device:TPU:2, one launch (start us, length us, event | category | flops | bytes accessed | tf_op | source)
XLA Modules:
  0.0 790.2 jit_solution(12073721462881868055)
XLA Ops:
  6.5 5.1 copy.102
  11.9 1.7 collective-permute-start
  14.6 14.4 %fusion.357 = f32[1,3,64,4096]{3,0,2,1:T(1,128)S(1)} fusion(f32[1,3,64,4096]{3,0,2,1:T(1,128)S(1)} %copy.102, f32[1,3,64,2]{3,0,2,1:T(1,128)S(1)} %collective-permute-done, f32[3,64]{1,0:T(4,128)S(1)} %get-tuple-element.108, f32[3,64]{1,0:T(4,128)S(1)} %get-tuple-element.109, f32[3,64]{1,0:T(4,128)S(1)} %bitcast.239), kind=kLoop, calls=%fused_computation.398 | loop fusion | flops 5505024 | bytes 6295296 | tf_op jit(solution)/shard_map/add | solution.py:93
  30.7 2.5 fusion.373
  33.2 11.7 %all-to-all-start = ((f32[1,64,4096]{2,0,1:T(1,128)}), f32[1,64,4096]{2,0,1:T(1,128)S(1)}, u32[]{:S(2)}, u32[]{:S(2)}) async-start(f32[1,64,4096]{2,0,1:T(1,128)} %fusion.373), calls=%async_computation | async-start | bytes 2097152 | tf_op jit(solution)/shard_map/all_to_all | solution.py:103
  47.2 2.9 sine_negate_fusion.3
  50.1 16.9 %all-to-all-done = f32[1,64,4096]{2,0,1:T(1,128)S(1)} async-done(((f32[1,64,4096]{2,0,1:T(1,128)}), f32[1,64,4096]{2,0,1:T(1,128)S(1)}, u32[]{:S(2)}, u32[]{:S(2)}) %all-to-all-start) | async-done | bytes 1048608 | tf_op jit(solution)/shard_map/all_to_all | solution.py:103
  67.0 16.8 %copy.105 = f32[1,4,16,4096]{1,3,2,0:T(8,128)} copy(f32[1,4,16,4096]{3,0,1,2:T(1,128)S(1)} %bitcast.236) | data formatting | bytes 2097152 | tf_op jit(solution)/shard_map/all_to_all | solution.py:103
  85.3 4.7 fusion.358
  90.1 4.7 fusion.360
  94.8 7.9 fusion.376
  102.7 9.4 %fusion.378 = f32[4,256,512]{2,1,0:T(8,128)} fusion(f32[4,512,256]{2,1,0:T(8,128)S(1)} %fusion.360, f32[4,512,256]{2,1,0:T(8,128)S(1)} %fusion.358, f32[256,512]{0,1:T(8,128)S(1)} %copy-done.13, f32[256,512]{0,1:T(8,128)S(1)} %copy-done.14), kind=kOutput, calls=%fused_computation.430 | convolution fusion | flops 3227254784 | bytes 7340032 | tf_op jit(solution)/shard_map/ckn,nm->ckm/dot_general | solution.py:43
  112.1 8.9 %fusion.380 = f32[4,256,512]{2,1,0:T(8,128)} fusion(f32[4,512,256]{2,1,0:T(8,128)S(1)} %fusion.360, f32[4,512,256]{2,1,0:T(8,128)S(1)} %fusion.358, f32[256,512]{0,1:T(8,128)S(1)} %copy-done.13, f32[256,512]{0,1:T(8,128)S(1)} %copy-done.14), kind=kOutput, calls=%fused_computation.432 | convolution fusion | flops 3226992640 | bytes 7340032 | tf_op jit(solution)/shard_map/ckn,nm->ckm/dot_general | solution.py:46
  121.1 9.1 %fusion.382 = f32[4,256,512]{2,1,0:T(8,128)} fusion(f32[4,512,256]{2,1,0:T(8,128)S(1)} %fusion.360, f32[4,512,256]{2,1,0:T(8,128)S(1)} %fusion.358, f32[256,512]{0,1:T(8,128)S(1)} %copy-done.13, f32[256,512]{0,1:T(8,128)S(1)} %copy-done.14), kind=kOutput, calls=%fused_computation.434 | convolution fusion | flops 3226992640 | bytes 7340032 | tf_op jit(solution)/shard_map/ckn,nm->ckm/dot_general | solution.py:43
  130.5 2.7 convolution_bitcast_fusion.1
  133.3 2.7 fusion.366
  136.0 4.0 fusion.404
  139.9 3.7 fusion.406
  143.7 3.7 fusion.410
  147.3 3.7 fusion.412
  151.1 155.0 %conditional.1 = (f32[4,65536]{0,1:T(8,128)}) conditional(s32[]{:T(128)} %convert_element_type.197, (f32[4,65536]{0,1:T(8,128)}, s32[256]{0:T(256)S(1)}, s32[256]{0:T(256)S(1)}, s32[256]{0:T(256)S(1)}, s32[256]{0:T(256)S(1)}, /*index=5*/s32[256]{0:T(256)S(1)}, s32[256]{0:T(256)S(1)}, f32[4,256,512]{2,1,0:T(8,128)}, f32[4,256,512]{2,1,0:T(8,128)}, ...), branch_computations={%region_0.1_spmd, %region_1.2_spmd} | conditional | flops 32275955712 | bytes 148904064 | solution.py:130
  151.1 18.4 %copy.120 = f32[4,65536]{1,0:T(4,128)S(1)} copy(f32[4,65536]{0,1:T(8,128)} %get-tuple-element.68) | data formatting | bytes 2097152 | tf_op jit(solution)/shard_map
  169.8 4.7 fusion
  174.5 4.7 fusion.2
  179.3 4.0 fusion.45
  183.3 7.5 fusion.31
  190.8 4.0 fusion.55
  194.8 7.6 convolution_subtract_fusion.1
  202.5 8.0 %fusion.24 = f32[4,256,512]{2,1,0:T(8,128)S(1)} fusion(f32[4,512,256]{2,1,0:T(8,128)S(1)} %fusion.2, f32[4,512,256]{2,1,0:T(8,128)S(1)} %fusion, f32[256,512]{0,1:T(8,128)S(1)} %get-tuple-element.94, f32[256,512]{0,1:T(8,128)S(1)} %get-tuple-element.93), kind=kOutput, calls=%fused_computation.36 | convolution fusion | flops 3227254784 | bytes 7340032 | tf_op jit(solution)/shard_map/cond/branch_0_fun/ckn,nm->ckm/dot_general | solution.py:46
  210.5 8.6 %multiply_add_fusion = (f32[4,256,512]{2,1,0:T(8,128)S(1)}, f32[4,256,512]{2,1,0:T(8,128)S(1)}) fusion(f32[4,256,512]{2,1,0:T(8,128)S(1)} %convolution_subtract_fusion.1, f32[4,256,512]{2,1,0:T(8,128)S(1)} %get-tuple-element.55, f32[4,256,512]{2,1,0:T(8,128)S(1)} %copy-done.11, f32[4,256,512]{2,1,0:T(8,128)S(1)} %copy-done.12, ...), kind=kOutput, calls=%fused_computation.19 | convolution fusion | flops 3231711232 | bytes 22020096 | tf_op jit(solution)/shard_map/cond/branch_0_fun/ckn,nm->ckm/dot_general | solution.py:46
  219.1 8.4 %fusion.28 = f32[4,256,512]{2,1,0:T(8,128)S(1)} fusion(f32[4,256,512]{2,1,0:T(8,128)S(1)} %get-tuple-element.92), kind=kOutput, calls=%fused_computation.40 | convolution fusion | flops 3224895488 | bytes 4194304 | tf_op jit(solution)/shard_map/cond/branch_0_fun/ckn,nm->ckm/dot_general | solution.py:56
  227.5 8.4 %convolution_subtract_fusion = f32[4,256,512]{2,1,0:T(8,128)S(1)} fusion(f32[4,256,512]{2,1,0:T(8,128)S(1)} %fusion.28, f32[4,256,512]{2,1,0:T(8,128)S(1)} %get-tuple-element.91), kind=kOutput, calls=%fused_computation.24 | convolution fusion | flops 3225419776 | bytes 6291456 | tf_op jit(solution)/shard_map/cond/branch_0_fun/ckn,nm->ckm/dot_general | solution.py:56
  236.0 8.6 %fusion.21 = f32[4,256,512]{2,1,0:T(8,128)S(1)} fusion(f32[4,256,512]{2,1,0:T(8,128)S(1)} %get-tuple-element.92), kind=kOutput, calls=%fused_computation.33 | convolution fusion | flops 3224895488 | bytes 4194304 | tf_op jit(solution)/shard_map/cond/branch_0_fun/ckn,nm->ckm/dot_general | solution.py:59
  244.6 8.6 %convolution_add_fusion = f32[4,256,512]{2,1,0:T(8,128)} fusion(f32[4,256,512]{2,1,0:T(8,128)S(1)} %fusion.21, f32[4,256,512]{2,1,0:T(8,128)S(1)} %get-tuple-element.91), kind=kOutput, calls=%fused_computation.23 | convolution fusion | flops 3225419776 | bytes 6291456 | tf_op jit(solution)/shard_map/cond/branch_0_fun/ckn,nm->ckm/dot_general | solution.py:59
  253.2 1.9 fusion.112
  255.3 3.0 fusion.111
  259.6 6.2 fusion.6
  265.8 5.9 multiply_bitcast_fusion
  271.7 1.9 copy.88
  275.1 16.1 %copy.153 = f32[4,65536]{0,1:T(8,128)} copy(f32[4,65536]{1,0:T(4,128)S(1)} %slice.45) | data formatting | bytes 2097152 | tf_op jit(solution)/shard_map/cond | solution.py:130
  306.1 33.3 %multiply_add_fusion.5 = f32[4,65536]{0,1:T(8,128)} fusion(f32[4,65536]{0,1:T(8,128)} %get-tuple-element.90, f32[4]{0:T(128)S(1)} %copy-done.20, f32[1,4,16,4096]{1,3,2,0:T(8,128)} %copy.105), kind=kLoop, calls=%fused_computation.392 | loop fusion | flops 524288 | bytes 3145744 | tf_op jit(solution)/shard_map/add | solution.py:131
  339.9 291.0 %reduce = f32[65536,4]{1,0:T(8,128)} reduce(f32[65536,1,4]{2,1,0:T(1,128)} %bitcast.224, f32[]{:T(128)} %broadcast.842), dimensions={1}, to_apply=%bitcast.201.reduce_sub_computation | reduce | bytes 2097156
  630.9 29.1 %reshape.387 = f32[16,1,16384]{2,1,0:T(1,128)S(1)} reshape(f32[65536,4]{1,0:T(8,128)} %reduce) | data formatting | bytes 2097152
  660.0 20.9 %all_to_all.33 = f32[16,1,16384]{2,1,0:T(1,128)S(1)} all-to-all(f32[16,1,16384]{2,1,0:T(1,128)S(1)} %reshape.387), channel_id=1, replica_groups=mesh['rep'=8,'seq'=16] {'seq'}, dimensions={0} | all-to-all | bytes 2097152 | tf_op jit(solution)/shard_map/all_to_all | solution.py:132
  680.9 3.1 reduce.1
  684.1 74.8 %reshape.388 = f32[65536,1,4]{2,1,0:T(1,128)} reshape(f32[16,16384]{1,0:T(8,128)S(1)} %reduce.1) | data formatting | bytes 2097152
  758.8 19.5 %copy.123 = f32[1,4,16,4096]{3,0,1,2:T(1,128)S(1)} copy(f32[1,4,16,4096]{1,3,2,0:T(8,128)} %bitcast.225) | data formatting | bytes 2097152 | tf_op jit(solution)/shard_map/all_to_all | solution.py:132
  778.3 2.9 fusion.375
  (50 shorter events, 11.5 us)
Async XLA Ops:
  6.5 7.2 copy-start.19
  6.5 77.2 %all-gather.2.cloned.1.call-start = ((), (), s32[]{:S(2)}) async-start(), calls=%async_computation.2 | async-start | bytes 1179648 | tf_op jit(solution)/shard_map/all_gather | solution.py:104
  11.9 2.7 collective-permute-start
  14.4 14.6 %copy-start.16 = (f32[4096]{0:T(1024)}, f32[4096]{0:T(1024)S(1)}, u32[]{:S(2)}) copy-start(f32[4096]{0:T(1024)S(1)} %fusion.441) | copy-start | bytes 49156
  29.1 1.6 copy-start.1
  33.2 33.8 %all-to-all-start = ((f32[1,64,4096]{2,0,1:T(1,128)}), f32[1,64,4096]{2,0,1:T(1,128)S(1)}, u32[]{:S(2)}, u32[]{:S(2)}) async-start(f32[1,64,4096]{2,0,1:T(1,128)} %fusion.373), calls=%async_computation | async-start | bytes 2097152 | tf_op jit(solution)/shard_map/all_to_all | solution.py:103
  90.1 4.7 copy-start.13
  90.1 4.7 copy-start.14
  121.1 9.1 %copy-start.2 = (f32[4,65536]{1,0:T(4,128)S(1)}, f32[4,65536]{1,0:T(4,128)}, u32[]{:S(2)}) copy-start(f32[4,65536]{1,0:T(4,128)} %all-gather.2.cloned.1.call-done) | copy-start | bytes 3145732
  121.1 9.1 %copy-start.18 = (pred[65536]{0:T(1024)(128)(4,1)S(1)}, pred[65536]{0:T(1024)(128)(4,1)}, u32[]{:S(2)}) copy-start(pred[65536]{0:T(1024)(128)(4,1)} %constant.188.clone.1) | copy-start | bytes 196612
  151.1 155.0 %copy-start.20 = (f32[4]{0:T(128)S(1)}, f32[4]{0:T(128)}, u32[]{:S(2)}) copy-start(f32[4]{0:T(128)} %param.10) | copy-start | bytes 52
  202.5 8.0 %copy-start.10 = (f32[4,256,512]{2,1,0:T(8,128)S(1)}, f32[4,256,512]{2,1,0:T(8,128)}, u32[]{:S(2)}) copy-start(f32[4,256,512]{2,1,0:T(8,128)} %get-tuple-element.54) | copy-start | bytes 6291460 | tf_op jit(solution)/shard_map/cond
  202.5 8.0 %copy-start.11 = (f32[4,256,512]{2,1,0:T(8,128)S(1)}, f32[4,256,512]{2,1,0:T(8,128)}, u32[]{:S(2)}) copy-start(f32[4,256,512]{2,1,0:T(8,128)} %get-tuple-element.56) | copy-start | bytes 6291460 | tf_op jit(solution)/shard_map/cond
  202.5 8.0 %copy-start.12 = (f32[4,256,512]{2,1,0:T(8,128)S(1)}, f32[4,256,512]{2,1,0:T(8,128)}, u32[]{:S(2)}) copy-start(f32[4,256,512]{2,1,0:T(8,128)} %get-tuple-element.53) | copy-start | bytes 6291460 | tf_op jit(solution)/shard_map/cond
  259.6 6.3 copy-start
  758.8 19.5 %copy-start.17 = (f32[4096]{0:T(1024)S(1)}, f32[4096]{0:T(1024)}, u32[]{:S(2)}) copy-start(f32[4096]{0:T(1024)} %copy-done.16) | copy-start | bytes 49156
Sparse Core Ops, SparseCore 0:
  13.8 46.5 all-gather.1
where the time goes:
time: 799 us; the launch traced here: 790 us
  other arithmetic  365 us (46%)
  local copies, waits for them, and re-layouts  191 us (24%)
  matrix products  153 us (19%)
  blocking collectives  20.9 us (3%)
  waiting for transfers between devices  17.1 us (2%)
  loops' own time  15.1 us (2%)
  between operations  14.8 us (2%)
  starting transfers between devices  13.5 us (2%)
    unnamed x1, other arithmetic  291 us
    unnamed x24, local copies, waits for them, and re-layouts  111 us
    add x1, other arithmetic, body(): convolved = convolved + skip_gain[:, None] * channel_rows  33.3 us
    dot_general x3, matrix products, forward(): jnp.einsum('ckn,nm->ckm', turned_imag, last_real, precision=HIGH)  21.2 us
    all_to_all x1, blocking collectives, body(): lax.all_to_all(convolved[None], 'seq', split_axis=2, concat_axis=1, tiled...  20.9 us
    dot_general x3, matrix products, forward(): jnp.einsum('ckn,nm->ckm', turned_imag, last_imag, precision=HIGH)  20.8 us
    dot_general x3, matrix products, forward(): jnp.einsum('ckn,nm->ckm', turned_real, last_real, precision=HIGH)  20.4 us
    dot_general x3, matrix products, forward(): jnp.einsum('ckn,nm->ckm', turned_real, last_imag, precision=HIGH)  19.8 us
  transfers between devices with their start and end apart: 3, of which 2 were waited for; matrix products, arithmetic and copies ran while one was open for 5% of the time, Pallas kernels for 0%

commit v1 on v0

v1 whole, which is shorter than its diff:
```python
import math

import jax
import jax.numpy as jnp
import ml_dtypes
import numpy as np
from jax import lax
from jax.experimental import pallas as pl
from jax.experimental.pallas import tpu as pltpu
from jax.sharding import Mesh
from jax.sharding import PartitionSpec as P

R = 256
N = R * R
BF = jnp.bfloat16
F32 = jnp.float32


def halves(table):
    high = table.astype(np.float32).astype(ml_dtypes.bfloat16)
    low = (table - high.astype(np.float64)).astype(np.float32).astype(ml_dtypes.bfloat16)
    return high, low


def tables():
    row = np.arange(R, dtype=np.float64)
    first = 2.0 * math.pi / R * np.outer(row + 0.25, row)
    outer = np.concatenate([np.cos(first), -np.sin(first)], axis=0)
    twist = 2.0 * math.pi / N * np.outer(row + 0.25, row)
    turn = np.stack([np.cos(twist), -np.sin(twist)]).astype(np.float32)
    last = 2.0 * math.pi / R * np.outer(row, row)
    inner = np.block([[np.cos(last), -np.sin(last)], [np.sin(last), np.cos(last)]])
    outer_high, outer_low = halves(outer)
    back_high, back_low = halves(outer.T.copy())
    inner_high, inner_low = halves(inner)
    inv_high, inv_low = halves(inner.T.copy())
    return (
        np.concatenate([outer_high, outer_low], axis=0),
        np.concatenate([back_high, back_low], axis=0),
        np.concatenate([inner_high, inner_low], axis=0),
        np.concatenate([inv_high, inv_low], axis=0),
        turn,
    )


def split(value):
    high = value.astype(BF)
    return high, (value - high.astype(F32)).astype(BF)


def dot(left, right):
    return jnp.dot(left, right, preferred_element_type=F32)


def wide_dot(left_high, left_low, right_high, right_low):
    return dot(left_high, right_high) + dot(left_low, right_high) + dot(left_high, right_low)


def to_spectrum(signal, outer_ref, inner_ref, turn_ref):
    high, low = split(signal)
    first = wide_dot(outer_ref[0 : 2 * R], outer_ref[2 * R : 4 * R], high, low)
    real, imag = first[0:R], first[R : 2 * R]
    turn_real, turn_imag = turn_ref[0], turn_ref[1]
    turned = jnp.concatenate(
        [real * turn_real - imag * turn_imag, real * turn_imag + imag * turn_real], axis=1
    )
    high, low = split(turned)
    spec = wide_dot(high, low, inner_ref[0 : 2 * R], inner_ref[2 * R : 4 * R])
    return spec[:, 0:R], spec[:, R : 2 * R]


def to_signal(real, imag, back_ref, inv_ref, turn_ref):
    high, low = split(jnp.concatenate([real, imag], axis=1))
    mid = wide_dot(high, low, inv_ref[0 : 2 * R], inv_ref[2 * R : 4 * R])
    real, imag = mid[:, 0:R], mid[:, R : 2 * R]
    turn_real, turn_imag = turn_ref[0], turn_ref[1]
    turned = jnp.concatenate(
        [real * turn_real + imag * turn_imag, imag * turn_real - real * turn_imag], axis=0
    )
    high, low = split(turned)
    return wide_dot(back_ref[0:R], back_ref[R : 2 * R], high, low)


def gate_kernel(length_ref, taps_ref, features_ref, gated_ref, query_ref, column_ref):
    step = pl.program_id(0)
    group = features_ref.shape[2]
    width = features_ref.shape[3]

    @pl.when(step == 0)
    def _():
        taps = jnp.concatenate([taps_ref[j] for j in range(3)], axis=0)
        padded = jnp.concatenate([taps, jnp.zeros((7, taps.shape[1]), F32)], axis=0)
        column_ref[:, 0:16] = padded.T

    limit = length_ref[0] - lax.axis_index("seq") * width
    lane = lax.broadcasted_iota(jnp.int32, (8, width), 1)
    near = lane[:, 0:128]
    for sub in range(group // 8):
        rows = pl.ds(pl.multiple_of(step * group + sub * 8, 8), 8)
        column = column_ref[rows, :]

        def stream(j):
            here = features_ref[0, j, sub * 8 : sub * 8 + 8, :]
            one = pltpu.roll(here, 1, 1)
            two = pltpu.roll(here, 2, 1)
            t0, t1, t2 = (column[:, 3 * j + i : 3 * j + i + 1] for i in range(3))
            value = t0 * here + t1 * jnp.where(lane < 1, 0.0, one) + t2 * jnp.where(lane < 2, 0.0, two)
            over = t1 * jnp.where(near < 1, one[:, 0:128], 0.0) + t2 * jnp.where(
                near < 2, two[:, 0:128], 0.0
            )
            return value, over

        valid = lane < limit
        query, _ = stream(0)
        query_ref[sub * 8 : sub * 8 + 8, :] = jnp.where(valid, query, 0.0)
        key, key_over = stream(1)
        value, value_over = stream(2)
        gated = jnp.where(valid, key * value, 0.0)
        edge = jnp.where(
            near < 2,
            key[:, 0:128],
            jnp.where(
                near < 4,
                pltpu.roll(value[:, 0:128], 2, 1),
                jnp.where(near < 6, pltpu.roll(key_over, 4, 1), pltpu.roll(value_over, 6, 1)),
            ),
        )
        for part in range(2):
            dest = sub * 2 + part
            for tile in range(width // 128):
                place, half = tile // 2, tile % 2
                gated_ref[dest, pl.ds(half * 16 + place, 4, stride=32), :] = gated[
                    4 * part : 4 * part + 4, tile * 128 : tile * 128 + 128
                ]
            gated_ref[dest, 128:132, :] = edge[4 * part : 4 * part + 4]
            gated_ref[dest, 132:136, :] = jnp.zeros((4, 128), F32)


def gate(lengths, short_filter, features):
    _, streams, channels, width = features.shape
    group = 16
    return pl.pallas_call(
        gate_kernel,
        grid=(channels // group,),
        in_specs=[
            pl.BlockSpec(memory_space=pltpu.SMEM),
            pl.BlockSpec(short_filter.shape, lambda i: (0, 0, 0)),
            pl.BlockSpec((1, streams, group, width), lambda i: (0, 0, i, 0)),
        ],
        out_specs=[
            pl.BlockSpec((group // 4, 136, 128), lambda i: (i, 0, 0)),
            pl.BlockSpec((group, width), lambda i: (i, 0)),
        ],
        out_shape=[
            jax.ShapeDtypeStruct((channels // 4, 136, 128), F32),
            jax.ShapeDtypeStruct((channels, width), F32),
        ],
        scratch_shapes=[pltpu.VMEM((channels, 128), F32)],
        compiler_params=pltpu.CompilerParams(vmem_limit_bytes=24 << 20),
        name="gate",
    )(lengths, short_filter, features)


def filter_kernel(skip_ref, filter_ref, outer_ref, inner_ref, turn_ref, spec_ref):
    for channel in range(4):
        taps = jnp.concatenate(
            [filter_ref[y, x, channel] for y in range(4) for x in range(2)], axis=0
        )
        real, imag = to_spectrum(taps, outer_ref, inner_ref, turn_ref)
        spec_ref[channel, 0] = (real + skip_ref[channel]) * (1.0 / N)
        spec_ref[channel, 1] = imag * (1.0 / N)


VM = pl.BlockSpec(memory_space=pltpu.VMEM)
SM = pl.BlockSpec(memory_space=pltpu.SMEM)


def filter_spectrum(skip_gain, filter_parts, consts):
    outer, _, inner, _, turn = consts
    return pl.pallas_call(
        filter_kernel,
        in_specs=[SM, VM, VM, VM, VM],
        out_specs=VM,
        out_shape=jax.ShapeDtypeStruct((4, 2, R, R), F32),
        compiler_params=pltpu.CompilerParams(vmem_limit_bytes=32 << 20),
        name="filter_spectrum",
    )(skip_gain, filter_parts, outer, inner, turn)


def conv_kernel(
    length_ref, moved_ref, spec_ref, outer_ref, back_ref, inner_ref, inv_ref, turn_ref, out_ref, signal_ref
):
    blocks = moved_ref.shape[0]
    width = N // blocks
    lane = lax.broadcasted_iota(jnp.int32, (blocks, 128), 1)
    block = lax.broadcasted_iota(jnp.int32, (blocks, 128), 0)
    inside = (lane < 2) & (block * width + lane < length_ref[0])
    for channel in range(4):
        for half in range(2):
            start = channel * 32 + half * 16
            signal_ref[:, half * 128 : half * 128 + 128] = moved_ref[:, start : start + 16, :].reshape(R, 128)
        edge = jnp.concatenate([moved_ref[b, 128 + channel : 129 + channel, :] for b in range(blocks)], axis=0)
        behind = jnp.where(block < 1, 0.0, pltpu.roll(edge, 1, 0))
        key = edge + pltpu.roll(behind, 124, 1)
        value = pltpu.roll(edge, 126, 1) + pltpu.roll(behind, 122, 1)
        mended = jnp.where(inside, key * value, 0.0)
        for b in range(blocks):
            row = signal_ref[16 * b : 16 * b + 1, 0:128]
            signal_ref[16 * b : 16 * b + 1, 0:128] = jnp.where(lane[0:1] < 2, mended[b : b + 1], row)
        real, imag = to_spectrum(signal_ref[...], outer_ref, inner_ref, turn_ref)
        spec_real, spec_imag = spec_ref[channel, 0], spec_ref[channel, 1]
        result = to_signal(
            real * spec_real - imag * spec_imag,
            real * spec_imag + imag * spec_real,
            back_ref,
            inv_ref,
            turn_ref,
        )
        for half in range(2):
            start = channel * 32 + half * 16
            out_ref[:, start : start + 16, :] = result[:, half * 128 : half * 128 + 128].reshape(blocks, 16, 128)


def convolve(lengths, moved, spec, consts):
    outer, back, inner, inv, turn = consts
    return pl.pallas_call(
        conv_kernel,
        in_specs=[SM] + [VM] * 7,
        out_specs=VM,
        out_shape=jax.ShapeDtypeStruct((moved.shape[0], 128, 128), F32),
        scratch_shapes=[pltpu.VMEM((R, R), F32)],
        compiler_params=pltpu.CompilerParams(vmem_limit_bytes=40 << 20),
        name="convolve",
    )(lengths, moved, spec, outer, back, inner, inv, turn)


def mix_kernel(length_ref, taps_ref, tail_ref, query_ref, back_ref, out_ref):
    group, width = query_ref.shape
    limit = length_ref[0] - lax.axis_index("seq") * width
    lane = lax.broadcasted_iota(jnp.int32, (8, 128), 1)
    for sub in range(group // 8):
        t1 = taps_ref[sub * 8 : sub * 8 + 8, 1:2]
        t2 = taps_ref[sub * 8 : sub * 8 + 8, 2:3]
        far = tail_ref[sub * 8 : sub * 8 + 8, 0:1]
        near = tail_ref[sub * 8 : sub * 8 + 8, 1:2]
        mend = jnp.where(lane == 0, t1 * near + t2 * far, jnp.where(lane == 1, t2 * near, 0.0))
        mend = jnp.where(lane < limit, mend, 0.0)
        for tile in range(width // 128):
            place, half = tile // 2, tile % 2
            query = query_ref[sub * 8 : sub * 8 + 8, tile * 128 : tile * 128 + 128]
            if tile == 0:
                query = query + mend
            parts = [
                back_ref[sub * 2 + part, pl.ds(half * 16 + place, 4, stride=32), :] for part in range(2)
            ]
            out_ref[0, sub * 8 : sub * 8 + 8, tile * 128 : tile * 128 + 128] = query * jnp.concatenate(
                parts, axis=0
            )


def mix(lengths, taps, tail, query, returned):
    channels, width = query.shape
    group = 16
    return pl.pallas_call(
        mix_kernel,
        grid=(channels // group,),
        in_specs=[
            SM,
            pl.BlockSpec((group, 3), lambda i: (i, 0)),
            pl.BlockSpec((group, 2), lambda i: (i, 0)),
            pl.BlockSpec((group, width), lambda i: (i, 0)),
            pl.BlockSpec((group // 4, 128, 128), lambda i: (i, 0, 0)),
        ],
        out_specs=pl.BlockSpec((1, group, width), lambda i: (0, i, 0)),
        out_shape=jax.ShapeDtypeStruct((1, channels, width), F32),
        compiler_params=pltpu.CompilerParams(vmem_limit_bytes=24 << 20),
        name="mix",
    )(lengths, taps, tail, query, returned)


def body(features, short_filter, long_filter, skip_gain, lengths):
    seq_dev = features.shape[3]
    n_seq = lax.axis_size("seq")
    consts = tuple(jnp.asarray(t) for t in tables())
    mine = long_filter.reshape(4, 32, R)
    other = lax.ppermute(mine, "x_lo", [(0, 1), (1, 0)])
    first = lax.axis_index("x_lo") == 0
    pair = jnp.stack([jnp.where(first, mine, other), jnp.where(first, other, mine)])
    filter_parts = lax.all_gather(pair, "y", axis=0, tiled=False)
    gated, query = gate(lengths, short_filter, features)
    moved = lax.all_to_all(gated, "seq", split_axis=0, concat_axis=0, tiled=True)
    tail = lax.ppermute(features[0, 0, :, seq_dev - 2 :], "seq", [(i, i + 1) for i in range(n_seq - 1)])
    spec = filter_spectrum(skip_gain, filter_parts, consts)
    convolved = convolve(lengths, moved, spec, consts)
    returned = lax.all_to_all(convolved, "seq", split_axis=0, concat_axis=0, tiled=True)
    return mix(lengths, short_filter[0].T, tail, query, returned)


def solution(mesh):
    devices = mesh.devices
    reps, seqs = devices.shape
    finer = Mesh(devices.reshape(reps // 2, 2, seqs), ("y", "x_lo", "seq"))
    rep = ("y", "x_lo")
    return jax.shard_map(
        body,
        mesh=finer,
        in_specs=(P(rep, None, None, "seq"), P(), P("seq", rep), P("seq"), P(rep)),
        out_specs=P(rep, None, "seq"),
        check_vma=False,
    )
```

time: 799 us -> 101 us (0.13)
  the two profiles are of different devices: /device:TPU:2 before, /device:TPU:0 now
where the time goes in v1:
time: 101 us; the launch traced here: 99.9 us
  waiting for transfers between devices  28.7 us (28%)
  Pallas kernels  19.8 us (20%)
  starting transfers between devices  19.1 us (19%)
  local copies, waits for them, and re-layouts  16.5 us (16%)
  between operations  14.1 us (14%)
  other arithmetic  1.66 us (2%)
    unnamed x32, local copies, waits for them, and re-layouts  15.7 us
    all_to_all x1, waiting for transfers between devices, body(): lax.all_to_all(convolved, 'seq', split_axis=0, concat_axis=0, tiled=True)  14 us
    all_gather x1, waiting for transfers between devices, body(): filter_parts = lax.all_gather(pair, 'y', axis=0, tiled=False)  10.4 us
    pallas_call x1, Pallas kernels, convolve(): pl.pallas_call(conv_kernel, in_specs=[SM] + [VM] * 7, out_specs=VM, out_s...  9.67 us
    all_to_all x1, starting transfers between devices, body(): lax.all_to_all(gated, 'seq', split_axis=0, concat_axis=0, tiled=True)  8.13 us
    all_to_all x1, starting transfers between devices, body(): lax.all_to_all(convolved, 'seq', split_axis=0, concat_axis=0, tiled=True)  7.04 us
    pallas_call x1, Pallas kernels, gate(): pl.pallas_call(gate_kernel, grid=(channels // group,), in_specs=[pl.Block...  4.08 us
    pallas_call x1, Pallas kernels, filter_spectrum(): pl.pallas_call(filter_kernel, in_specs=[SM, VM, VM, VM, VM], out_specs=VM...  3.78 us
  transfers between devices with their start and end apart: 5, of which 4 were waited for; matrix products, arithmetic and copies ran while one was open for 1% of the time, Pallas kernels for 8%

profile of v1, /device:TPU:0, one launch (start us, length us, event | category | flops | bytes accessed | tf_op | source)
XLA Modules:
  0.0 99.9 jit_solution(17515172133324044953)
XLA Ops:
  6.5 0.0 all-gather.3.cloned.1.call-start
  6.5 0.9 copy.25
  7.5 1.7 %collective-permute-start.1 = (f32[4,32,256]{2,1,0:T(8,128)S(1)}, f32[4,32,256]{2,1,0:T(8,128)S(1)}, u32[]{:S(2)}, u32[]{:S(2)}) collective-permute-start(f32[4,32,256]{2,1,0:T(8,128)S(1)} %bitcast.22), channel_id=1, source_target_pairs={{0,16},{16,0},{1,17},{17,1},{2,18},{18,2},{3,19},{19,3},{4,20},{20... | collective-permute-start | bytes 393224 | tf_op jit(solution)/shard_map/ppermute | solution.py:286
  9.1 3.5 %collective-permute-done.1 = f32[4,32,256]{2,1,0:T(8,128)S(1)} collective-permute-done((f32[4,32,256]{2,1,0:T(8,128)S(1)}, f32[4,32,256]{2,1,0:T(8,128)S(1)}, u32[]{:S(2)}, u32[]{:S(2)}) %collective-permute-start.1) | collective-permute-done | bytes 131104 | tf_op jit(solution)/shard_map/ppermute | solution.py:286
  12.6 0.9 select_bitcast_fusion.1
  13.6 0.7 pad_maximum_fusion
  14.3 0.0 all-gather.3.cloned.1.call-update
  15.0 0.0 copy-start.3
  15.0 1.9 %copy-done.3 = f32[1,3,64,4096]{3,2,1,0:T(8,128)S(1)} copy-done((f32[1,3,64,4096]{3,2,1,0:T(8,128)S(1)}, f32[1,3,64,4096]{3,2,1,0:T(8,128)}, u32[]{:S(2)}) %copy-start.3) | copy-done | bytes 3145752
  16.9 0.0 copy-start.13
  16.9 0.7 copy-done.13
  17.5 0.0 copy-start.14
  17.5 4.1 %gate.1 = (f32[16,136,128]{2,1,0:T(8,128)}, f32[64,4096]{1,0:T(8,128)S(1)}) custom-call(s32[1]{0:T(128)S(6)} %copy.26.length_ref, f32[3,3,64]{2,1,0:T(4,128)S(1)} %copy-done.13, f32[1,3,64,4096]{3,2,1,0:T(8,128)S(1)} %copy-done.3), custom_call_target="tpu_custom_call" | custom-call | tf_op jit(solution)/shard_map/gate/pallas_call | solution.py:142
  21.6 0.0 copy-start.9
  21.6 1.0 copy-done.9
  22.6 8.1 %all-to-all-start = ((f32[16,136,128]{2,1,0:T(8,128)}), f32[16,136,128]{2,1,0:T(8,128)S(1)}, u32[]{:S(2)}, u32[]{:S(2)}) async-start(f32[16,136,128]{2,1,0:T(8,128)} %get-tuple-element.8), calls=%async_computation | async-start | bytes 2228224 | tf_op jit(solution)/shard_map/all_to_all | solution.py:291
  30.7 10.4 %all-gather.3.cloned.1.call-done = f32[8,4,32,256]{3,2,1,0:T(8,128)} async-done(((f32[2,4,32,256]{3,2,1,0:T(8,128)}), f32[8,4,32,256]{3,2,1,0:T(8,128)}) %all-gather.3.cloned.1.call-update) | async-done | bytes 1048592 | tf_op jit(solution)/shard_map/all_gather | solution.py:289
  41.1 0.0 copy-done.14
  41.1 1.2 %copy-done.1 = bf16[1024,512]{1,0:T(8,128)(2,1)S(1)} copy-done((bf16[1024,512]{1,0:T(8,128)(2,1)S(1)}, bf16[1024,512]{1,0:T(8,128)(2,1)}, u32[]{:S(2)}) %copy-start.1) | copy-done | bytes 1048600
  42.3 0.0 copy-start.4
  42.3 1.0 %copy-done.4 = bf16[1024,256]{1,0:T(8,128)(2,1)S(1)} copy-done((bf16[1024,256]{1,0:T(8,128)(2,1)S(1)}, bf16[1024,256]{1,0:T(8,128)(2,1)}, u32[]{:S(2)}) %copy-start.4) | copy-done | bytes 524312
  43.4 0.0 copy-start.6
  43.4 1.0 %copy-done.6 = f32[2,256,256]{2,1,0:T(8,128)S(1)} copy-done((f32[2,256,256]{2,1,0:T(8,128)S(1)}, f32[2,256,256]{2,1,0:T(8,128)}, u32[]{:S(2)}) %copy-start.6) | copy-done | bytes 524312
  44.4 1.2 %copy-done.11 = f32[8,4,32,256]{3,2,1,0:T(8,128)S(1)} copy-done((f32[8,4,32,256]{3,2,1,0:T(8,128)S(1)}, f32[8,4,32,256]{3,2,1,0:T(8,128)}, u32[]{:S(2)}) %copy-start.11) | copy-done | bytes 1048600
  45.6 3.8 %filter_spectrum.1.spec_ref = f32[4,2,256,256]{3,2,1,0:T(8,128)S(1)} custom-call(f32[4]{0:T(128)S(1)} %copy-done.14, f32[4,2,4,32,256]{4,3,2,1,0:T(8,128)S(1)} %bitcast.18, bf16[1024,256]{1,0:T(8,128)(2,1)S(1)} %copy-done.4, bf16[1024,512]{1,0:T(8,128)(2,1)S(1)} %copy-done.1, f32[2,256,256]{2,1,0:T(8,128)S(1)} %copy-done.6), custom_call_target="tpu_custom_call" | custom-call | tf_op jit(solution)/shard_map/filter_spectrum/pallas_call | solution.py:180
  49.4 0.0 all-to-all-done.moved_ref
  49.5 0.0 copy-start.2
  49.5 1.2 %copy-done.2 = bf16[1024,512]{1,0:T(8,128)(2,1)S(1)} copy-done((bf16[1024,512]{1,0:T(8,128)(2,1)S(1)}, bf16[1024,512]{1,0:T(8,128)(2,1)}, u32[]{:S(2)}) %copy-start.2) | copy-done | bytes 1048600
  50.7 0.0 copy-start.5
  50.7 1.0 %copy-done.5 = bf16[1024,256]{1,0:T(8,128)(2,1)S(1)} copy-done((bf16[1024,256]{1,0:T(8,128)(2,1)S(1)}, bf16[1024,256]{1,0:T(8,128)(2,1)}, u32[]{:S(2)}) %copy-start.5) | copy-done | bytes 524312
  51.7 0.0 copy-start.7
  51.7 1.0 %copy-done.7 = f32[2,256,256]{2,1,0:T(8,128)S(1)} copy-done((f32[2,256,256]{2,1,0:T(8,128)S(1)}, f32[2,256,256]{2,1,0:T(8,128)}, u32[]{:S(2)}) %copy-start.7) | copy-done | bytes 524312
  52.8 0.0 copy-start.8
  52.8 1.2 %copy-done.8 = bf16[1024,512]{1,0:T(8,128)(2,1)S(1)} copy-done((bf16[1024,512]{1,0:T(8,128)(2,1)S(1)}, bf16[1024,512]{1,0:T(8,128)(2,1)}, u32[]{:S(2)}) %copy-start.8) | copy-done | bytes 1048600
  54.0 0.0 copy-start.12
  54.0 1.0 %copy-done.12 = bf16[512,512]{1,0:T(8,128)(2,1)S(1)} copy-done((bf16[512,512]{1,0:T(8,128)(2,1)S(1)}, bf16[512,512]{1,0:T(8,128)(2,1)}, u32[]{:S(2)}) %copy-start.12) | copy-done | bytes 524312
  55.0 9.7 %convolve.1 = f32[16,128,128]{2,1,0:T(8,128)S(1)} custom-call(s32[1]{0:T(128)S(6)} %copy.26.length_ref, f32[16,136,128]{2,1,0:T(8,128)S(1)} %all-to-all-done.moved_ref, f32[4,2,256,256]{3,2,1,0:T(8,128)S(1)} %filter_spectrum.1.spec_ref, bf16[1024,256]{1,0:T(8,128)(2,1)S(1)} %copy-done.5, bf16[512,512]{1,0:T(8,128)(2,1)S(1)} %copy-done.12, ...), custom_call_target="tpu_custom_call" | custom-call | tf_op jit(solution)/shard_map/convolve/pallas_call | solution.py:226
  64.7 0.0 copy-start
  64.7 1.0 %copy-done = f32[16,128,128]{2,1,0:T(8,128)} copy-done((f32[16,128,128]{2,1,0:T(8,128)}, f32[16,128,128]{2,1,0:T(8,128)S(1)}, u32[]{:S(2)}) %copy-start) | copy-done | bytes 1048600
  65.7 7.0 %all-to-all-start.1 = ((f32[16,128,128]{2,1,0:T(8,128)}), f32[16,128,128]{2,1,0:T(8,128)S(1)}, u32[]{:S(2)}, u32[]{:S(2)}) async-start(f32[16,128,128]{2,1,0:T(8,128)} %copy-done), calls=%async_computation.1 | async-start | bytes 2097152 | tf_op jit(solution)/shard_map/all_to_all | solution.py:295
  72.8 0.8 slice_bitcast_fusion
  73.6 2.3 %collective-permute-start = (f32[64,2]{1,0:T(8,128)S(1)}, f32[64,2]{1,0:T(8,128)S(1)}, u32[]{:S(2)}, u32[]{:S(2)}) collective-permute-start(f32[64,2]{1,0:T(8,128)S(1)} %slice_bitcast_fusion), channel_id=1, source_target_pairs={{0,1},{1,2},{2,3},{3,4},{4,5},{5,6},{6,7},{7,8},{8,9},{9,10},{10,1... | collective-permute-start | bytes 1544 | tf_op jit(solution)/shard_map/ppermute | solution.py:292
  75.9 0.0 slice-done
  75.9 0.1 copy.18
  76.0 0.7 collective-permute-done.tail_ref
  76.8 14.0 %all-to-all-done.1.back_ref = f32[16,128,128]{2,1,0:T(8,128)S(1)} async-done(((f32[16,128,128]{2,1,0:T(8,128)}), f32[16,128,128]{2,1,0:T(8,128)S(1)}, u32[]{:S(2)}, u32[]{:S(2)}) %all-to-all-start.1) | async-done | bytes 1048608 | tf_op jit(solution)/shard_map/all_to_all | solution.py:295
  90.8 0.0 copy-done.10
  90.8 2.3 %mix.1 = f32[1,64,4096]{2,1,0:T(8,128)} custom-call(s32[1]{0:T(128)S(6)} %copy.26.length_ref, f32[64,3]{1,0:T(8,128)S(1)} %bitcast.19, f32[64,2]{1,0:T(8,128)S(1)} %collective-permute-done.tail_ref, f32[64,4096]{1,0:T(8,128)S(1)} %copy-done.10, f32[16,128,128]{2,1,0:T(8,128)S(1)} %all-to-all-done.1.back_ref), custom_call_target="tpu_custom_call" | custom-call | tf_op jit(solution)/shard_map/mix/pallas_call | solution.py:264
  (4 shorter events, 0.0 us)
Async XLA Ops:
  6.5 34.5 %all-gather.3.cloned.1.call-start = ((), (), s32[]{:S(2)}) async-start(), calls=%async_computation.2 | async-start | bytes 1310720 | tf_op jit(solution)/shard_map/all_gather | solution.py:289
  7.5 5.2 %collective-permute-start.1 = (f32[4,32,256]{2,1,0:T(8,128)S(1)}, f32[4,32,256]{2,1,0:T(8,128)S(1)}, u32[]{:S(2)}, u32[]{:S(2)}) collective-permute-start(f32[4,32,256]{2,1,0:T(8,128)S(1)} %bitcast.22), channel_id=1, source_target_pairs={{0,16},{16,0},{1,17},{17,1},{2,18},{18,2},{3,19},{19,3},{4,20},{20... | collective-permute-start | bytes 393224 | tf_op jit(solution)/shard_map/ppermute | solution.py:286
  15.0 1.9 %copy-start.3 = (f32[1,3,64,4096]{3,2,1,0:T(8,128)S(1)}, f32[1,3,64,4096]{3,2,1,0:T(8,128)}, u32[]{:S(2)}) copy-start(f32[1,3,64,4096]{3,2,1,0:T(8,128)} %features_ref.1) | copy-start | bytes 9437188
  16.9 0.7 copy-start.13
  17.5 23.5 %copy-start.14 = (f32[4]{0:T(128)S(1)}, f32[4]{0:T(128)}, u32[]{:S(2)}) copy-start(f32[4]{0:T(128)} %skip_ref.1) | copy-start | bytes 52
  21.6 1.0 copy-start.9
  22.6 26.9 %all-to-all-start = ((f32[16,136,128]{2,1,0:T(8,128)}), f32[16,136,128]{2,1,0:T(8,128)S(1)}, u32[]{:S(2)}, u32[]{:S(2)}) async-start(f32[16,136,128]{2,1,0:T(8,128)} %get-tuple-element.8), calls=%async_computation | async-start | bytes 2228224 | tf_op jit(solution)/shard_map/all_to_all | solution.py:291
  41.1 1.2 %copy-start.1 = (bf16[1024,512]{1,0:T(8,128)(2,1)S(1)}, bf16[1024,512]{1,0:T(8,128)(2,1)}, u32[]{:S(2)}) copy-start(bf16[1024,512]{1,0:T(8,128)(2,1)} %constant.20.clone.inner_ref) | copy-start | bytes 3145732
  42.3 1.0 %copy-start.4 = (bf16[1024,256]{1,0:T(8,128)(2,1)S(1)}, bf16[1024,256]{1,0:T(8,128)(2,1)}, u32[]{:S(2)}) copy-start(bf16[1024,256]{1,0:T(8,128)(2,1)} %constant.18.clone.outer_ref) | copy-start | bytes 1572868
  43.4 1.0 %copy-start.6 = (f32[2,256,256]{2,1,0:T(8,128)S(1)}, f32[2,256,256]{2,1,0:T(8,128)}, u32[]{:S(2)}) copy-start(f32[2,256,256]{2,1,0:T(8,128)} %constant.22.clone.turn_ref) | copy-start | bytes 1572868
  44.4 1.2 %copy-start.11 = (f32[8,4,32,256]{3,2,1,0:T(8,128)S(1)}, f32[8,4,32,256]{3,2,1,0:T(8,128)}, u32[]{:S(2)}) copy-start(f32[8,4,32,256]{3,2,1,0:T(8,128)} %all-gather.3.cloned.1.call-done) | copy-start | bytes 3145732
  49.5 1.2 %copy-start.2 = (bf16[1024,512]{1,0:T(8,128)(2,1)S(1)}, bf16[1024,512]{1,0:T(8,128)(2,1)}, u32[]{:S(2)}) copy-start(bf16[1024,512]{1,0:T(8,128)(2,1)} %constant.20.clone.inner_ref) | copy-start | bytes 3145732
  50.7 1.0 %copy-start.5 = (bf16[1024,256]{1,0:T(8,128)(2,1)S(1)}, bf16[1024,256]{1,0:T(8,128)(2,1)}, u32[]{:S(2)}) copy-start(bf16[1024,256]{1,0:T(8,128)(2,1)} %constant.18.clone.outer_ref) | copy-start | bytes 1572868
  51.7 1.0 %copy-start.7 = (f32[2,256,256]{2,1,0:T(8,128)S(1)}, f32[2,256,256]{2,1,0:T(8,128)}, u32[]{:S(2)}) copy-start(f32[2,256,256]{2,1,0:T(8,128)} %constant.22.clone.turn_ref) | copy-start | bytes 1572868
  52.8 1.2 %copy-start.8 = (bf16[1024,512]{1,0:T(8,128)(2,1)S(1)}, bf16[1024,512]{1,0:T(8,128)(2,1)}, u32[]{:S(2)}) copy-start(bf16[1024,512]{1,0:T(8,128)(2,1)} %constant.21.clone.inv_ref) | copy-start | bytes 3145732
  54.0 1.0 %copy-start.12 = (bf16[512,512]{1,0:T(8,128)(2,1)S(1)}, bf16[512,512]{1,0:T(8,128)(2,1)}, u32[]{:S(2)}) copy-start(bf16[512,512]{1,0:T(8,128)(2,1)} %constant.19.clone.back_ref) | copy-start | bytes 1572868
  64.7 1.0 %copy-start = (f32[16,128,128]{2,1,0:T(8,128)}, f32[16,128,128]{2,1,0:T(8,128)S(1)}, u32[]{:S(2)}) copy-start(f32[16,128,128]{2,1,0:T(8,128)S(1)} %convolve.1) | copy-start | bytes 3145732
  65.7 10.2 %slice-start = ((f32[3,3,64]{2,1,0:T(4,128)}), f32[1,3,64]{2,1,0:T(4,128)S(1)}, s32[]{:S(2)}) async-start(f32[3,3,64]{2,1,0:T(4,128)} %taps_ref.1), calls=%async_computation.3 | async-start | bytes 4096 | tf_op jit(solution)/shard_map/slice | solution.py:296
  65.7 25.1 %copy-start.10 = (f32[64,4096]{1,0:T(8,128)S(1)}, f32[64,4096]{1,0:T(8,128)}, u32[]{:S(2)}) copy-start(f32[64,4096]{1,0:T(8,128)} %copy-done.9) | copy-start | bytes 3145732
  65.7 25.1 %all-to-all-start.1 = ((f32[16,128,128]{2,1,0:T(8,128)}), f32[16,128,128]{2,1,0:T(8,128)S(1)}, u32[]{:S(2)}, u32[]{:S(2)}) async-start(f32[16,128,128]{2,1,0:T(8,128)} %copy-done), calls=%async_computation.1 | async-start | bytes 2097152 | tf_op jit(solution)/shard_map/all_to_all | solution.py:295
  73.6 3.2 %collective-permute-start = (f32[64,2]{1,0:T(8,128)S(1)}, f32[64,2]{1,0:T(8,128)S(1)}, u32[]{:S(2)}, u32[]{:S(2)}) collective-permute-start(f32[64,2]{1,0:T(8,128)S(1)} %slice_bitcast_fusion), channel_id=1, source_target_pairs={{0,1},{1,2},{2,3},{3,4},{4,5},{5,6},{6,7},{7,8},{8,9},{9,10},{10,1... | collective-permute-start | bytes 1544 | tf_op jit(solution)/shard_map/ppermute | solution.py:292
Sparse Core Ops, SparseCore 0:
  14.4 26.6 all-gather.2

commit v2 on v0

v2 whole, which is shorter than its diff:
```python
import math

import jax
import jax.numpy as jnp
import ml_dtypes
import numpy as np
from jax import lax
from jax.experimental import pallas as pl
from jax.experimental.pallas import tpu as pltpu
from jax.sharding import Mesh
from jax.sharding import PartitionSpec as P

R = 256
N = R * R
BF = jnp.bfloat16
F32 = jnp.float32
SPAN = 36

VM = pl.BlockSpec(memory_space=pltpu.VMEM)
SM = pl.BlockSpec(memory_space=pltpu.SMEM)
HB = pl.BlockSpec(memory_space=pltpu.HBM)


def halves(table, axis):
    high = table.astype(np.float32).astype(ml_dtypes.bfloat16)
    low = (table - high.astype(np.float64)).astype(np.float32).astype(ml_dtypes.bfloat16)
    return np.concatenate([high, low], axis=axis)


def tables():
    row = np.arange(R, dtype=np.float64)
    first = 2.0 * math.pi / R * np.outer(row + 0.25, row)
    outer = np.concatenate([np.cos(first), -np.sin(first)], axis=0)
    twist = 2.0 * math.pi / N * np.outer(row + 0.25, row)
    turn = np.stack([np.cos(twist), -np.sin(twist)]).astype(np.float32)
    last = 2.0 * math.pi / R * np.outer(row, row)
    inner = np.block([[np.cos(last), -np.sin(last)], [np.sin(last), np.cos(last)]])
    return np.concatenate([halves(outer, 1), halves(outer.T, 0), halves(inner, 0)], axis=0), turn


TABLES = (
    ((2 * R, 3 * R), BF),
    ((R, 6 * R), BF),
    ((6 * R, 2 * R), BF),
)


def load_outer(table_hbm, outer_ref, sem):
    return [
        pltpu.make_async_copy(table_hbm.at[0 : 2 * R, :], outer_ref.at[:, 0 : 2 * R], sem.at[0]),
        pltpu.make_async_copy(table_hbm.at[0 : 2 * R, 0:R], outer_ref.at[:, 2 * R : 3 * R], sem.at[1]),
    ]


def load_back(table_hbm, back_ref, sem):
    high, low = slice(2 * R, 3 * R), slice(3 * R, 4 * R)
    return [
        pltpu.make_async_copy(table_hbm.at[rows, :], back_ref.at[:, 2 * R * i : 2 * R * (i + 1)], sem.at[2 + i])
        for i, rows in enumerate((high, low, high))
    ]


def load_inner(table_hbm, inner_ref, sem):
    high, both = slice(4 * R, 6 * R), slice(4 * R, 8 * R)
    return [
        pltpu.make_async_copy(table_hbm.at[high, :], inner_ref.at[0 : 2 * R, :], sem.at[5]),
        pltpu.make_async_copy(table_hbm.at[both, :], inner_ref.at[2 * R : 6 * R, :], sem.at[6]),
    ]


def start(copies):
    for copy in copies:
        copy.start()
    return copies


def finish(copies):
    for copy in copies:
        copy.wait()


def split(value):
    high = value.astype(BF)
    return high, (value - high.astype(F32)).astype(BF)


def dot(left, right):
    return jnp.dot(left, right, preferred_element_type=F32)


CHUNK = 16


def chunks():
    return [slice(i, i + CHUNK) for i in range(0, R, CHUNK)]


def put_column(ref, where, rows, value):
    high, low = split(value)
    size = ref.shape[-2] // 3
    for place, part in enumerate((high, high, low)):
        ref[where, rows.start + place * size : rows.stop + place * size, :] = part


def put_row(ref, first, rows, left, right):
    rows = slice(first + rows.start, first + rows.stop)
    left_high, left_low = split(left)
    right_high, right_low = split(right)
    for place, part in enumerate((left_high, right_high, left_low, right_low, left_high, right_high)):
        ref[rows, place * R : (place + 1) * R] = part


def outer_stage(case, column_ref, first_ref, outer_ref, turn_ref, row_ref, base):
    first_ref[...] = dot(outer_ref[...], column_ref[case])
    for rows in chunks():
        real, imag = first_ref[rows, :], first_ref[R + rows.start : R + rows.stop, :]
        turn_real, turn_imag = turn_ref[0, rows, :], turn_ref[1, rows, :]
        put_row(
            row_ref, base, rows, real * turn_real - imag * turn_imag, real * turn_imag + imag * turn_real
        )


def taps_columns(taps_ref, column_ref):
    taps = jnp.concatenate([taps_ref[j] for j in range(3)], axis=0)
    padded = jnp.concatenate([taps, jnp.zeros((7, taps.shape[1]), F32)], axis=0)
    column_ref[:, 0:16] = padded.T


def gate_kernel(length_ref, taps_ref, features_ref, out_ref, column_ref, in_ref, send_ref, in_sem, out_sem):
    width = features_ref.shape[3]
    parts = in_ref.shape[0]
    group = in_ref.shape[2]
    copies = [
        pltpu.make_async_copy(
            features_ref.at[0, pl.ds(1, 2), pl.ds(group * part, group), :], in_ref.at[part], in_sem.at[part]
        )
        for part in range(parts)
    ]
    for copy in copies:
        copy.start()
    taps_columns(taps_ref, column_ref)
    limit = length_ref[0] - lax.axis_index("seq") * width
    lane = lax.broadcasted_iota(jnp.int32, (8, width), 1)
    near = lane[:, 0:128]
    valid = lane < limit
    sends = []
    for part in range(parts):
        copies[part].wait()
        for sub in range(group // 8):
            channel = part * group + sub * 8
            column = column_ref[channel : channel + 8, :]

            def stream(j):
                here = in_ref[part, j - 1, sub * 8 : sub * 8 + 8, :]
                one = pltpu.roll(here, 1, 1)
                two = pltpu.roll(here, 2, 1)
                t0, t1, t2 = (column[:, 3 * j + i : 3 * j + i + 1] for i in range(3))
                value = t0 * here + t1 * jnp.where(lane < 1, 0.0, one) + t2 * jnp.where(lane < 2, 0.0, two)
                over = t1 * jnp.where(near < 1, one[:, 0:128], 0.0) + t2 * jnp.where(
                    near < 2, two[:, 0:128], 0.0
                )
                return value, over

            key, key_over = stream(1)
            value, value_over = stream(2)
            gated = jnp.where(valid, key * value, 0.0)
            for tile in range(width // 128):
                row = channel * SPAN + (tile % 2) * 16 + tile // 2
                send_ref[pl.ds(row, 8, stride=SPAN), :] = gated[:, tile * 128 : tile * 128 + 128]
            flag = jnp.where(near < limit, 1.0, 0.0)
            edge = jnp.where(near < 2, key[:, 0:128], 0.0)
            for place, item in ((1, value[:, 0:128]), (2, key_over), (3, value_over), (4, flag)):
                inside = (near >= 2 * place) & (near < 2 * place + 2)
                edge = jnp.where(inside, pltpu.roll(item, 2 * place, 1), edge)
            send_ref[pl.ds(channel * SPAN + 32, 8, stride=SPAN), :] = edge
        rows = pl.ds(part * group * SPAN, group * SPAN)
        there = pl.ds(part * group * SPAN, group * SPAN)
        send = pltpu.make_async_copy(send_ref.at[rows, :], out_ref.at[there, :], out_sem.at[part])
        send.start()
        sends.append(send)
    for send in sends:
        send.wait()


def gate(lengths, short_filter, features):
    _, _, channels, width = features.shape
    parts = 4
    return pl.pallas_call(
        gate_kernel,
        in_specs=[SM, VM, HB],
        out_specs=HB,
        out_shape=jax.ShapeDtypeStruct((channels * SPAN, 128), F32),
        scratch_shapes=[
            pltpu.VMEM((channels, 128), F32),
            pltpu.VMEM((parts, 2, channels // parts, width), F32),
            pltpu.VMEM((channels * SPAN, 128), F32),
            pltpu.SemaphoreType.DMA((parts,)),
            pltpu.SemaphoreType.DMA((parts,)),
        ],
        compiler_params=pltpu.CompilerParams(vmem_limit_bytes=60 << 20),
        cost_estimate=pl.CostEstimate(flops=1 << 20, bytes_accessed=12 << 20, transcendentals=0),
        name="gate",
    )(lengths, short_filter, features)


def pair_kernel(mine_ref, other_ref, out_ref):
    x = lax.axis_index("x_lo")
    mine = jnp.where(x == 0, mine_ref[0:2, :], mine_ref[2:4, :])
    other = jnp.where(x == 0, other_ref[0:2, :], other_ref[2:4, :])
    parts = (jnp.where(x == 0, mine, other), jnp.where(x == 0, other, mine))
    for channel in range(2):
        for place in range(2):
            for row in range(32):
                out_ref[channel, place, row : row + 1, :] = parts[place][
                    channel : channel + 1, row * R : row * R + R
                ]


def pair_up(mine, other):
    return pl.pallas_call(
        pair_kernel,
        in_specs=[VM, VM],
        out_specs=VM,
        out_shape=jax.ShapeDtypeStruct((2, 2, 32, R), F32),
        compiler_params=pltpu.CompilerParams(vmem_limit_bytes=4 << 20),
        name="pair_up",
    )(mine, other)


def filter_kernel(
    skip_ref, p0, p1, p2, p3, table_hbm, turn_hbm, spec_ref, turn_ref, column_ref, first_ref, row_ref, outer_ref, inner_ref, sem
):
    outer_copies = start(load_outer(table_hbm, outer_ref, sem))
    turn_copies = start([pltpu.make_async_copy(turn_hbm, turn_ref, sem.at[7])])
    inner_copies = start(load_inner(table_hbm, inner_ref, sem))
    y, x = lax.axis_index("y"), lax.axis_index("x_lo")
    for away, part in enumerate((p0, p1, p2, p3)):
        first = lax.rem(y + 4 - away, 4) * 64
        for channel in range(2):
            for place in range(2):
                for half in range(2):
                    high, low = split(part[channel, place, 16 * half : 16 * half + 16, :])
                    for third, piece in enumerate((high, high, low)):
                        at = pl.multiple_of(third * R + first + 32 * place + 16 * half, 16)
                        column_ref[channel, pl.ds(at, 16), :] = piece
    finish(outer_copies + turn_copies)
    for channel in range(2):
        outer_stage(channel, column_ref, first_ref.at[channel], outer_ref, turn_ref, row_ref, channel * R)
    finish(inner_copies)
    spec = dot(row_ref[...], inner_ref[...]) * (1.0 / N)
    for channel in range(2):
        skip = skip_ref[2 * x + channel] * (1.0 / N)
        spec_ref[channel, 0] = spec[channel * R : (channel + 1) * R, 0:R] + skip
        spec_ref[channel, 1] = spec[channel * R : (channel + 1) * R, R : 2 * R]


def filter_spectrum(skip_gain, parts, table, turn):
    return pl.pallas_call(
        filter_kernel,
        in_specs=[SM] + [VM] * 4 + [HB] * 2,
        out_specs=[VM] * 2,
        out_shape=[jax.ShapeDtypeStruct((2, 2, R, R), F32), jax.ShapeDtypeStruct(turn.shape, F32)],
        scratch_shapes=[
            pltpu.VMEM((2, 3 * R, R), BF),
            pltpu.VMEM((2, 2 * R, R), F32),
            pltpu.VMEM((2 * R, 6 * R), BF),
            pltpu.VMEM(*TABLES[0]),
            pltpu.VMEM(*TABLES[2]),
            pltpu.SemaphoreType.DMA((8,)),
        ],
        compiler_params=pltpu.CompilerParams(vmem_limit_bytes=24 << 20),
        name="filter_spectrum",
    )(skip_gain, *parts, table, turn)


def conv_kernel(
    moved_ref,
    spec_ref,
    turn_ref,
    table_hbm,
    out_hbm,
    column_ref,
    first_ref,
    row_ref,
    mid_ref,
    last_ref,
    result_ref,
    outer_ref,
    back_ref,
    inner_ref,
    sem,
    out_sem,
):
    outer_copies = start(load_outer(table_hbm, outer_ref, sem))
    inner_copies = start(load_inner(table_hbm, inner_ref, sem))
    back_copies = start(load_back(table_hbm, back_ref, sem))
    blocks = N // 4096
    lane = lax.broadcasted_iota(jnp.int32, (blocks, 128), 1)
    block = lax.broadcasted_iota(jnp.int32, (blocks, 128), 0)
    for case in range(4):
        rep, channel = case // 2, case % 2
        begin = channel * SPAN
        edge = jnp.concatenate(
            [moved_ref[2 * b + rep, begin + 32 : begin + 33, :] for b in range(blocks)], axis=0
        )
        behind = jnp.where(block < 1, 0.0, pltpu.roll(edge, 1, 0))
        key = edge + pltpu.roll(behind, 124, 1)
        value = pltpu.roll(edge, 126, 1) + pltpu.roll(behind, 122, 1)
        mended = key * value * pltpu.roll(edge, 120, 1)
        for b in range(blocks):
            left = moved_ref[2 * b + rep, begin : begin + 16, :]
            right = moved_ref[2 * b + rep, begin + 16 : begin + 32, :]
            left = jnp.where((block < 1) & (lane < 2), mended[b : b + 1], left)
            put_column(column_ref, case, slice(16 * b, 16 * b + 16), jnp.concatenate([left, right], axis=1))
    finish(outer_copies)
    for case in range(4):
        outer_stage(case, column_ref, first_ref.at[case], outer_ref, turn_ref, row_ref, case * R)
    finish(inner_copies)
    sends = []
    size = GROUP * R
    for group in range(4 // GROUP):
        every = slice(group * size, (group + 1) * size)
        mid_ref[every, :] = dot(row_ref[every, :], inner_ref[...])
        for case in range(group * GROUP, (group + 1) * GROUP):
            channel = case % 2
            for rows in chunks():
                here = slice(case * R + rows.start, case * R + rows.stop)
                real, imag = mid_ref[here, 0:R], mid_ref[here, R : 2 * R]
                spec_real, spec_imag = spec_ref[channel, 0, rows, :], spec_ref[channel, 1, rows, :]
                put_row(
                    row_ref,
                    case * R,
                    rows,
                    real * spec_imag + imag * spec_real,
                    real * spec_real - imag * spec_imag,
                )
    for group in range(4 // GROUP):
        every = slice(group * size, (group + 1) * size)
        mid_ref[every, :] = dot(row_ref[every, :], inner_ref[...])
        if group == 0:
            finish(back_copies)
        for case in range(group * GROUP, (group + 1) * GROUP):
            rep, channel = case // 2, case % 2
            for rows in chunks():
                here = slice(case * R + rows.start, case * R + rows.stop)
                imag, real = mid_ref[here, 0:R], mid_ref[here, R : 2 * R]
                turn_real, turn_imag = turn_ref[0, rows, :], turn_ref[1, rows, :]
                put_column(last_ref, case, rows, real * turn_real + imag * turn_imag)
                below = slice(R + rows.start, R + rows.stop)
                put_column(last_ref, case, below, imag * turn_real - real * turn_imag)
            result = dot(back_ref[...], last_ref[case])
            for half in range(2):
                result_ref[case, :, half * 16 : half * 16 + 16, :] = result[
                    :, half * 128 : half * 128 + 128
                ].reshape(blocks, 16, 128)
            sends += start(
                [
                    pltpu.make_async_copy(
                        result_ref.at[case],
                        out_hbm.reshape(16, 2, 64, 128).at[:, rep, pl.ds(channel * 32, 32), :],
                        out_sem.at[case],
                    )
                ]
            )
    finish(sends)


GROUP = 2


def convolve(moved, spec, turn, table):
    return pl.pallas_call(
        conv_kernel,
        in_specs=[VM] * 3 + [HB],
        out_specs=HB,
        out_shape=jax.ShapeDtypeStruct((32, 64, 128), F32),
        scratch_shapes=[
            pltpu.VMEM((4, 3 * R, R), BF),
            pltpu.VMEM((4, 2 * R, R), F32),
            pltpu.VMEM((4 * R, 6 * R), BF),
            pltpu.VMEM((4 * R, 2 * R), F32),
            pltpu.VMEM((4, 6 * R, R), BF),
            pltpu.VMEM((4, 16, 32, 128), F32),
        ]
        + [pltpu.VMEM(*table_like) for table_like in TABLES]
        + [pltpu.SemaphoreType.DMA((8,)), pltpu.SemaphoreType.DMA((4,))],
        compiler_params=pltpu.CompilerParams(vmem_limit_bytes=60 << 20),
        name="convolve",
    )(moved, spec, turn, table)


def query_kernel(length_ref, taps_ref, tail_ref, features_ref, out_ref, column_ref):
    group, width = out_ref.shape

    @pl.when(pl.program_id(0) == 0)
    def _():
        taps_columns(taps_ref, column_ref)

    limit = length_ref[0] - lax.axis_index("seq") * width
    lane = lax.broadcasted_iota(jnp.int32, (8, width), 1)
    near = lane[:, 0:128]
    for sub in range(group // 8):
        rows = pl.ds(pl.multiple_of(pl.program_id(0) * group + sub * 8, 8), 8)
        column, tail = column_ref[rows, :], tail_ref[rows, :]
        here = features_ref[sub * 8 : sub * 8 + 8, :]
        t0, t1, t2 = (column[:, i : i + 1] for i in range(3))
        one = jnp.where(lane < 1, 0.0, pltpu.roll(here, 1, 1))
        two = jnp.where(lane < 2, 0.0, pltpu.roll(here, 2, 1))
        value = t0 * here + t1 * one + t2 * two
        out_ref[sub * 8 : sub * 8 + 8, :] = jnp.where(lane < limit, value, 0.0)
        far, last = tail[:, 126:127], tail[:, 127:128]
        mend = jnp.where(near == 0, t1 * last + t2 * far, jnp.where(near == 1, t2 * last, 0.0))
        out_ref[sub * 8 : sub * 8 + 8, 0:128] = jnp.where(near < limit, value[:, 0:128] + mend, 0.0)


def query(lengths, short_filter, tail, features):
    _, streams, channels, width = features.shape
    group = 16
    return pl.pallas_call(
        query_kernel,
        grid=(channels // group,),
        in_specs=[SM, VM, VM, pl.BlockSpec((None, None, group, width), lambda i: (0, 0, i, 0))],
        out_specs=pl.BlockSpec((group, width), lambda i: (i, 0)),
        out_shape=jax.ShapeDtypeStruct((channels, width), F32),
        scratch_shapes=[pltpu.VMEM((channels, 128), F32)],
        compiler_params=pltpu.CompilerParams(vmem_limit_bytes=12 << 20),
        name="query",
    )(lengths, short_filter, tail, features)


def mix_kernel(query_hbm, back_hbm, out_hbm, query_ref, back_ref, out_ref, sem):
    channels, width = out_ref.shape
    parts = 4
    group = channels // parts
    loads = []
    for part in range(parts):
        rows, there = pl.ds(group * part, group), pl.ds(32 * group * part, 32 * group)
        loads.append(
            start(
                [
                    pltpu.make_async_copy(query_hbm.at[rows, :], query_ref.at[rows, :], sem.at[0, part]),
                    pltpu.make_async_copy(back_hbm.at[there, :], back_ref.at[there, :], sem.at[1, part]),
                ]
            )
        )
    sends = []
    for part in range(parts):
        finish(loads[part])
        for sub in range(group // 8):
            channel = part * group + sub * 8
            for tile in range(width // 128):
                row = channel * 32 + (tile % 2) * 16 + tile // 2
                lanes = slice(tile * 128, tile * 128 + 128)
                out_ref[channel : channel + 8, lanes] = (
                    query_ref[channel : channel + 8, lanes] * back_ref[pl.ds(row, 8, stride=32), :]
                )
        rows = pl.ds(group * part, group)
        sends += start([pltpu.make_async_copy(out_ref.at[rows, :], out_hbm.at[0, rows, :], sem.at[2, part])])
    finish(sends)


def mix(query, returned):
    return pl.pallas_call(
        mix_kernel,
        in_specs=[HB, HB],
        out_specs=HB,
        out_shape=jax.ShapeDtypeStruct((1,) + query.shape, F32),
        scratch_shapes=[
            pltpu.VMEM(query.shape, F32),
            pltpu.VMEM(returned.shape, F32),
            pltpu.VMEM(query.shape, F32),
            pltpu.SemaphoreType.DMA((3, 4)),
        ],
        compiler_params=pltpu.CompilerParams(vmem_limit_bytes=60 << 20),
        name="mix",
    )(query, returned)


def exchange(blocks):
    return lax.all_to_all(blocks, ("seq", "x_lo"), split_axis=0, concat_axis=0, tiled=True)


def body(features, short_filter, long_filter, skip_gain, lengths):
    seq_dev = features.shape[3]
    n_seq = lax.axis_size("seq")
    table, turn = (jnp.asarray(t) for t in tables())
    other = lax.ppermute(long_filter, "x_lo", [(0, 1), (1, 0)])
    gated = gate(lengths, short_filter, features)
    gated, other = lax.optimization_barrier((gated, other))
    moved = exchange(gated.reshape(2 * n_seq, 2 * SPAN, 128))
    pair = pair_up(long_filter, other)
    parts = [pair] + [
        lax.ppermute(pair, "y", [(i, (i + away) % 4) for i in range(4)]) for away in range(1, 4)
    ]
    spec, turn = filter_spectrum(skip_gain, parts, table, turn)
    convolved = convolve(moved, spec, turn, table)
    returned = exchange(convolved)
    tail = lax.ppermute(features[0, 0, :, seq_dev - 128 :], "seq", [(i, i + 1) for i in range(n_seq - 1)])
    return mix(query(lengths, short_filter, tail, features), returned.reshape(2 * n_seq * 64, 128))


def solution(mesh):
    devices = mesh.devices
    reps, seqs = devices.shape
    finer = Mesh(devices.reshape(reps // 2, 2, seqs), ("y", "x_lo", "seq"))
    rep = ("y", "x_lo")
    return jax.shard_map(
        body,
        mesh=finer,
        in_specs=(P(rep, None, None, "seq"), P(), P("seq", rep), P("seq"), P(rep)),
        out_specs=P(rep, None, "seq"),
        check_vma=False,
    )
```

time: 799 us -> 68.7 us (0.09)
  the two profiles are of different devices: /device:TPU:2 before, /device:TPU:0 now
where the time goes in v2:
time: 68.7 us; the launch traced here: 68.3 us
  starting transfers between devices  22.3 us (32%)
  waiting for transfers between devices  21.6 us (31%)
  Pallas kernels  20.8 us (30%)
  local copies, waits for them, and re-layouts  2.78 us (4%)
  between operations  0.82 us (1%)
    all_to_all x2, waiting for transfers between devices, exchange(): lax.all_to_all(blocks, ('seq', 'x_lo'), split_axis=0, concat_axis=0, tile...  15.8 us
    all_to_all x2, starting transfers between devices, exchange(): lax.all_to_all(blocks, ('seq', 'x_lo'), split_axis=0, concat_axis=0, tile...  12.8 us
    pallas_call x1, Pallas kernels, convolve(): pl.pallas_call(conv_kernel, in_specs=[VM] * 3 + [HB], out_specs=HB, out_s...  9.66 us
    ppermute x3, starting transfers between devices, body(): lax.ppermute(pair, 'y', [(i, (i + away) % 4) for i in range(4)])  5.89 us
    ppermute x3, waiting for transfers between devices, body(): lax.ppermute(pair, 'y', [(i, (i + away) % 4) for i in range(4)])  5.05 us
    pallas_call x1, Pallas kernels, gate(): pl.pallas_call(gate_kernel, in_specs=[SM, VM, HB], out_specs=HB, out_shap...  4.6 us
    unnamed x18, local copies, waits for them, and re-layouts  2.77 us
    pallas_call x1, Pallas kernels, filter_spectrum(): pl.pallas_call(filter_kernel, in_specs=[SM] + [VM] * 4 + [HB] * 2, out_sp...  2.59 us
  transfers between devices with their start and end apart: 7, of which 5 were waited for; matrix products, arithmetic and copies ran while one was open for 0% of the time, Pallas kernels for 13%

profile of v2, /device:TPU:0, one launch (start us, length us, event | category | flops | bytes accessed | tf_op | source)
XLA Modules:
  0.0 68.3 jit_solution(14791810354617789785)
XLA Ops:
  0.0 1.6 %collective-permute-start.1 = (f32[4,8192]{1,0:T(4,128)}, f32[4,8192]{1,0:T(4,128)S(1)}, u32[]{:S(2)}, u32[]{:S(2)}) collective-permute-start(f32[4,8192]{1,0:T(4,128)} %mine_ref.1), channel_id=1, source_target_pairs={{0,16},{16,0},{1,17},{17,1},{2,18},{18,2},{3,19},{19,3},{4,20},{20... | collective-permute-start | bytes 393224 | tf_op jit(solution)/shard_map/ppermute | solution.py:487
  2.2 0.0 copy-start.6
  2.2 4.6 %gate.1 = f32[2304,128]{1,0:T(8,128)} custom-call(s32[1]{0:T(128)S(6)} %copy.8.length_ref, f32[3,3,64]{2,1,0:T(4,128)} %taps_ref.3, f32[1,3,64,4096]{3,2,1,0:T(8,128)} %features_ref.3), custom_call_target="tpu_custom_call" | custom-call | flops 1048576 | bytes 12582912 | tf_op jit(solution)/shard_map/gate/pallas_call | solution.py:188
  6.8 0.0 copy-start.1
  6.9 0.0 copy-start.5
  6.9 0.0 copy-start.8
  6.9 0.0 collective-permute-done.1.other_ref
  6.9 8.1 %all-to-all-start = ((f32[32,72,128]{2,1,0:T(8,128)}), f32[32,72,128]{2,1,0:T(8,128)}, u32[]{:S(2)}, u32[]{:S(2)}) async-start(f32[32,72,128]{2,1,0:T(8,128)} %bitcast.4), calls=%async_computation | async-start | bytes 2359296 | tf_op jit(solution)/shard_map/all_to_all | solution.py:480
  15.0 0.0 copy-done.6
  15.0 0.1 pair_up.1.p0
  15.1 1.6 %collective-permute-start.2 = (f32[2,2,32,256]{3,2,1,0:T(8,128)S(1)}, f32[2,2,32,256]{3,2,1,0:T(8,128)S(1)}, u32[]{:S(2)}, u32[]{:S(2)}) collective-permute-start(f32[2,2,32,256]{3,2,1,0:T(8,128)S(1)} %pair_up.1.p0), channel_id=1, source_target_pairs={{0,32},{32,64},{64,96},{96,0},{1,33},{33,65},{65,97},{97,1},{2,34}... | collective-permute-start | bytes 393224 | tf_op jit(solution)/shard_map/ppermute | solution.py:493
  16.8 2.9 %collective-permute-start.3 = (f32[2,2,32,256]{3,2,1,0:T(8,128)S(1)}, f32[2,2,32,256]{3,2,1,0:T(8,128)S(1)}, u32[]{:S(2)}, u32[]{:S(2)}) collective-permute-start(f32[2,2,32,256]{3,2,1,0:T(8,128)S(1)} %pair_up.1.p0), channel_id=1, source_target_pairs={{0,64},{32,96},{64,0},{96,32},{1,65},{33,97},{65,1},{97,33},{2,66}... | collective-permute-start | bytes 393224 | tf_op jit(solution)/shard_map/ppermute | solution.py:493
  19.7 1.3 %collective-permute-start.4 = (f32[2,2,32,256]{3,2,1,0:T(8,128)S(1)}, f32[2,2,32,256]{3,2,1,0:T(8,128)S(1)}, u32[]{:S(2)}, u32[]{:S(2)}) collective-permute-start(f32[2,2,32,256]{3,2,1,0:T(8,128)S(1)} %pair_up.1.p0), channel_id=1, source_target_pairs={{0,96},{32,0},{64,32},{96,64},{1,97},{33,1},{65,33},{97,65},{2,98}... | collective-permute-start | bytes 393224 | tf_op jit(solution)/shard_map/ppermute | solution.py:493
  21.0 1.1 %collective-permute-done.2.p1 = f32[2,2,32,256]{3,2,1,0:T(8,128)S(1)} collective-permute-done((f32[2,2,32,256]{3,2,1,0:T(8,128)S(1)}, f32[2,2,32,256]{3,2,1,0:T(8,128)S(1)}, u32[]{:S(2)}, u32[]{:S(2)}) %collective-permute-start.2) | collective-permute-done | bytes 131104 | tf_op jit(solution)/shard_map/ppermute | solution.py:493
  22.1 4.0 %collective-permute-done.3.p2 = f32[2,2,32,256]{3,2,1,0:T(8,128)S(1)} collective-permute-done((f32[2,2,32,256]{3,2,1,0:T(8,128)S(1)}, f32[2,2,32,256]{3,2,1,0:T(8,128)S(1)}, u32[]{:S(2)}, u32[]{:S(2)}) %collective-permute-start.3) | collective-permute-done | bytes 131104 | tf_op jit(solution)/shard_map/ppermute | solution.py:493
  26.1 0.0 collective-permute-done.4.p3
  26.1 0.0 copy-done.1
  26.1 0.0 copy-done.5
  26.1 0.0 copy-done.8
  26.1 2.6 %filter_spectrum.1 = (f32[2,2,256,256]{3,2,1,0:T(8,128)S(1)}, f32[2,256,256]{2,1,0:T(8,128)S(1)}) custom-call(f32[4]{0:T(128)S(1)} %copy-done.8, f32[2,2,32,256]{3,2,1,0:T(8,128)S(1)} %pair_up.1.p0, f32[2,2,32,256]{3,2,1,0:T(8,128)S(1)} %collective-permute-done.2.p1, f32[2,2,32,256]{3,2,1,0:T(8,128)S(1)} %collective-permute-done.3.p2, ...), custom_call_target="tpu_custom_call" | custom-call | tf_op jit(solution)/shard_map/filter_spectrum/pallas_call | solution.py:258
  28.7 0.0 copy-start.3
  28.7 1.0 %copy-done.3 = f32[2,2,256,256]{3,2,1,0:T(8,128)} copy-done((f32[2,2,256,256]{3,2,1,0:T(8,128)}, f32[2,2,256,256]{3,2,1,0:T(8,128)S(1)}, u32[]{:S(2)}) %copy-start.3) | copy-done | bytes 1048600
  29.7 0.0 copy-start.4
  29.7 0.8 %copy-done.4 = f32[2,256,256]{2,1,0:T(8,128)} copy-done((f32[2,256,256]{2,1,0:T(8,128)}, f32[2,256,256]{2,1,0:T(8,128)S(1)}, u32[]{:S(2)}) %copy-start.4) | copy-done | bytes 524312
  30.5 3.5 %all-to-all-done.moved_ref = f32[32,72,128]{2,1,0:T(8,128)} async-done(((f32[32,72,128]{2,1,0:T(8,128)}), f32[32,72,128]{2,1,0:T(8,128)}, u32[]{:S(2)}, u32[]{:S(2)}) %all-to-all-start) | async-done | bytes 1179680 | tf_op jit(solution)/shard_map/all_to_all | solution.py:480
  33.9 0.0 copy-start
  33.9 9.7 %convolve.1 = f32[32,64,128]{2,1,0:T(8,128)} custom-call(f32[32,72,128]{2,1,0:T(8,128)} %all-to-all-done.moved_ref, f32[2,2,256,256]{3,2,1,0:T(8,128)} %copy-done.3, f32[2,256,256]{2,1,0:T(8,128)} %copy-done.4, bf16[2048,512]{1,0:T(8,128)(2,1)} %constant.4.clone.table_hbm), custom_call_target="tpu_custom_call" | custom-call | tf_op jit(solution)/shard_map/convolve/pallas_call | solution.py:372
  43.6 0.0 copy-start.7
  43.6 4.7 %all-to-all-start.1 = ((f32[32,64,128]{2,1,0:T(8,128)}), f32[32,64,128]{2,1,0:T(8,128)}, u32[]{:S(2)}, u32[]{:S(2)}) async-start(f32[32,64,128]{2,1,0:T(8,128)} %convolve.1), calls=%async_computation.1 | async-start | bytes 2097152 | tf_op jit(solution)/shard_map/all_to_all | solution.py:480
  48.3 0.0 copy-done
  48.3 2.0 %collective-permute-start = (f32[64,128]{1,0:T(8,128)S(1)}, f32[64,128]{1,0:T(8,128)S(1)}, u32[]{:S(2)}, u32[]{:S(2)}) collective-permute-start(f32[64,128]{1,0:T(8,128)S(1)} %slice_bitcast_fusion), channel_id=1, source_target_pairs={{0,1},{1,2},{2,3},{3,4},{4,5},{5,6},{6,7},{7,8},{8,9},{9,10},{10,1... | collective-permute-start | bytes 98312 | tf_op jit(solution)/shard_map/ppermute | solution.py:498
  50.4 0.8 %collective-permute-done.tail_ref = f32[64,128]{1,0:T(8,128)S(1)} collective-permute-done((f32[64,128]{1,0:T(8,128)S(1)}, f32[64,128]{1,0:T(8,128)S(1)}, u32[]{:S(2)}, u32[]{:S(2)}) %collective-permute-start) | collective-permute-done | bytes 32800 | tf_op jit(solution)/shard_map/ppermute | solution.py:498
  51.2 0.0 copy-done.7
  51.2 1.4 %query.1.query_hbm = f32[64,4096]{1,0:T(8,128)S(1)} custom-call(s32[1]{0:T(128)S(6)} %copy.8.length_ref, f32[3,3,64]{2,1,0:T(4,128)S(1)} %copy-done.7, f32[64,128]{1,0:T(8,128)S(1)} %collective-permute-done.tail_ref, f32[1,3,64,4096]{3,2,1,0:T(8,128)S(1)} %copy-done), custom_call_target="tpu_custom_call" | custom-call | tf_op jit(solution)/shard_map/query/pallas_call | solution.py:419
  52.6 0.0 copy-start.2
  52.6 1.0 %copy-done.2 = f32[64,4096]{1,0:T(8,128)} copy-done((f32[64,4096]{1,0:T(8,128)}, f32[64,4096]{1,0:T(8,128)S(1)}, u32[]{:S(2)}) %copy-start.2) | copy-done | bytes 1048600
  53.5 12.3 %all-to-all-done.1 = f32[32,64,128]{2,1,0:T(8,128)} async-done(((f32[32,64,128]{2,1,0:T(8,128)}), f32[32,64,128]{2,1,0:T(8,128)}, u32[]{:S(2)}, u32[]{:S(2)}) %all-to-all-start.1) | async-done | bytes 1048608 | tf_op jit(solution)/shard_map/all_to_all | solution.py:480
  65.8 2.5 %mix.1 = f32[1,64,4096]{2,1,0:T(8,128)} custom-call(f32[64,4096]{1,0:T(8,128)} %copy-done.2, f32[2048,128]{1,0:T(8,128)} %bitcast.2.back_hbm), custom_call_target="tpu_custom_call" | custom-call | tf_op jit(solution)/shard_map/mix/pallas_call | solution.py:463
  (1 shorter events, 0.0 us)
Async XLA Ops:
  0.0 6.9 %collective-permute-start.1 = (f32[4,8192]{1,0:T(4,128)}, f32[4,8192]{1,0:T(4,128)S(1)}, u32[]{:S(2)}, u32[]{:S(2)}) collective-permute-start(f32[4,8192]{1,0:T(4,128)} %mine_ref.1), channel_id=1, source_target_pairs={{0,16},{16,0},{1,17},{17,1},{2,18},{18,2},{3,19},{19,3},{4,20},{20... | collective-permute-start | bytes 393224 | tf_op jit(solution)/shard_map/ppermute | solution.py:487
  2.2 12.8 %copy-start.6 = (f32[4,8192]{1,0:T(4,128)S(1)}, f32[4,8192]{1,0:T(4,128)}, u32[]{:S(2)}) copy-start(f32[4,8192]{1,0:T(4,128)} %mine_ref.1) | copy-start | bytes 393220
  6.8 19.2 %copy-start.1 = (bf16[2048,512]{1,0:T(8,128)(2,1)S(1)}, bf16[2048,512]{1,0:T(8,128)(2,1)}, u32[]{:S(2)}) copy-start(bf16[2048,512]{1,0:T(8,128)(2,1)} %constant.4.clone.table_hbm) | copy-start | bytes 6291460
  6.9 19.2 %copy-start.5 = (f32[2,256,256]{2,1,0:T(8,128)S(1)}, f32[2,256,256]{2,1,0:T(8,128)}, u32[]{:S(2)}) copy-start(f32[2,256,256]{2,1,0:T(8,128)} %constant.5.clone.turn_hbm) | copy-start | bytes 1572868
  6.9 19.2 %copy-start.8 = (f32[4]{0:T(128)S(1)}, f32[4]{0:T(128)}, u32[]{:S(2)}) copy-start(f32[4]{0:T(128)} %skip_ref.1) | copy-start | bytes 52
  6.9 27.0 %all-to-all-start = ((f32[32,72,128]{2,1,0:T(8,128)}), f32[32,72,128]{2,1,0:T(8,128)}, u32[]{:S(2)}, u32[]{:S(2)}) async-start(f32[32,72,128]{2,1,0:T(8,128)} %bitcast.4), calls=%async_computation | async-start | bytes 2359296 | tf_op jit(solution)/shard_map/all_to_all | solution.py:480
  15.1 7.0 %collective-permute-start.2 = (f32[2,2,32,256]{3,2,1,0:T(8,128)S(1)}, f32[2,2,32,256]{3,2,1,0:T(8,128)S(1)}, u32[]{:S(2)}, u32[]{:S(2)}) collective-permute-start(f32[2,2,32,256]{3,2,1,0:T(8,128)S(1)} %pair_up.1.p0), channel_id=1, source_target_pairs={{0,32},{32,64},{64,96},{96,0},{1,33},{33,65},{65,97},{97,1},{2,34}... | collective-permute-start | bytes 393224 | tf_op jit(solution)/shard_map/ppermute | solution.py:493
  16.8 9.3 %collective-permute-start.3 = (f32[2,2,32,256]{3,2,1,0:T(8,128)S(1)}, f32[2,2,32,256]{3,2,1,0:T(8,128)S(1)}, u32[]{:S(2)}, u32[]{:S(2)}) collective-permute-start(f32[2,2,32,256]{3,2,1,0:T(8,128)S(1)} %pair_up.1.p0), channel_id=1, source_target_pairs={{0,64},{32,96},{64,0},{96,32},{1,65},{33,97},{65,1},{97,33},{2,66}... | collective-permute-start | bytes 393224 | tf_op jit(solution)/shard_map/ppermute | solution.py:493
  19.7 6.4 %collective-permute-start.4 = (f32[2,2,32,256]{3,2,1,0:T(8,128)S(1)}, f32[2,2,32,256]{3,2,1,0:T(8,128)S(1)}, u32[]{:S(2)}, u32[]{:S(2)}) collective-permute-start(f32[2,2,32,256]{3,2,1,0:T(8,128)S(1)} %pair_up.1.p0), channel_id=1, source_target_pairs={{0,96},{32,0},{64,32},{96,64},{1,97},{33,1},{65,33},{97,65},{2,98}... | collective-permute-start | bytes 393224 | tf_op jit(solution)/shard_map/ppermute | solution.py:493
  28.7 1.0 %copy-start.3 = (f32[2,2,256,256]{3,2,1,0:T(8,128)}, f32[2,2,256,256]{3,2,1,0:T(8,128)S(1)}, u32[]{:S(2)}) copy-start(f32[2,2,256,256]{3,2,1,0:T(8,128)S(1)} %get-tuple-element.11.spec_ref) | copy-start | bytes 3145732
  29.7 0.8 %copy-start.4 = (f32[2,256,256]{2,1,0:T(8,128)}, f32[2,256,256]{2,1,0:T(8,128)S(1)}, u32[]{:S(2)}) copy-start(f32[2,256,256]{2,1,0:T(8,128)S(1)} %get-tuple-element.12.turn_ref) | copy-start | bytes 1572868
  33.9 14.4 %copy-start = (f32[1,3,64,4096]{3,2,1,0:T(8,128)S(1)}, f32[1,3,64,4096]{3,2,1,0:T(8,128)}, u32[]{:S(2)}) copy-start(f32[1,3,64,4096]{3,2,1,0:T(8,128)} %features_ref.3) | copy-start | bytes 9437188
  43.6 7.6 %copy-start.7 = (f32[3,3,64]{2,1,0:T(4,128)S(1)}, f32[3,3,64]{2,1,0:T(4,128)}, u32[]{:S(2)}) copy-start(f32[3,3,64]{2,1,0:T(4,128)} %taps_ref.3) | copy-start | bytes 6916
  43.6 22.2 %all-to-all-start.1 = ((f32[32,64,128]{2,1,0:T(8,128)}), f32[32,64,128]{2,1,0:T(8,128)}, u32[]{:S(2)}, u32[]{:S(2)}) async-start(f32[32,64,128]{2,1,0:T(8,128)} %convolve.1), calls=%async_computation.1 | async-start | bytes 2097152 | tf_op jit(solution)/shard_map/all_to_all | solution.py:480
  48.3 2.8 %collective-permute-start = (f32[64,128]{1,0:T(8,128)S(1)}, f32[64,128]{1,0:T(8,128)S(1)}, u32[]{:S(2)}, u32[]{:S(2)}) collective-permute-start(f32[64,128]{1,0:T(8,128)S(1)} %slice_bitcast_fusion), channel_id=1, source_target_pairs={{0,1},{1,2},{2,3},{3,4},{4,5},{5,6},{6,7},{7,8},{8,9},{9,10},{10,1... | collective-permute-start | bytes 98312 | tf_op jit(solution)/shard_map/ppermute | solution.py:498
  52.6 1.0 %copy-start.2 = (f32[64,4096]{1,0:T(8,128)}, f32[64,4096]{1,0:T(8,128)S(1)}, u32[]{:S(2)}) copy-start(f32[64,4096]{1,0:T(8,128)S(1)} %query.1.query_hbm) | copy-start | bytes 3145732

commit v3 on v2

--- a/solution.py
+++ b/solution.py
@@ -46,26 +46,30 @@
 
 
 def load_outer(table_hbm, outer_ref, sem):
+    return [pltpu.make_async_copy(table_hbm.at[0 : 2 * R, :], outer_ref.at[:, 0 : 2 * R], sem)]
+
+
+def load_back(table_hbm, back_ref, sem):
     return [
-        pltpu.make_async_copy(table_hbm.at[0 : 2 * R, :], outer_ref.at[:, 0 : 2 * R], sem.at[0]),
-        pltpu.make_async_copy(table_hbm.at[0 : 2 * R, 0:R], outer_ref.at[:, 2 * R : 3 * R], sem.at[1]),
+        pltpu.make_async_copy(
+            table_hbm.at[(2 + i) * R : (3 + i) * R, :], back_ref.at[:, 2 * R * i : 2 * R * (i + 1)], sem.at[i]
+        )
+        for i in range(2)
     ]
 
 
-def load_back(table_hbm, back_ref, sem):
-    high, low = slice(2 * R, 3 * R), slice(3 * R, 4 * R)
-    return [
-        pltpu.make_async_copy(table_hbm.at[rows, :], back_ref.at[:, 2 * R * i : 2 * R * (i + 1)], sem.at[2 + i])
-        for i, rows in enumerate((high, low, high))
-    ]
-
-
 def load_inner(table_hbm, inner_ref, sem):
-    high, both = slice(4 * R, 6 * R), slice(4 * R, 8 * R)
-    return [
-        pltpu.make_async_copy(table_hbm.at[high, :], inner_ref.at[0 : 2 * R, :], sem.at[5]),
-        pltpu.make_async_copy(table_hbm.at[both, :], inner_ref.at[2 * R : 6 * R, :], sem.at[6]),
-    ]
+    return [pltpu.make_async_copy(table_hbm.at[4 * R : 8 * R, :], inner_ref.at[2 * R : 6 * R, :], sem)]
+
+
+def repeat_rows(ref, source, target, count):
+    for i in range(0, count, 64):
+        ref[target + i : target + i + 64, :] = ref[source + i : source + i + 64, :]
+
+
+def repeat_lanes(ref, target, count):
+    for i in range(0, ref.shape[0], 64):
+        ref[i : i + 64, target : target + count] = ref[i : i + 64, 0:count]
 
 
 def start(copies):
@@ -95,11 +99,12 @@
     return [slice(i, i + CHUNK) for i in range(0, R, CHUNK)]
 
 
-def put_column(ref, where, rows, value):
+def put_column(ref, case, rows, value):
     high, low = split(value)
     size = ref.shape[-2] // 3
+    lanes = slice(case % 2 * R, (case % 2 + 1) * R)
     for place, part in enumerate((high, high, low)):
-        ref[where, rows.start + place * size : rows.stop + place * size, :] = part
+        ref[case // 2, rows.start + place * size : rows.stop + place * size, lanes] = part
 
 
 def put_row(ref, first, rows, left, right):
@@ -110,14 +115,20 @@
         ref[rows, place * R : (place + 1) * R] = part
 
 
-def outer_stage(case, column_ref, first_ref, outer_ref, turn_ref, row_ref, base):
-    first_ref[...] = dot(outer_ref[...], column_ref[case])
-    for rows in chunks():
-        real, imag = first_ref[rows, :], first_ref[R + rows.start : R + rows.stop, :]
-        turn_real, turn_imag = turn_ref[0, rows, :], turn_ref[1, rows, :]
-        put_row(
-            row_ref, base, rows, real * turn_real - imag * turn_imag, real * turn_imag + imag * turn_real
-        )
+def outer_stage(pair, column_ref, first_ref, outer_ref, turn_ref, row_ref):
+    first_ref[...] = dot(outer_ref[...], column_ref[pair])
+    for side in range(2):
+        lanes = slice(side * R, (side + 1) * R)
+        for rows in chunks():
+            real, imag = first_ref[rows, lanes], first_ref[R + rows.start : R + rows.stop, lanes]
+            turn_real, turn_imag = turn_ref[0, rows, :], turn_ref[1, rows, :]
+            put_row(
+                row_ref,
+                (2 * pair + side) * R,
+                rows,
+                real * turn_real - imag * turn_imag,
+                real * turn_imag + imag * turn_real,
+            )
 
 
 def taps_columns(taps_ref, column_ref):
@@ -126,7 +137,9 @@
     column_ref[:, 0:16] = padded.T
 
 
-def gate_kernel(length_ref, taps_ref, features_ref, out_ref, column_ref, in_ref, send_ref, in_sem, out_sem):
+def gate_kernel(length_ref, taps_hbm, features_ref, out_ref, taps_ref, column_ref, in_ref, send_ref, in_sem, out_sem):
+    taps_copy = pltpu.make_async_copy(taps_hbm, taps_ref, in_sem.at[in_ref.shape[0]])
+    taps_copy.start()
     width = features_ref.shape[3]
     parts = in_ref.shape[0]
     group = in_ref.shape[2]
@@ -138,11 +151,10 @@
     ]
     for copy in copies:
         copy.start()
+    taps_copy.wait()
     taps_columns(taps_ref, column_ref)
-    limit = length_ref[0] - lax.axis_index("seq") * width
-    lane = lax.broadcasted_iota(jnp.int32, (8, width), 1)
-    near = lane[:, 0:128]
-    valid = lane < limit
+    limit = length_ref[...].reshape(1, 1) - lax.axis_index("seq") * width
+    near = lax.broadcasted_iota(jnp.int32, (8, 128), 1)
     sends = []
     for part in range(parts):
         copies[part].wait()
@@ -150,26 +162,41 @@
             channel = part * group + sub * 8
             column = column_ref[channel : channel + 8, :]
 
-            def stream(j):
-                here = in_ref[part, j - 1, sub * 8 : sub * 8 + 8, :]
-                one = pltpu.roll(here, 1, 1)
-                two = pltpu.roll(here, 2, 1)
-                t0, t1, t2 = (column[:, 3 * j + i : 3 * j + i + 1] for i in range(3))
-                value = t0 * here + t1 * jnp.where(lane < 1, 0.0, one) + t2 * jnp.where(lane < 2, 0.0, two)
-                over = t1 * jnp.where(near < 1, one[:, 0:128], 0.0) + t2 * jnp.where(
-                    near < 2, two[:, 0:128], 0.0
+            tap = [[jnp.broadcast_to(column[:, 3 * j + i : 3 * j + i + 1], (8, 128)) for i in range(3)] for j in (1, 2)]
+
+            def tile_of(j, tile):
+                lanes = slice(tile * 128, tile * 128 + 128)
+                return in_ref[part, j, sub * 8 : sub * 8 + 8, lanes]
+
+            last = width // 128 - 1
+            before = [tile_of(j, last) for j in range(2)]
+            turned = [[pltpu.roll(before[j], i, 1) for i in (1, 2)] for j in range(2)]
+            over = [
+                tap[j][1] * jnp.where(near < 1, turned[j][0], 0.0) + tap[j][2] * jnp.where(near < 2, turned[j][1], 0.0)
+                for j in range(2)
+            ]
+            turned = [[jnp.zeros((8, 128), F32)] * 2] * 2
+            for tile in range(width // 128):
+                values = []
+                for j in range(2):
+                    here = tile_of(j, tile)
+                    one, two = pltpu.roll(here, 1, 1), pltpu.roll(here, 2, 1)
+                    values.append(
+                        tap[j][0] * here
+                        + tap[j][1] * jnp.where(near < 1, turned[j][0], one)
+                        + tap[j][2] * jnp.where(near < 2, turned[j][1], two)
+                    )
+                    turned = [turned[i] if i != j else [one, two] for i in range(2)]
+                if tile == 0:
+                    key, value = values
+                row = channel * SPAN + (tile % 2) * 16 + tile // 2
+                send_ref[pl.ds(row, 8, stride=SPAN), :] = jnp.where(
+                    near + tile * 128 < limit, values[0] * values[1], 0.0
                 )
-                return value, over
-
-            key, key_over = stream(1)
-            value, value_over = stream(2)
-            gated = jnp.where(valid, key * value, 0.0)
-            for tile in range(width // 128):
-                row = channel * SPAN + (tile % 2) * 16 + tile // 2
-                send_ref[pl.ds(row, 8, stride=SPAN), :] = gated[:, tile * 128 : tile * 128 + 128]
+            key_over, value_over = over
             flag = jnp.where(near < limit, 1.0, 0.0)
-            edge = jnp.where(near < 2, key[:, 0:128], 0.0)
-            for place, item in ((1, value[:, 0:128]), (2, key_over), (3, value_over), (4, flag)):
+            edge = jnp.where(near < 2, key, 0.0)
+            for place, item in ((1, value), (2, key_over), (3, value_over), (4, flag)):
                 inside = (near >= 2 * place) & (near < 2 * place + 2)
                 edge = jnp.where(inside, pltpu.roll(item, 2 * place, 1), edge)
             send_ref[pl.ds(channel * SPAN + 32, 8, stride=SPAN), :] = edge
@@ -187,14 +214,15 @@
     parts = 4
     return pl.pallas_call(
         gate_kernel,
-        in_specs=[SM, VM, HB],
+        in_specs=[VM, HB, HB],
         out_specs=HB,
         out_shape=jax.ShapeDtypeStruct((channels * SPAN, 128), F32),
         scratch_shapes=[
+            pltpu.VMEM(short_filter.shape, F32),
             pltpu.VMEM((channels, 128), F32),
             pltpu.VMEM((parts, 2, channels // parts, width), F32),
             pltpu.VMEM((channels * SPAN, 128), F32),
-            pltpu.SemaphoreType.DMA((parts,)),
+            pltpu.SemaphoreType.DMA((parts + 1,)),
             pltpu.SemaphoreType.DMA((parts,)),
         ],
         compiler_params=pltpu.CompilerParams(vmem_limit_bytes=60 << 20),
@@ -228,11 +256,26 @@
 
 
 def filter_kernel(
-    skip_ref, p0, p1, p2, p3, table_hbm, turn_hbm, spec_ref, turn_ref, column_ref, first_ref, row_ref, outer_ref, inner_ref, sem
+    skip_ref,
+    p0,
+    p1,
+    p2,
+    p3,
+    table_hbm,
+    turn_hbm,
+    spec_hbm,
+    turn_ref,
+    column_ref,
+    first_ref,
+    row_ref,
+    spec_ref,
+    outer_ref,
+    inner_ref,
+    sem,
 ):
-    outer_copies = start(load_outer(table_hbm, outer_ref, sem))
-    turn_copies = start([pltpu.make_async_copy(turn_hbm, turn_ref, sem.at[7])])
-    inner_copies = start(load_inner(table_hbm, inner_ref, sem))
+    outer_copies = start(load_outer(table_hbm, outer_ref, sem.at[0]))
+    turn_copies = start([pltpu.make_async_copy(turn_hbm, turn_ref, sem.at[1])])
+    inner_copies = start(load_inner(table_hbm, inner_ref, sem.at[2]))
     y, x = lax.axis_index("y"), lax.axis_index("x_lo")
     for away, part in enumerate((p0, p1, p2, p3)):
         first = lax.rem(y + 4 - away, 4) * 64
@@ -242,43 +285,53 @@
                     high, low = split(part[channel, place, 16 * half : 16 * half + 16, :])
                     for third, piece in enumerate((high, high, low)):
                         at = pl.multiple_of(third * R + first + 32 * place + 16 * half, 16)
-                        column_ref[channel, pl.ds(at, 16), :] = piece
+                        column_ref[0, pl.ds(at, 16), channel * R : (channel + 1) * R] = piece
     finish(outer_copies + turn_copies)
+    repeat_lanes(outer_ref, 2 * R, R)
+    outer_stage(0, column_ref, first_ref, outer_ref, turn_ref, row_ref)
+    finish(inner_copies)
+    repeat_rows(inner_ref, 2 * R, 0, 2 * R)
+    sends = []
     for channel in range(2):
-        outer_stage(channel, column_ref, first_ref.at[channel], outer_ref, turn_ref, row_ref, channel * R)
-    finish(inner_copies)
-    spec = dot(row_ref[...], inner_ref[...]) * (1.0 / N)
-    for channel in range(2):
-        skip = skip_ref[2 * x + channel] * (1.0 / N)
-        spec_ref[channel, 0] = spec[channel * R : (channel + 1) * R, 0:R] + skip
-        spec_ref[channel, 1] = spec[channel * R : (channel + 1) * R, R : 2 * R]
+        spec = dot(row_ref[channel * R : (channel + 1) * R, :], inner_ref[...]) * (1.0 / N)
+        spec_ref[channel, 0] = spec[:, 0:R] + skip_ref[2 * x + channel] * (1.0 / N)
+        spec_ref[channel, 1] = spec[:, R : 2 * R]
+        sends += start(
+            [pltpu.make_async_copy(spec_ref.at[channel], spec_hbm.at[channel], sem.at[3 + channel])]
+        )
+    finish(sends)
 
 
 def filter_spectrum(skip_gain, parts, table, turn):
     return pl.pallas_call(
         filter_kernel,
         in_specs=[SM] + [VM] * 4 + [HB] * 2,
-        out_specs=[VM] * 2,
-        out_shape=[jax.ShapeDtypeStruct((2, 2, R, R), F32), jax.ShapeDtypeStruct(turn.shape, F32)],
+        out_specs=HB,
+        out_shape=jax.ShapeDtypeStruct((2, 2, R, R), F32),
         scratch_shapes=[
-            pltpu.VMEM((2, 3 * R, R), BF),
-            pltpu.VMEM((2, 2 * R, R), F32),
+            pltpu.VMEM(turn.shape, F32),
+            pltpu.VMEM((1, 3 * R, 2 * R), BF),
+            pltpu.VMEM((2 * R, 2 * R), F32),
             pltpu.VMEM((2 * R, 6 * R), BF),
+            pltpu.VMEM((2, 2, R, R), F32),
             pltpu.VMEM(*TABLES[0]),
             pltpu.VMEM(*TABLES[2]),
-            pltpu.SemaphoreType.DMA((8,)),
+            pltpu.SemaphoreType.DMA((5,)),
         ],
-        compiler_params=pltpu.CompilerParams(vmem_limit_bytes=24 << 20),
+        compiler_params=pltpu.CompilerParams(vmem_limit_bytes=40 << 20),
         name="filter_spectrum",
     )(skip_gain, *parts, table, turn)
 
 
 def conv_kernel(
+    moved_hbm,
+    spec_hbm,
+    turn_hbm,
+    table_hbm,
+    out_hbm,
     moved_ref,
     spec_ref,
     turn_ref,
-    table_hbm,
-    out_hbm,
     column_ref,
     first_ref,
     row_ref,
@@ -291,38 +344,56 @@
     sem,
     out_sem,
 ):
-    outer_copies = start(load_outer(table_hbm, outer_ref, sem))
-    inner_copies = start(load_inner(table_hbm, inner_ref, sem))
-    back_copies = start(load_back(table_hbm, back_ref, sem))
+    cut = 40
+    moved_copies = [
+        pltpu.make_async_copy(moved_hbm.at[:, rows, :], moved_ref.at[:, rows, :], sem.at[i])
+        for i, rows in enumerate((slice(0, cut), slice(cut, 2 * SPAN)))
+    ]
+    start(moved_copies[0:1])
+    outer_copies = start(load_outer(table_hbm, outer_ref, sem.at[2]))
+    turn_copies = start([pltpu.make_async_copy(turn_hbm, turn_ref, sem.at[3])])
+    start(moved_copies[1:2])
+    inner_copies = start(load_inner(table_hbm, inner_ref, sem.at[4]))
+    spec_copies = start([pltpu.make_async_copy(spec_hbm, spec_ref, sem.at[5])])
+    back_copies = start(load_back(table_hbm, back_ref, sem.at[6:8]))
     blocks = N // 4096
     lane = lax.broadcasted_iota(jnp.int32, (blocks, 128), 1)
     block = lax.broadcasted_iota(jnp.int32, (blocks, 128), 0)
-    for case in range(4):
-        rep, channel = case // 2, case % 2
+    for channel in range(2):
+        finish(moved_copies[channel : channel + 1])
         begin = channel * SPAN
-        edge = jnp.concatenate(
-            [moved_ref[2 * b + rep, begin + 32 : begin + 33, :] for b in range(blocks)], axis=0
-        )
-        behind = jnp.where(block < 1, 0.0, pltpu.roll(edge, 1, 0))
-        key = edge + pltpu.roll(behind, 124, 1)
-        value = pltpu.roll(edge, 126, 1) + pltpu.roll(behind, 122, 1)
-        mended = key * value * pltpu.roll(edge, 120, 1)
-        for b in range(blocks):
-            left = moved_ref[2 * b + rep, begin : begin + 16, :]
-            right = moved_ref[2 * b + rep, begin + 16 : begin + 32, :]
-            left = jnp.where((block < 1) & (lane < 2), mended[b : b + 1], left)
-            put_column(column_ref, case, slice(16 * b, 16 * b + 16), jnp.concatenate([left, right], axis=1))
-    finish(outer_copies)
-    for case in range(4):
-        outer_stage(case, column_ref, first_ref.at[case], outer_ref, turn_ref, row_ref, case * R)
-    finish(inner_copies)
+        for rep in range(2):
+            case = 2 * channel + rep
+            edge = jnp.concatenate(
+                [moved_ref[2 * b + rep, begin + 32 : begin + 33, :] for b in range(blocks)], axis=0
+            )
+            behind = jnp.where(block < 1, 0.0, pltpu.roll(edge, 1, 0))
+            key = edge + pltpu.roll(behind, 124, 1)
+            value = pltpu.roll(edge, 126, 1) + pltpu.roll(behind, 122, 1)
+            mended = key * value * pltpu.roll(edge, 120, 1)
+            for b in range(blocks):
+                left = moved_ref[2 * b + rep, begin : begin + 16, :]
+                right = moved_ref[2 * b + rep, begin + 16 : begin + 32, :]
+                left = jnp.where((block < 1) & (lane < 2), mended[b : b + 1], left)
+                put_column(
+                    column_ref, case, slice(16 * b, 16 * b + 16), jnp.concatenate([left, right], axis=1)
+                )
+        if channel == 0:
+            finish(outer_copies + turn_copies)
+            repeat_lanes(outer_ref, 2 * R, R)
+        outer_stage(channel, column_ref, first_ref.at[channel], outer_ref, turn_ref, row_ref)
+    finish(inner_copies + spec_copies + back_copies)
+    repeat_rows(inner_ref, 2 * R, 0, 2 * R)
+    repeat_lanes(back_ref, 4 * R, 2 * R)
     sends = []
-    size = GROUP * R
-    for group in range(4 // GROUP):
+    size = 2 * R
+    def forward_inner(group):
         every = slice(group * size, (group + 1) * size)
         mid_ref[every, :] = dot(row_ref[every, :], inner_ref[...])
-        for case in range(group * GROUP, (group + 1) * GROUP):
-            channel = case % 2
+
+    def multiply(group):
+        for case in range(2 * group, 2 * group + 2):
+            channel = case // 2
             for rows in chunks():
                 here = slice(case * R + rows.start, case * R + rows.stop)
                 real, imag = mid_ref[here, 0:R], mid_ref[here, R : 2 * R]
@@ -334,13 +405,9 @@
                     real * spec_imag + imag * spec_real,
                     real * spec_real - imag * spec_imag,
                 )
-    for group in range(4 // GROUP):
-        every = slice(group * size, (group + 1) * size)
-        mid_ref[every, :] = dot(row_ref[every, :], inner_ref[...])
-        if group == 0:
-            finish(back_copies)
-        for case in range(group * GROUP, (group + 1) * GROUP):
-            rep, channel = case // 2, case % 2
+
+    def untwist(group):
+        for case in range(2 * group, 2 * group + 2):
             for rows in chunks():
                 here = slice(case * R + rows.start, case * R + rows.stop)
                 imag, real = mid_ref[here, 0:R], mid_ref[here, R : 2 * R]
@@ -348,39 +415,52 @@
                 put_column(last_ref, case, rows, real * turn_real + imag * turn_imag)
                 below = slice(R + rows.start, R + rows.stop)
                 put_column(last_ref, case, below, imag * turn_real - real * turn_imag)
-            result = dot(back_ref[...], last_ref[case])
+
+    def backward_outer(group):
+        result = dot(back_ref[...], last_ref[group])
+        for rep in range(2):
             for half in range(2):
-                result_ref[case, :, half * 16 : half * 16 + 16, :] = result[
-                    :, half * 128 : half * 128 + 128
-                ].reshape(blocks, 16, 128)
-            sends += start(
-                [
-                    pltpu.make_async_copy(
-                        result_ref.at[case],
-                        out_hbm.reshape(16, 2, 64, 128).at[:, rep, pl.ds(channel * 32, 32), :],
-                        out_sem.at[case],
-                    )
-                ]
+                lanes = slice(rep * R + half * 128, rep * R + half * 128 + 128)
+                result_ref[group, rep, :, half * 16 : half * 16 + 16, :] = result[:, lanes].reshape(
+                    blocks, 16, 128
+                )
+            sends.extend(
+                start(
+                    [
+                        pltpu.make_async_copy(
+                            result_ref.at[group, rep],
+                            out_hbm.reshape(16, 2, 64, 128).at[:, rep, pl.ds(group * 32, 32), :],
+                            out_sem.at[2 * group + rep],
+                        )
+                    ]
+                )
             )
+
+    stages = (forward_inner, multiply, forward_inner, untwist, backward_outer)
+    groups = 2
+    for step in range(len(stages) + groups - 1):
+        for group in range(groups):
+            if 0 <= step - group < len(stages):
+                stages[step - group](group)
     finish(sends)
-
-
-GROUP = 2
 
 
 def convolve(moved, spec, turn, table):
     return pl.pallas_call(
         conv_kernel,
-        in_specs=[VM] * 3 + [HB],
+        in_specs=[HB] * 4,
         out_specs=HB,
         out_shape=jax.ShapeDtypeStruct((32, 64, 128), F32),
         scratch_shapes=[
-            pltpu.VMEM((4, 3 * R, R), BF),
-            pltpu.VMEM((4, 2 * R, R), F32),
+            pltpu.VMEM(moved.shape, F32),
+            pltpu.VMEM(spec.shape, F32),
+            pltpu.VMEM(turn.shape, F32),
+            pltpu.VMEM((2, 3 * R, 2 * R), BF),
+            pltpu.VMEM((2, 2 * R, 2 * R), F32),
             pltpu.VMEM((4 * R, 6 * R), BF),
             pltpu.VMEM((4 * R, 2 * R), F32),
-            pltpu.VMEM((4, 6 * R, R), BF),
-            pltpu.VMEM((4, 16, 32, 128), F32),
+            pltpu.VMEM((2, 6 * R, 2 * R), BF),
+            pltpu.VMEM((2, 2, 16, 32, 128), F32),
         ]
         + [pltpu.VMEM(*table_like) for table_like in TABLES]
         + [pltpu.SemaphoreType.DMA((8,)), pltpu.SemaphoreType.DMA((4,))],
@@ -389,11 +469,12 @@
     )(moved, spec, turn, table)
 
 
-def query_kernel(length_ref, taps_ref, tail_ref, features_ref, out_ref, column_ref):
+def query_kernel(length_hbm, taps_ref, tail_ref, features_ref, out_ref, length_ref, column_ref, sem):
     group, width = out_ref.shape
 
     @pl.when(pl.program_id(0) == 0)
     def _():
+        finish(start([pltpu.make_async_copy(length_hbm, length_ref, sem)]))
         taps_columns(taps_ref, column_ref)
 
     limit = length_ref[0] - lax.axis_index("seq") * width
@@ -419,10 +500,14 @@
     return pl.pallas_call(
         query_kernel,
         grid=(channels // group,),
-        in_specs=[SM, VM, VM, pl.BlockSpec((None, None, group, width), lambda i: (0, 0, i, 0))],
+        in_specs=[HB, VM, VM, pl.BlockSpec((None, None, group, width), lambda i: (0, 0, i, 0))],
         out_specs=pl.BlockSpec((group, width), lambda i: (i, 0)),
         out_shape=jax.ShapeDtypeStruct((channels, width), F32),
-        scratch_shapes=[pltpu.VMEM((channels, 128), F32)],
+        scratch_shapes=[
+            pltpu.SMEM((1,), jnp.int32),
+            pltpu.VMEM((channels, 128), F32),
+            pltpu.SemaphoreType.DMA,
+        ],
         compiler_params=pltpu.CompilerParams(vmem_limit_bytes=12 << 20),
         name="query",
     )(lengths, short_filter, tail, features)
@@ -492,7 +577,7 @@
     parts = [pair] + [
         lax.ppermute(pair, "y", [(i, (i + away) % 4) for i in range(4)]) for away in range(1, 4)
     ]
-    spec, turn = filter_spectrum(skip_gain, parts, table, turn)
+    spec = filter_spectrum(skip_gain, parts, table, turn)
     convolved = convolve(moved, spec, turn, table)
     returned = exchange(convolved)
     tail = lax.ppermute(features[0, 0, :, seq_dev - 128 :], "seq", [(i, i + 1) for i in range(n_seq - 1)])

time: 68.7 us -> 66.8 us (0.972)
  Pallas kernels: 20.8 us -> 19 us
  local copies, waits for them, and re-layouts: 2.78 us -> 1.99 us
    pallas_call x3, Pallas kernels: 15.6 us -> 13.6 us  [the longest x1 8.31 us: convolve(): pl.pallas_call(conv_kernel, in_specs=[HB] * 4, out_specs=HB, out_shape=ja...]
    unnamed x18 -> x16, local copies, waits for them, and re-layouts: 2.77 us -> 1.98 us
  transfers between devices with their start and end apart: 7 -> 7, of which waited for: 5 -> 5; matrix products, arithmetic and copies ran while one was open for 0% -> 0% of each run, Pallas kernels for 13% -> 12%
where the time goes in v3:
time: 66.8 us; the launch traced here: 65.9 us
  starting transfers between devices  22.4 us (34%)
  waiting for transfers between devices  21.7 us (32%)
  Pallas kernels  19 us (28%)
  local copies, waits for them, and re-layouts  1.99 us (3%)
  between operations  0.82 us (1%)
    all_to_all x2, waiting for transfers between devices, exchange(): lax.all_to_all(blocks, ('seq', 'x_lo'), split_axis=0, concat_axis=0, tile...  15.8 us
    all_to_all x2, starting transfers between devices, exchange(): lax.all_to_all(blocks, ('seq', 'x_lo'), split_axis=0, concat_axis=0, tile...  12.9 us
    pallas_call x1, Pallas kernels, convolve(): pl.pallas_call(conv_kernel, in_specs=[HB] * 4, out_specs=HB, out_shape=ja...  8.31 us
    ppermute x3, starting transfers between devices, body(): lax.ppermute(pair, 'y', [(i, (i + away) % 4) for i in range(4)])  5.89 us
    ppermute x3, waiting for transfers between devices, body(): lax.ppermute(pair, 'y', [(i, (i + away) % 4) for i in range(4)])  5.05 us
    pallas_call x1, Pallas kernels, gate(): pl.pallas_call(gate_kernel, in_specs=[VM, HB, HB], out_specs=HB, out_shap...  3.4 us
    pallas_call x1, Pallas kernels, filter_spectrum(): pl.pallas_call(filter_kernel, in_specs=[SM] + [VM] * 4 + [HB] * 2, out_sp...  2.77 us
    pallas_call x1, Pallas kernels, mix(): pl.pallas_call(mix_kernel, in_specs=[HB, HB], out_specs=HB, out_shape=jax...  2.48 us
  transfers between devices with their start and end apart: 7, of which 5 were waited for; matrix products, arithmetic and copies ran while one was open for 0% of the time, Pallas kernels for 12%

profile of v3, /device:TPU:0, one launch (start us, length us, event | category | flops | bytes accessed | tf_op | source)
XLA Modules:
  0.0 65.9 jit_solution(7966756856225892600)
XLA Ops:
  0.0 1.6 %collective-permute-start.1 = (f32[4,8192]{1,0:T(4,128)}, f32[4,8192]{1,0:T(4,128)S(1)}, u32[]{:S(2)}, u32[]{:S(2)}) collective-permute-start(f32[4,8192]{1,0:T(4,128)} %mine_ref.1), channel_id=1, source_target_pairs={{0,16},{16,0},{1,17},{17,1},{2,18},{18,2},{3,19},{19,3},{4,20},{20... | collective-permute-start | bytes 393224 | tf_op jit(solution)/shard_map/ppermute | solution.py:572
  2.2 0.0 copy-start.5
  2.2 3.4 %gate.1 = f32[2304,128]{1,0:T(8,128)} custom-call(s32[1]{0:T(128)S(6)} %copy.8.length_hbm.length_ref, f32[3,3,64]{2,1,0:T(4,128)} %taps_hbm.1, f32[1,3,64,4096]{3,2,1,0:T(8,128)} %features_ref.3), custom_call_target="tpu_custom_call" | custom-call | flops 1048576 | bytes 12582912 | tf_op jit(solution)/shard_map/gate/pallas_call | solution.py:215
  5.6 0.0 copy-start.1
  5.7 0.0 copy-start.4
  5.7 0.0 copy-start.7
  5.7 0.0 collective-permute-done.1.other_ref
  5.7 8.2 %all-to-all-start = ((f32[32,72,128]{2,1,0:T(8,128)}), f32[32,72,128]{2,1,0:T(8,128)}, u32[]{:S(2)}, u32[]{:S(2)}) async-start(f32[32,72,128]{2,1,0:T(8,128)} %bitcast.4), calls=%async_computation | async-start | bytes 2359296 | tf_op jit(solution)/shard_map/all_to_all | solution.py:565
  13.9 0.0 copy-done.5
  14.0 0.1 pair_up.1.p0
  14.0 1.6 %collective-permute-start.2 = (f32[2,2,32,256]{3,2,1,0:T(8,128)S(1)}, f32[2,2,32,256]{3,2,1,0:T(8,128)S(1)}, u32[]{:S(2)}, u32[]{:S(2)}) collective-permute-start(f32[2,2,32,256]{3,2,1,0:T(8,128)S(1)} %pair_up.1.p0), channel_id=1, source_target_pairs={{0,32},{32,64},{64,96},{96,0},{1,33},{33,65},{65,97},{97,1},{2,34}... | collective-permute-start | bytes 393224 | tf_op jit(solution)/shard_map/ppermute | solution.py:578
  15.7 2.9 %collective-permute-start.3 = (f32[2,2,32,256]{3,2,1,0:T(8,128)S(1)}, f32[2,2,32,256]{3,2,1,0:T(8,128)S(1)}, u32[]{:S(2)}, u32[]{:S(2)}) collective-permute-start(f32[2,2,32,256]{3,2,1,0:T(8,128)S(1)} %pair_up.1.p0), channel_id=1, source_target_pairs={{0,64},{32,96},{64,0},{96,32},{1,65},{33,97},{65,1},{97,33},{2,66}... | collective-permute-start | bytes 393224 | tf_op jit(solution)/shard_map/ppermute | solution.py:578
  18.6 1.3 %collective-permute-start.4 = (f32[2,2,32,256]{3,2,1,0:T(8,128)S(1)}, f32[2,2,32,256]{3,2,1,0:T(8,128)S(1)}, u32[]{:S(2)}, u32[]{:S(2)}) collective-permute-start(f32[2,2,32,256]{3,2,1,0:T(8,128)S(1)} %pair_up.1.p0), channel_id=1, source_target_pairs={{0,96},{32,0},{64,32},{96,64},{1,97},{33,1},{65,33},{97,65},{2,98}... | collective-permute-start | bytes 393224 | tf_op jit(solution)/shard_map/ppermute | solution.py:578
  19.9 1.1 %collective-permute-done.2.p1 = f32[2,2,32,256]{3,2,1,0:T(8,128)S(1)} collective-permute-done((f32[2,2,32,256]{3,2,1,0:T(8,128)S(1)}, f32[2,2,32,256]{3,2,1,0:T(8,128)S(1)}, u32[]{:S(2)}, u32[]{:S(2)}) %collective-permute-start.2) | collective-permute-done | bytes 131104 | tf_op jit(solution)/shard_map/ppermute | solution.py:578
  21.0 4.0 %collective-permute-done.3.p2 = f32[2,2,32,256]{3,2,1,0:T(8,128)S(1)} collective-permute-done((f32[2,2,32,256]{3,2,1,0:T(8,128)S(1)}, f32[2,2,32,256]{3,2,1,0:T(8,128)S(1)}, u32[]{:S(2)}, u32[]{:S(2)}) %collective-permute-start.3) | collective-permute-done | bytes 131104 | tf_op jit(solution)/shard_map/ppermute | solution.py:578
  25.0 0.0 collective-permute-done.4.p3
  25.0 0.0 copy-done.1
  25.0 0.0 copy-done.4
  25.0 0.0 copy-done.7
  25.0 2.8 %filter_spectrum.1.spec_hbm = f32[2,2,256,256]{3,2,1,0:T(8,128)S(1)} custom-call(f32[4]{0:T(128)S(1)} %copy-done.7, f32[2,2,32,256]{3,2,1,0:T(8,128)S(1)} %pair_up.1.p0, f32[2,2,32,256]{3,2,1,0:T(8,128)S(1)} %collective-permute-done.2.p1, f32[2,2,32,256]{3,2,1,0:T(8,128)S(1)} %collective-permute-done.3.p2, f32[2,2,32,256]{3,2,1,0:T(8,128)S(1)} %collective-permute-done.4.p3, ...), custom_call_target="tpu_custom_call" | custom-call | tf_op jit(solution)/shard_map/filter_spectrum/pallas_call | solution.py:306
  27.8 0.0 copy-start.3
  27.8 1.0 %copy-done.3 = f32[2,2,256,256]{3,2,1,0:T(8,128)} copy-done((f32[2,2,256,256]{3,2,1,0:T(8,128)}, f32[2,2,256,256]{3,2,1,0:T(8,128)S(1)}, u32[]{:S(2)}) %copy-start.3) | copy-done | bytes 1048600
  28.8 4.1 %all-to-all-done.moved_hbm = f32[32,72,128]{2,1,0:T(8,128)} async-done(((f32[32,72,128]{2,1,0:T(8,128)}), f32[32,72,128]{2,1,0:T(8,128)}, u32[]{:S(2)}, u32[]{:S(2)}) %all-to-all-start) | async-done | bytes 1179680 | tf_op jit(solution)/shard_map/all_to_all | solution.py:565
  32.9 0.0 copy-start
  32.9 8.3 %convolve.1 = f32[32,64,128]{2,1,0:T(8,128)} custom-call(f32[32,72,128]{2,1,0:T(8,128)} %all-to-all-done.moved_hbm, f32[2,2,256,256]{3,2,1,0:T(8,128)} %copy-done.3, f32[2,256,256]{2,1,0:T(8,128)} %constant.5.clone.turn_hbm, bf16[2048,512]{1,0:T(8,128)(2,1)} %constant.4.clone.table_hbm), custom_call_target="tpu_custom_call" | custom-call | tf_op jit(solution)/shard_map/convolve/pallas_call | solution.py:449
  41.2 0.0 copy-start.6
  41.2 4.7 %all-to-all-start.1 = ((f32[32,64,128]{2,1,0:T(8,128)}), f32[32,64,128]{2,1,0:T(8,128)}, u32[]{:S(2)}, u32[]{:S(2)}) async-start(f32[32,64,128]{2,1,0:T(8,128)} %convolve.1), calls=%async_computation.1 | async-start | bytes 2097152 | tf_op jit(solution)/shard_map/all_to_all | solution.py:565
  45.9 0.0 copy-done
  45.9 2.0 %collective-permute-start = (f32[64,128]{1,0:T(8,128)S(1)}, f32[64,128]{1,0:T(8,128)S(1)}, u32[]{:S(2)}, u32[]{:S(2)}) collective-permute-start(f32[64,128]{1,0:T(8,128)S(1)} %slice_bitcast_fusion), channel_id=1, source_target_pairs={{0,1},{1,2},{2,3},{3,4},{4,5},{5,6},{6,7},{7,8},{8,9},{9,10},{10,1... | collective-permute-start | bytes 98312 | tf_op jit(solution)/shard_map/ppermute | solution.py:583
  47.9 0.8 %collective-permute-done.tail_ref = f32[64,128]{1,0:T(8,128)S(1)} collective-permute-done((f32[64,128]{1,0:T(8,128)S(1)}, f32[64,128]{1,0:T(8,128)S(1)}, u32[]{:S(2)}, u32[]{:S(2)}) %collective-permute-start) | collective-permute-done | bytes 32800 | tf_op jit(solution)/shard_map/ppermute | solution.py:583
  48.8 0.0 copy-done.6
  48.8 1.9 %query.1.query_hbm = f32[64,4096]{1,0:T(8,128)S(1)} custom-call(s32[1]{0:T(128)S(6)} %copy.8.length_hbm.length_ref, f32[3,3,64]{2,1,0:T(4,128)S(1)} %copy-done.6, f32[64,128]{1,0:T(8,128)S(1)} %collective-permute-done.tail_ref, f32[1,3,64,4096]{3,2,1,0:T(8,128)S(1)} %copy-done), custom_call_target="tpu_custom_call" | custom-call | tf_op jit(solution)/shard_map/query/pallas_call | solution.py:500
  50.7 0.0 copy-start.2
  50.7 1.0 %copy-done.2 = f32[64,4096]{1,0:T(8,128)} copy-done((f32[64,4096]{1,0:T(8,128)}, f32[64,4096]{1,0:T(8,128)S(1)}, u32[]{:S(2)}) %copy-start.2) | copy-done | bytes 1048600
  51.7 11.7 %all-to-all-done.1 = f32[32,64,128]{2,1,0:T(8,128)} async-done(((f32[32,64,128]{2,1,0:T(8,128)}), f32[32,64,128]{2,1,0:T(8,128)}, u32[]{:S(2)}, u32[]{:S(2)}) %all-to-all-start.1) | async-done | bytes 1048608 | tf_op jit(solution)/shard_map/all_to_all | solution.py:565
  63.4 2.5 %mix.1 = f32[1,64,4096]{2,1,0:T(8,128)} custom-call(f32[64,4096]{1,0:T(8,128)} %copy-done.2, f32[2048,128]{1,0:T(8,128)} %bitcast.2.back_hbm), custom_call_target="tpu_custom_call" | custom-call | tf_op jit(solution)/shard_map/mix/pallas_call | solution.py:548
  (1 shorter events, 0.0 us)
Async XLA Ops:
  0.0 5.7 %collective-permute-start.1 = (f32[4,8192]{1,0:T(4,128)}, f32[4,8192]{1,0:T(4,128)S(1)}, u32[]{:S(2)}, u32[]{:S(2)}) collective-permute-start(f32[4,8192]{1,0:T(4,128)} %mine_ref.1), channel_id=1, source_target_pairs={{0,16},{16,0},{1,17},{17,1},{2,18},{18,2},{3,19},{19,3},{4,20},{20... | collective-permute-start | bytes 393224 | tf_op jit(solution)/shard_map/ppermute | solution.py:572
  2.2 11.7 %copy-start.5 = (f32[4,8192]{1,0:T(4,128)S(1)}, f32[4,8192]{1,0:T(4,128)}, u32[]{:S(2)}) copy-start(f32[4,8192]{1,0:T(4,128)} %mine_ref.1) | copy-start | bytes 393220
  5.6 19.3 %copy-start.1 = (bf16[2048,512]{1,0:T(8,128)(2,1)S(1)}, bf16[2048,512]{1,0:T(8,128)(2,1)}, u32[]{:S(2)}) copy-start(bf16[2048,512]{1,0:T(8,128)(2,1)} %constant.4.clone.table_hbm) | copy-start | bytes 6291460
  5.7 19.3 %copy-start.4 = (f32[2,256,256]{2,1,0:T(8,128)S(1)}, f32[2,256,256]{2,1,0:T(8,128)}, u32[]{:S(2)}) copy-start(f32[2,256,256]{2,1,0:T(8,128)} %constant.5.clone.turn_hbm) | copy-start | bytes 1572868
  5.7 19.3 %copy-start.7 = (f32[4]{0:T(128)S(1)}, f32[4]{0:T(128)}, u32[]{:S(2)}) copy-start(f32[4]{0:T(128)} %skip_ref.1) | copy-start | bytes 52
  5.7 27.2 %all-to-all-start = ((f32[32,72,128]{2,1,0:T(8,128)}), f32[32,72,128]{2,1,0:T(8,128)}, u32[]{:S(2)}, u32[]{:S(2)}) async-start(f32[32,72,128]{2,1,0:T(8,128)} %bitcast.4), calls=%async_computation | async-start | bytes 2359296 | tf_op jit(solution)/shard_map/all_to_all | solution.py:565
  14.0 7.0 %collective-permute-start.2 = (f32[2,2,32,256]{3,2,1,0:T(8,128)S(1)}, f32[2,2,32,256]{3,2,1,0:T(8,128)S(1)}, u32[]{:S(2)}, u32[]{:S(2)}) collective-permute-start(f32[2,2,32,256]{3,2,1,0:T(8,128)S(1)} %pair_up.1.p0), channel_id=1, source_target_pairs={{0,32},{32,64},{64,96},{96,0},{1,33},{33,65},{65,97},{97,1},{2,34}... | collective-permute-start | bytes 393224 | tf_op jit(solution)/shard_map/ppermute | solution.py:578
  15.7 9.3 %collective-permute-start.3 = (f32[2,2,32,256]{3,2,1,0:T(8,128)S(1)}, f32[2,2,32,256]{3,2,1,0:T(8,128)S(1)}, u32[]{:S(2)}, u32[]{:S(2)}) collective-permute-start(f32[2,2,32,256]{3,2,1,0:T(8,128)S(1)} %pair_up.1.p0), channel_id=1, source_target_pairs={{0,64},{32,96},{64,0},{96,32},{1,65},{33,97},{65,1},{97,33},{2,66}... | collective-permute-start | bytes 393224 | tf_op jit(solution)/shard_map/ppermute | solution.py:578
  18.6 6.4 %collective-permute-start.4 = (f32[2,2,32,256]{3,2,1,0:T(8,128)S(1)}, f32[2,2,32,256]{3,2,1,0:T(8,128)S(1)}, u32[]{:S(2)}, u32[]{:S(2)}) collective-permute-start(f32[2,2,32,256]{3,2,1,0:T(8,128)S(1)} %pair_up.1.p0), channel_id=1, source_target_pairs={{0,96},{32,0},{64,32},{96,64},{1,97},{33,1},{65,33},{97,65},{2,98}... | collective-permute-start | bytes 393224 | tf_op jit(solution)/shard_map/ppermute | solution.py:578
  27.8 1.0 %copy-start.3 = (f32[2,2,256,256]{3,2,1,0:T(8,128)}, f32[2,2,256,256]{3,2,1,0:T(8,128)S(1)}, u32[]{:S(2)}) copy-start(f32[2,2,256,256]{3,2,1,0:T(8,128)S(1)} %filter_spectrum.1.spec_hbm) | copy-start | bytes 3145732
  32.9 13.0 %copy-start = (f32[1,3,64,4096]{3,2,1,0:T(8,128)S(1)}, f32[1,3,64,4096]{3,2,1,0:T(8,128)}, u32[]{:S(2)}) copy-start(f32[1,3,64,4096]{3,2,1,0:T(8,128)} %features_ref.3) | copy-start | bytes 9437188
  41.2 7.6 %copy-start.6 = (f32[3,3,64]{2,1,0:T(4,128)S(1)}, f32[3,3,64]{2,1,0:T(4,128)}, u32[]{:S(2)}) copy-start(f32[3,3,64]{2,1,0:T(4,128)} %taps_hbm.1) | copy-start | bytes 6916
  41.2 22.2 %all-to-all-start.1 = ((f32[32,64,128]{2,1,0:T(8,128)}), f32[32,64,128]{2,1,0:T(8,128)}, u32[]{:S(2)}, u32[]{:S(2)}) async-start(f32[32,64,128]{2,1,0:T(8,128)} %convolve.1), calls=%async_computation.1 | async-start | bytes 2097152 | tf_op jit(solution)/shard_map/all_to_all | solution.py:565
  45.9 2.8 %collective-permute-start = (f32[64,128]{1,0:T(8,128)S(1)}, f32[64,128]{1,0:T(8,128)S(1)}, u32[]{:S(2)}, u32[]{:S(2)}) collective-permute-start(f32[64,128]{1,0:T(8,128)S(1)} %slice_bitcast_fusion), channel_id=1, source_target_pairs={{0,1},{1,2},{2,3},{3,4},{4,5},{5,6},{6,7},{7,8},{8,9},{9,10},{10,1... | collective-permute-start | bytes 98312 | tf_op jit(solution)/shard_map/ppermute | solution.py:583
  50.7 1.0 %copy-start.2 = (f32[64,4096]{1,0:T(8,128)}, f32[64,4096]{1,0:T(8,128)S(1)}, u32[]{:S(2)}) copy-start(f32[64,4096]{1,0:T(8,128)S(1)} %query.1.query_hbm) | copy-start | bytes 3145732

commit v4 on v3

--- a/solution.py
+++ b/solution.py
@@ -469,7 +469,7 @@
     )(moved, spec, turn, table)
 
 
-def query_kernel(length_hbm, taps_ref, tail_ref, features_ref, out_ref, length_ref, column_ref, sem):
+def query_kernel(length_hbm, taps_ref, features_ref, out_ref, edge_ref, length_ref, column_ref, sem):
     group, width = out_ref.shape
 
     @pl.when(pl.program_id(0) == 0)
@@ -482,27 +482,33 @@
     near = lane[:, 0:128]
     for sub in range(group // 8):
         rows = pl.ds(pl.multiple_of(pl.program_id(0) * group + sub * 8, 8), 8)
-        column, tail = column_ref[rows, :], tail_ref[rows, :]
+        column = column_ref[rows, :]
         here = features_ref[sub * 8 : sub * 8 + 8, :]
         t0, t1, t2 = (column[:, i : i + 1] for i in range(3))
         one = jnp.where(lane < 1, 0.0, pltpu.roll(here, 1, 1))
         two = jnp.where(lane < 2, 0.0, pltpu.roll(here, 2, 1))
         value = t0 * here + t1 * one + t2 * two
         out_ref[sub * 8 : sub * 8 + 8, :] = jnp.where(lane < limit, value, 0.0)
-        far, last = tail[:, 126:127], tail[:, 127:128]
-        mend = jnp.where(near == 0, t1 * last + t2 * far, jnp.where(near == 1, t2 * last, 0.0))
-        out_ref[sub * 8 : sub * 8 + 8, 0:128] = jnp.where(near < limit, value[:, 0:128] + mend, 0.0)
-
-
-def query(lengths, short_filter, tail, features):
+        here = slice(sub * 8, sub * 8 + 8)
+        edge_ref[here, 0:128] = jnp.where((near < 1) & (near < limit), t1, 0.0)
+        edge_ref[here, 128:256] = jnp.where((near < 2) & (near < limit), t2, 0.0)
+
+
+def query(lengths, short_filter, features):
     _, streams, channels, width = features.shape
     group = 16
     return pl.pallas_call(
         query_kernel,
         grid=(channels // group,),
-        in_specs=[HB, VM, VM, pl.BlockSpec((None, None, group, width), lambda i: (0, 0, i, 0))],
-        out_specs=pl.BlockSpec((group, width), lambda i: (i, 0)),
-        out_shape=jax.ShapeDtypeStruct((channels, width), F32),
+        in_specs=[HB, VM, pl.BlockSpec((None, None, group, width), lambda i: (0, 0, i, 0))],
+        out_specs=[
+            pl.BlockSpec((group, width), lambda i: (i, 0)),
+            pl.BlockSpec((group, 256), lambda i: (i, 0)),
+        ],
+        out_shape=[
+            jax.ShapeDtypeStruct((channels, width), F32),
+            jax.ShapeDtypeStruct((channels, 256), F32),
+        ],
         scratch_shapes=[
             pltpu.SMEM((1,), jnp.int32),
             pltpu.VMEM((channels, 128), F32),
@@ -510,13 +516,21 @@
         ],
         compiler_params=pltpu.CompilerParams(vmem_limit_bytes=12 << 20),
         name="query",
-    )(lengths, short_filter, tail, features)
-
-
-def mix_kernel(query_hbm, back_hbm, out_hbm, query_ref, back_ref, out_ref, sem):
+    )(lengths, short_filter, features)
+
+
+def mix_kernel(
+    query_hbm, edge_hbm, tail_hbm, back_hbm, out_hbm, query_ref, edge_ref, tail_ref, back_ref, out_ref, sem
+):
     channels, width = out_ref.shape
     parts = 4
     group = channels // parts
+    small = start(
+        [
+            pltpu.make_async_copy(edge_hbm, edge_ref, sem.at[3, 0]),
+            pltpu.make_async_copy(tail_hbm, tail_ref, sem.at[3, 1]),
+        ]
+    )
     loads = []
     for part in range(parts):
         rows, there = pl.ds(group * part, group), pl.ds(32 * group * part, 32 * group)
@@ -528,37 +542,44 @@
                 ]
             )
         )
+    finish(small)
     sends = []
     for part in range(parts):
         finish(loads[part])
         for sub in range(group // 8):
             channel = part * group + sub * 8
+            here = slice(channel, channel + 8)
+            tail = tail_ref[here, :]
+            mend = pltpu.roll(tail, 1, 1) * edge_ref[here, 0:128] + pltpu.roll(tail, 2, 1) * edge_ref[here, 128:256]
             for tile in range(width // 128):
                 row = channel * 32 + (tile % 2) * 16 + tile // 2
                 lanes = slice(tile * 128, tile * 128 + 128)
-                out_ref[channel : channel + 8, lanes] = (
-                    query_ref[channel : channel + 8, lanes] * back_ref[pl.ds(row, 8, stride=32), :]
-                )
+                value = query_ref[here, lanes]
+                if tile == 0:
+                    value = value + mend
+                out_ref[here, lanes] = value * back_ref[pl.ds(row, 8, stride=32), :]
         rows = pl.ds(group * part, group)
         sends += start([pltpu.make_async_copy(out_ref.at[rows, :], out_hbm.at[0, rows, :], sem.at[2, part])])
     finish(sends)
 
 
-def mix(query, returned):
+def mix(query, edge, tail, returned):
     return pl.pallas_call(
         mix_kernel,
-        in_specs=[HB, HB],
+        in_specs=[HB] * 4,
         out_specs=HB,
         out_shape=jax.ShapeDtypeStruct((1,) + query.shape, F32),
         scratch_shapes=[
             pltpu.VMEM(query.shape, F32),
+            pltpu.VMEM(edge.shape, F32),
+            pltpu.VMEM(tail.shape, F32),
             pltpu.VMEM(returned.shape, F32),
             pltpu.VMEM(query.shape, F32),
-            pltpu.SemaphoreType.DMA((3, 4)),
+            pltpu.SemaphoreType.DMA((4, 4)),
         ],
         compiler_params=pltpu.CompilerParams(vmem_limit_bytes=60 << 20),
         name="mix",
-    )(query, returned)
+    )(query, edge, tail, returned)
 
 
 def exchange(blocks):
@@ -581,7 +602,8 @@
     convolved = convolve(moved, spec, turn, table)
     returned = exchange(convolved)
     tail = lax.ppermute(features[0, 0, :, seq_dev - 128 :], "seq", [(i, i + 1) for i in range(n_seq - 1)])
-    return mix(query(lengths, short_filter, tail, features), returned.reshape(2 * n_seq * 64, 128))
+    gates, edge = query(lengths, short_filter, features)
+    return mix(gates, edge, tail, returned.reshape(2 * n_seq * 64, 128))
 
 
 def solution(mesh):

time: 66.8 us -> 66.4 us (level)
    ppermute x1, waiting for transfers between devices: 0.84 us -> 0.01 us  [body(): lax.ppermute(features[0, 0, :, seq_dev - 128:], 'seq', [(i, i + 1) for i...]
    unnamed x16 -> x20, local copies, waits for them, and re-layouts: 1.98 us -> 2.61 us
  transfers between devices with their start and end apart: 7 -> 7, of which waited for: 5 -> 4; matrix products, arithmetic and copies ran while one was open for 0% -> 0% of each run, Pallas kernels for 12% -> 12%
where the time goes in v4:
time: 66.4 us; the launch traced here: 66 us
  starting transfers between devices  22.4 us (34%)
  waiting for transfers between devices  21.3 us (32%)
  Pallas kernels  18.9 us (28%)
  local copies, waits for them, and re-layouts  2.61 us (4%)
  between operations  0.83 us (1%)
    all_to_all x2, waiting for transfers between devices, exchange(): lax.all_to_all(blocks, ('seq', 'x_lo'), split_axis=0, concat_axis=0, tile...  16.2 us
    all_to_all x2, starting transfers between devices, exchange(): lax.all_to_all(blocks, ('seq', 'x_lo'), split_axis=0, concat_axis=0, tile...  12.9 us
    pallas_call x1, Pallas kernels, convolve(): pl.pallas_call(conv_kernel, in_specs=[HB] * 4, out_specs=HB, out_shape=ja...  8.33 us
    ppermute x3, starting transfers between devices, body(): lax.ppermute(pair, 'y', [(i, (i + away) % 4) for i in range(4)])  5.89 us
    ppermute x3, waiting for transfers between devices, body(): lax.ppermute(pair, 'y', [(i, (i + away) % 4) for i in range(4)])  5.05 us
    pallas_call x1, Pallas kernels, gate(): pl.pallas_call(gate_kernel, in_specs=[VM, HB, HB], out_specs=HB, out_shap...  3.39 us
    pallas_call x1, Pallas kernels, filter_spectrum(): pl.pallas_call(filter_kernel, in_specs=[SM] + [VM] * 4 + [HB] * 2, out_sp...  2.77 us
    unnamed x20, local copies, waits for them, and re-layouts  2.61 us
  transfers between devices with their start and end apart: 7, of which 4 were waited for; matrix products, arithmetic and copies ran while one was open for 0% of the time, Pallas kernels for 12%

profile of v4, /device:TPU:0, one launch (start us, length us, event | category | flops | bytes accessed | tf_op | source)
XLA Modules:
  0.0 66.0 jit_solution(3678025608786746205)
XLA Ops:
  0.0 1.6 %collective-permute-start.1 = (f32[4,8192]{1,0:T(4,128)}, f32[4,8192]{1,0:T(4,128)S(1)}, u32[]{:S(2)}, u32[]{:S(2)}) collective-permute-start(f32[4,8192]{1,0:T(4,128)} %mine_ref.1), channel_id=1, source_target_pairs={{0,16},{16,0},{1,17},{17,1},{2,18},{18,2},{3,19},{19,3},{4,20},{20... | collective-permute-start | bytes 393224 | tf_op jit(solution)/shard_map/ppermute | solution.py:593
  2.2 0.0 copy-start.5
  2.2 3.4 %gate.1 = f32[2304,128]{1,0:T(8,128)} custom-call(s32[1]{0:T(128)S(6)} %copy.8.length_hbm.length_ref, f32[3,3,64]{2,1,0:T(4,128)} %taps_hbm.1, f32[1,3,64,4096]{3,2,1,0:T(8,128)} %features_ref.3), custom_call_target="tpu_custom_call" | custom-call | flops 1048576 | bytes 12582912 | tf_op jit(solution)/shard_map/gate/pallas_call | solution.py:215
  5.6 0.0 copy-start.1
  5.6 0.0 copy-start.3
  5.7 0.0 copy-start.8
  5.7 0.0 collective-permute-done.1.other_ref
  5.7 8.3 %all-to-all-start = ((f32[32,72,128]{2,1,0:T(8,128)}), f32[32,72,128]{2,1,0:T(8,128)}, u32[]{:S(2)}, u32[]{:S(2)}) async-start(f32[32,72,128]{2,1,0:T(8,128)} %bitcast.4), calls=%async_computation | async-start | bytes 2359296 | tf_op jit(solution)/shard_map/all_to_all | solution.py:586
  13.9 0.0 copy-done.5
  14.0 0.1 pair_up.1.p0
  14.0 1.6 %collective-permute-start.2 = (f32[2,2,32,256]{3,2,1,0:T(8,128)S(1)}, f32[2,2,32,256]{3,2,1,0:T(8,128)S(1)}, u32[]{:S(2)}, u32[]{:S(2)}) collective-permute-start(f32[2,2,32,256]{3,2,1,0:T(8,128)S(1)} %pair_up.1.p0), channel_id=1, source_target_pairs={{0,32},{32,64},{64,96},{96,0},{1,33},{33,65},{65,97},{97,1},{2,34}... | collective-permute-start | bytes 393224 | tf_op jit(solution)/shard_map/ppermute | solution.py:599
  15.7 2.9 %collective-permute-start.3 = (f32[2,2,32,256]{3,2,1,0:T(8,128)S(1)}, f32[2,2,32,256]{3,2,1,0:T(8,128)S(1)}, u32[]{:S(2)}, u32[]{:S(2)}) collective-permute-start(f32[2,2,32,256]{3,2,1,0:T(8,128)S(1)} %pair_up.1.p0), channel_id=1, source_target_pairs={{0,64},{32,96},{64,0},{96,32},{1,65},{33,97},{65,1},{97,33},{2,66}... | collective-permute-start | bytes 393224 | tf_op jit(solution)/shard_map/ppermute | solution.py:599
  18.6 1.3 %collective-permute-start.4 = (f32[2,2,32,256]{3,2,1,0:T(8,128)S(1)}, f32[2,2,32,256]{3,2,1,0:T(8,128)S(1)}, u32[]{:S(2)}, u32[]{:S(2)}) collective-permute-start(f32[2,2,32,256]{3,2,1,0:T(8,128)S(1)} %pair_up.1.p0), channel_id=1, source_target_pairs={{0,96},{32,0},{64,32},{96,64},{1,97},{33,1},{65,33},{97,65},{2,98}... | collective-permute-start | bytes 393224 | tf_op jit(solution)/shard_map/ppermute | solution.py:599
  19.9 1.1 %collective-permute-done.2.p1 = f32[2,2,32,256]{3,2,1,0:T(8,128)S(1)} collective-permute-done((f32[2,2,32,256]{3,2,1,0:T(8,128)S(1)}, f32[2,2,32,256]{3,2,1,0:T(8,128)S(1)}, u32[]{:S(2)}, u32[]{:S(2)}) %collective-permute-start.2) | collective-permute-done | bytes 131104 | tf_op jit(solution)/shard_map/ppermute | solution.py:599
  21.0 4.0 %collective-permute-done.3.p2 = f32[2,2,32,256]{3,2,1,0:T(8,128)S(1)} collective-permute-done((f32[2,2,32,256]{3,2,1,0:T(8,128)S(1)}, f32[2,2,32,256]{3,2,1,0:T(8,128)S(1)}, u32[]{:S(2)}, u32[]{:S(2)}) %collective-permute-start.3) | collective-permute-done | bytes 131104 | tf_op jit(solution)/shard_map/ppermute | solution.py:599
  25.0 0.0 collective-permute-done.4.p3
  25.0 0.0 copy-done.1
  25.0 0.0 copy-done.3
  25.0 0.0 copy-done.8
  25.0 2.8 %filter_spectrum.1.spec_hbm = f32[2,2,256,256]{3,2,1,0:T(8,128)S(1)} custom-call(f32[4]{0:T(128)S(1)} %copy-done.8, f32[2,2,32,256]{3,2,1,0:T(8,128)S(1)} %pair_up.1.p0, f32[2,2,32,256]{3,2,1,0:T(8,128)S(1)} %collective-permute-done.2.p1, f32[2,2,32,256]{3,2,1,0:T(8,128)S(1)} %collective-permute-done.3.p2, f32[2,2,32,256]{3,2,1,0:T(8,128)S(1)} %collective-permute-done.4.p3, ...), custom_call_target="tpu_custom_call" | custom-call | tf_op jit(solution)/shard_map/filter_spectrum/pallas_call | solution.py:306
  27.8 0.0 copy-start.2
  27.8 1.0 %copy-done.2 = f32[2,2,256,256]{3,2,1,0:T(8,128)} copy-done((f32[2,2,256,256]{3,2,1,0:T(8,128)}, f32[2,2,256,256]{3,2,1,0:T(8,128)S(1)}, u32[]{:S(2)}) %copy-start.2) | copy-done | bytes 1048600
  28.8 4.1 %all-to-all-done.moved_hbm = f32[32,72,128]{2,1,0:T(8,128)} async-done(((f32[32,72,128]{2,1,0:T(8,128)}), f32[32,72,128]{2,1,0:T(8,128)}, u32[]{:S(2)}, u32[]{:S(2)}) %all-to-all-start) | async-done | bytes 1179680 | tf_op jit(solution)/shard_map/all_to_all | solution.py:586
  32.9 0.0 copy-start
  32.9 8.3 %convolve.1 = f32[32,64,128]{2,1,0:T(8,128)} custom-call(f32[32,72,128]{2,1,0:T(8,128)} %all-to-all-done.moved_hbm, f32[2,2,256,256]{3,2,1,0:T(8,128)} %copy-done.2, f32[2,256,256]{2,1,0:T(8,128)} %constant.5.clone.turn_hbm, bf16[2048,512]{1,0:T(8,128)(2,1)} %constant.4.clone.table_hbm), custom_call_target="tpu_custom_call" | custom-call | tf_op jit(solution)/shard_map/convolve/pallas_call | solution.py:449
  41.2 0.0 copy-start.7
  41.2 4.7 %all-to-all-start.1 = ((f32[32,64,128]{2,1,0:T(8,128)}), f32[32,64,128]{2,1,0:T(8,128)}, u32[]{:S(2)}, u32[]{:S(2)}) async-start(f32[32,64,128]{2,1,0:T(8,128)} %convolve.1), calls=%async_computation.1 | async-start | bytes 2097152 | tf_op jit(solution)/shard_map/all_to_all | solution.py:586
  45.9 0.0 copy-done
  45.9 2.0 %collective-permute-start = (f32[64,128]{1,0:T(8,128)S(1)}, f32[64,128]{1,0:T(8,128)S(1)}, u32[]{:S(2)}, u32[]{:S(2)}) collective-permute-start(f32[64,128]{1,0:T(8,128)S(1)} %slice_bitcast_fusion), channel_id=1, source_target_pairs={{0,1},{1,2},{2,3},{3,4},{4,5},{5,6},{6,7},{7,8},{8,9},{9,10},{10,1... | collective-permute-start | bytes 98312 | tf_op jit(solution)/shard_map/ppermute | solution.py:604
  47.9 0.0 copy-done.7
  47.9 1.7 %query.1 = (f32[64,4096]{1,0:T(8,128)S(1)}, f32[64,256]{1,0:T(8,128)S(1)}) custom-call(s32[1]{0:T(128)S(6)} %copy.8.length_hbm.length_ref, f32[3,3,64]{2,1,0:T(4,128)S(1)} %copy-done.7, f32[1,3,64,4096]{3,2,1,0:T(8,128)S(1)} %copy-done), custom_call_target="tpu_custom_call" | custom-call | tf_op jit(solution)/shard_map/query/pallas_call | solution.py:500
  49.7 0.0 copy-start.4
  49.7 1.0 %copy-done.4 = f32[64,4096]{1,0:T(8,128)} copy-done((f32[64,4096]{1,0:T(8,128)}, f32[64,4096]{1,0:T(8,128)S(1)}, u32[]{:S(2)}) %copy-start.4) | copy-done | bytes 1048600
  50.7 0.0 copy-start.6
  50.7 0.6 copy-done.6
  51.3 0.0 collective-permute-done.tail_hbm
  51.3 0.0 copy-start.9
  51.3 12.1 %all-to-all-done.1 = f32[32,64,128]{2,1,0:T(8,128)} async-done(((f32[32,64,128]{2,1,0:T(8,128)}), f32[32,64,128]{2,1,0:T(8,128)}, u32[]{:S(2)}, u32[]{:S(2)}) %all-to-all-start.1) | async-done | bytes 1048608 | tf_op jit(solution)/shard_map/all_to_all | solution.py:586
  63.4 0.0 copy-done.9
  63.4 2.6 %mix.1 = f32[1,64,4096]{2,1,0:T(8,128)} custom-call(f32[64,4096]{1,0:T(8,128)} %copy-done.4, f32[64,256]{1,0:T(8,128)} %copy-done.6, f32[64,128]{1,0:T(8,128)} %copy-done.9, f32[2048,128]{1,0:T(8,128)} %bitcast.2.back_hbm), custom_call_target="tpu_custom_call" | custom-call | tf_op jit(solution)/shard_map/mix/pallas_call | solution.py:567
  (1 shorter events, 0.0 us)
Async XLA Ops:
  0.0 5.7 %collective-permute-start.1 = (f32[4,8192]{1,0:T(4,128)}, f32[4,8192]{1,0:T(4,128)S(1)}, u32[]{:S(2)}, u32[]{:S(2)}) collective-permute-start(f32[4,8192]{1,0:T(4,128)} %mine_ref.1), channel_id=1, source_target_pairs={{0,16},{16,0},{1,17},{17,1},{2,18},{18,2},{3,19},{19,3},{4,20},{20... | collective-permute-start | bytes 393224 | tf_op jit(solution)/shard_map/ppermute | solution.py:593
  2.2 11.7 %copy-start.5 = (f32[4,8192]{1,0:T(4,128)S(1)}, f32[4,8192]{1,0:T(4,128)}, u32[]{:S(2)}) copy-start(f32[4,8192]{1,0:T(4,128)} %mine_ref.1) | copy-start | bytes 393220
  5.6 19.4 %copy-start.1 = (bf16[2048,512]{1,0:T(8,128)(2,1)S(1)}, bf16[2048,512]{1,0:T(8,128)(2,1)}, u32[]{:S(2)}) copy-start(bf16[2048,512]{1,0:T(8,128)(2,1)} %constant.4.clone.table_hbm) | copy-start | bytes 6291460
  5.6 19.4 %copy-start.3 = (f32[2,256,256]{2,1,0:T(8,128)S(1)}, f32[2,256,256]{2,1,0:T(8,128)}, u32[]{:S(2)}) copy-start(f32[2,256,256]{2,1,0:T(8,128)} %constant.5.clone.turn_hbm) | copy-start | bytes 1572868
  5.7 19.3 %copy-start.8 = (f32[4]{0:T(128)S(1)}, f32[4]{0:T(128)}, u32[]{:S(2)}) copy-start(f32[4]{0:T(128)} %skip_ref.1) | copy-start | bytes 52
  5.7 27.2 %all-to-all-start = ((f32[32,72,128]{2,1,0:T(8,128)}), f32[32,72,128]{2,1,0:T(8,128)}, u32[]{:S(2)}, u32[]{:S(2)}) async-start(f32[32,72,128]{2,1,0:T(8,128)} %bitcast.4), calls=%async_computation | async-start | bytes 2359296 | tf_op jit(solution)/shard_map/all_to_all | solution.py:586
  14.0 7.0 %collective-permute-start.2 = (f32[2,2,32,256]{3,2,1,0:T(8,128)S(1)}, f32[2,2,32,256]{3,2,1,0:T(8,128)S(1)}, u32[]{:S(2)}, u32[]{:S(2)}) collective-permute-start(f32[2,2,32,256]{3,2,1,0:T(8,128)S(1)} %pair_up.1.p0), channel_id=1, source_target_pairs={{0,32},{32,64},{64,96},{96,0},{1,33},{33,65},{65,97},{97,1},{2,34}... | collective-permute-start | bytes 393224 | tf_op jit(solution)/shard_map/ppermute | solution.py:599
  15.7 9.3 %collective-permute-start.3 = (f32[2,2,32,256]{3,2,1,0:T(8,128)S(1)}, f32[2,2,32,256]{3,2,1,0:T(8,128)S(1)}, u32[]{:S(2)}, u32[]{:S(2)}) collective-permute-start(f32[2,2,32,256]{3,2,1,0:T(8,128)S(1)} %pair_up.1.p0), channel_id=1, source_target_pairs={{0,64},{32,96},{64,0},{96,32},{1,65},{33,97},{65,1},{97,33},{2,66}... | collective-permute-start | bytes 393224 | tf_op jit(solution)/shard_map/ppermute | solution.py:599
  18.6 6.4 %collective-permute-start.4 = (f32[2,2,32,256]{3,2,1,0:T(8,128)S(1)}, f32[2,2,32,256]{3,2,1,0:T(8,128)S(1)}, u32[]{:S(2)}, u32[]{:S(2)}) collective-permute-start(f32[2,2,32,256]{3,2,1,0:T(8,128)S(1)} %pair_up.1.p0), channel_id=1, source_target_pairs={{0,96},{32,0},{64,32},{96,64},{1,97},{33,1},{65,33},{97,65},{2,98}... | collective-permute-start | bytes 393224 | tf_op jit(solution)/shard_map/ppermute | solution.py:599
  27.8 1.0 %copy-start.2 = (f32[2,2,256,256]{3,2,1,0:T(8,128)}, f32[2,2,256,256]{3,2,1,0:T(8,128)S(1)}, u32[]{:S(2)}) copy-start(f32[2,2,256,256]{3,2,1,0:T(8,128)S(1)} %filter_spectrum.1.spec_hbm) | copy-start | bytes 3145732
  32.9 13.0 %copy-start = (f32[1,3,64,4096]{3,2,1,0:T(8,128)S(1)}, f32[1,3,64,4096]{3,2,1,0:T(8,128)}, u32[]{:S(2)}) copy-start(f32[1,3,64,4096]{3,2,1,0:T(8,128)} %features_ref.3) | copy-start | bytes 9437188
  41.2 6.7 %copy-start.7 = (f32[3,3,64]{2,1,0:T(4,128)S(1)}, f32[3,3,64]{2,1,0:T(4,128)}, u32[]{:S(2)}) copy-start(f32[3,3,64]{2,1,0:T(4,128)} %taps_hbm.1) | copy-start | bytes 6916
  41.2 22.2 %all-to-all-start.1 = ((f32[32,64,128]{2,1,0:T(8,128)}), f32[32,64,128]{2,1,0:T(8,128)}, u32[]{:S(2)}, u32[]{:S(2)}) async-start(f32[32,64,128]{2,1,0:T(8,128)} %convolve.1), calls=%async_computation.1 | async-start | bytes 2097152 | tf_op jit(solution)/shard_map/all_to_all | solution.py:586
  45.9 5.4 %collective-permute-start = (f32[64,128]{1,0:T(8,128)S(1)}, f32[64,128]{1,0:T(8,128)S(1)}, u32[]{:S(2)}, u32[]{:S(2)}) collective-permute-start(f32[64,128]{1,0:T(8,128)S(1)} %slice_bitcast_fusion), channel_id=1, source_target_pairs={{0,1},{1,2},{2,3},{3,4},{4,5},{5,6},{6,7},{7,8},{8,9},{9,10},{10,1... | collective-permute-start | bytes 98312 | tf_op jit(solution)/shard_map/ppermute | solution.py:604
  49.7 1.0 %copy-start.4 = (f32[64,4096]{1,0:T(8,128)}, f32[64,4096]{1,0:T(8,128)S(1)}, u32[]{:S(2)}) copy-start(f32[64,4096]{1,0:T(8,128)S(1)} %get-tuple-element.9.query_hbm) | copy-start | bytes 3145732
  50.7 0.6 copy-start.6
  51.3 12.1 %copy-start.9 = (f32[64,128]{1,0:T(8,128)}, f32[64,128]{1,0:T(8,128)S(1)}, u32[]{:S(2)}) copy-start(f32[64,128]{1,0:T(8,128)S(1)} %collective-permute-done.tail_hbm) | copy-start | bytes 98308

commit v5 on v4

--- a/solution.py
+++ b/solution.py
@@ -34,14 +34,15 @@
     twist = 2.0 * math.pi / N * np.outer(row + 0.25, row)
     turn = np.stack([np.cos(twist), -np.sin(twist)]).astype(np.float32)
     last = 2.0 * math.pi / R * np.outer(row, row)
-    inner = np.block([[np.cos(last), -np.sin(last)], [np.sin(last), np.cos(last)]])
-    return np.concatenate([halves(outer, 1), halves(outer.T, 0), halves(inner, 0)], axis=0), turn
+    cos, sin = np.cos(last), -np.sin(last)
+    inner = np.concatenate([cos, sin - cos, -cos - sin], axis=0)
+    return np.concatenate([halves(outer, 1), halves(outer.T, 0), halves(inner, 1)], axis=0), turn
 
 
 TABLES = (
     ((2 * R, 3 * R), BF),
     ((R, 6 * R), BF),
-    ((6 * R, 2 * R), BF),
+    ((3, 3 * R, R), BF),
 )
 
 
@@ -59,12 +60,19 @@
 
 
 def load_inner(table_hbm, inner_ref, sem):
-    return [pltpu.make_async_copy(table_hbm.at[4 * R : 8 * R, :], inner_ref.at[2 * R : 6 * R, :], sem)]
-
-
-def repeat_rows(ref, source, target, count):
-    for i in range(0, count, 64):
-        ref[target + i : target + i + 64, :] = ref[source + i : source + i + 64, :]
+    stack = table_hbm.reshape(7, R, 2 * R)
+    return [
+        pltpu.make_async_copy(
+            stack.at[4:7, :, i * R : (i + 1) * R], inner_ref.at[:, (i + 1) * R : (i + 2) * R, :], sem.at[i]
+        )
+        for i in range(2)
+    ]
+
+
+def repeat_inner(ref):
+    for third in range(3):
+        for i in range(0, R, 64):
+            ref[third, i : i + 64, :] = ref[third, R + i : R + i + 64, :]
 
 
 def repeat_lanes(ref, target, count):
@@ -109,10 +117,22 @@
 
 def put_row(ref, first, rows, left, right):
     rows = slice(first + rows.start, first + rows.stop)
-    left_high, left_low = split(left)
-    right_high, right_low = split(right)
-    for place, part in enumerate((left_high, right_high, left_low, right_low, left_high, right_high)):
-        ref[rows, place * R : (place + 1) * R] = part
+    for third, value in enumerate((left + right, left, right)):
+        high, low = split(value)
+        for place, part in enumerate((high, low, high)):
+            ref[rows, (3 * third + place) * R : (3 * third + place + 1) * R] = part
+
+
+def inner_stage(mid_ref, row_ref, inner_ref, every):
+    for third in range(3):
+        mid_ref[every, third * R : (third + 1) * R] = dot(
+            row_ref[every, 3 * third * R : 3 * (third + 1) * R], inner_ref[third]
+        )
+
+
+def inner_parts(mid_ref, here):
+    common = mid_ref[here, 0:R]
+    return common + mid_ref[here, 2 * R : 3 * R], common + mid_ref[here, R : 2 * R]
 
 
 def outer_stage(pair, column_ref, first_ref, outer_ref, turn_ref, row_ref):
@@ -268,6 +288,7 @@
     column_ref,
     first_ref,
     row_ref,
+    mid_ref,
     spec_ref,
     outer_ref,
     inner_ref,
@@ -275,7 +296,7 @@
 ):
     outer_copies = start(load_outer(table_hbm, outer_ref, sem.at[0]))
     turn_copies = start([pltpu.make_async_copy(turn_hbm, turn_ref, sem.at[1])])
-    inner_copies = start(load_inner(table_hbm, inner_ref, sem.at[2]))
+    inner_copies = start(load_inner(table_hbm, inner_ref, sem.at[2:4]))
     y, x = lax.axis_index("y"), lax.axis_index("x_lo")
     for away, part in enumerate((p0, p1, p2, p3)):
         first = lax.rem(y + 4 - away, 4) * 64
@@ -290,14 +311,17 @@
     repeat_lanes(outer_ref, 2 * R, R)
     outer_stage(0, column_ref, first_ref, outer_ref, turn_ref, row_ref)
     finish(inner_copies)
-    repeat_rows(inner_ref, 2 * R, 0, 2 * R)
+    repeat_inner(inner_ref)
     sends = []
     for channel in range(2):
-        spec = dot(row_ref[channel * R : (channel + 1) * R, :], inner_ref[...]) * (1.0 / N)
-        spec_ref[channel, 0] = spec[:, 0:R] + skip_ref[2 * x + channel] * (1.0 / N)
-        spec_ref[channel, 1] = spec[:, R : 2 * R]
+        inner_stage(mid_ref, row_ref, inner_ref, slice(channel * R, (channel + 1) * R))
+        skip = skip_ref[2 * x + channel]
+        for rows in chunks():
+            real, imag = inner_parts(mid_ref, slice(channel * R + rows.start, channel * R + rows.stop))
+            spec_ref[channel, 0, rows, :] = (real + skip) * (1.0 / N)
+            spec_ref[channel, 1, rows, :] = imag * (1.0 / N)
         sends += start(
-            [pltpu.make_async_copy(spec_ref.at[channel], spec_hbm.at[channel], sem.at[3 + channel])]
+            [pltpu.make_async_copy(spec_ref.at[channel], spec_hbm.at[channel], sem.at[4 + channel])]
         )
     finish(sends)
 
@@ -312,11 +336,12 @@
             pltpu.VMEM(turn.shape, F32),
             pltpu.VMEM((1, 3 * R, 2 * R), BF),
             pltpu.VMEM((2 * R, 2 * R), F32),
-            pltpu.VMEM((2 * R, 6 * R), BF),
+            pltpu.VMEM((2 * R, 9 * R), BF),
+            pltpu.VMEM((2 * R, 3 * R), F32),
             pltpu.VMEM((2, 2, R, R), F32),
             pltpu.VMEM(*TABLES[0]),
             pltpu.VMEM(*TABLES[2]),
-            pltpu.SemaphoreType.DMA((5,)),
+            pltpu.SemaphoreType.DMA((6,)),
         ],
         compiler_params=pltpu.CompilerParams(vmem_limit_bytes=40 << 20),
         name="filter_spectrum",
@@ -353,14 +378,17 @@
     outer_copies = start(load_outer(table_hbm, outer_ref, sem.at[2]))
     turn_copies = start([pltpu.make_async_copy(turn_hbm, turn_ref, sem.at[3])])
     start(moved_copies[1:2])
-    inner_copies = start(load_inner(table_hbm, inner_ref, sem.at[4]))
-    spec_copies = start([pltpu.make_async_copy(spec_hbm, spec_ref, sem.at[5])])
-    back_copies = start(load_back(table_hbm, back_ref, sem.at[6:8]))
+    inner_copies = start(load_inner(table_hbm, inner_ref, sem.at[4:6]))
+    spec_copies = start([pltpu.make_async_copy(spec_hbm, spec_ref, sem.at[6])])
+    back_copies = start(load_back(table_hbm, back_ref, sem.at[7:9]))
     blocks = N // 4096
     lane = lax.broadcasted_iota(jnp.int32, (blocks, 128), 1)
     block = lax.broadcasted_iota(jnp.int32, (blocks, 128), 0)
     for channel in range(2):
-        finish(moved_copies[channel : channel + 1])
+        finish(moved_copies[0:1] if channel == 0 else moved_copies[1:2] + inner_copies + spec_copies + back_copies)
+        if channel == 1:
+            repeat_inner(inner_ref)
+            repeat_lanes(back_ref, 4 * R, 2 * R)
         begin = channel * SPAN
         for rep in range(2):
             case = 2 * channel + rep
@@ -382,21 +410,18 @@
             finish(outer_copies + turn_copies)
             repeat_lanes(outer_ref, 2 * R, R)
         outer_stage(channel, column_ref, first_ref.at[channel], outer_ref, turn_ref, row_ref)
-    finish(inner_copies + spec_copies + back_copies)
-    repeat_rows(inner_ref, 2 * R, 0, 2 * R)
-    repeat_lanes(back_ref, 4 * R, 2 * R)
     sends = []
     size = 2 * R
     def forward_inner(group):
         every = slice(group * size, (group + 1) * size)
-        mid_ref[every, :] = dot(row_ref[every, :], inner_ref[...])
+        inner_stage(mid_ref, row_ref, inner_ref, every)
 
     def multiply(group):
         for case in range(2 * group, 2 * group + 2):
             channel = case // 2
             for rows in chunks():
                 here = slice(case * R + rows.start, case * R + rows.stop)
-                real, imag = mid_ref[here, 0:R], mid_ref[here, R : 2 * R]
+                real, imag = inner_parts(mid_ref, here)
                 spec_real, spec_imag = spec_ref[channel, 0, rows, :], spec_ref[channel, 1, rows, :]
                 put_row(
                     row_ref,
@@ -410,7 +435,7 @@
         for case in range(2 * group, 2 * group + 2):
             for rows in chunks():
                 here = slice(case * R + rows.start, case * R + rows.stop)
-                imag, real = mid_ref[here, 0:R], mid_ref[here, R : 2 * R]
+                imag, real = inner_parts(mid_ref, here)
                 turn_real, turn_imag = turn_ref[0, rows, :], turn_ref[1, rows, :]
                 put_column(last_ref, case, rows, real * turn_real + imag * turn_imag)
                 below = slice(R + rows.start, R + rows.stop)
@@ -457,13 +482,13 @@
             pltpu.VMEM(turn.shape, F32),
             pltpu.VMEM((2, 3 * R, 2 * R), BF),
             pltpu.VMEM((2, 2 * R, 2 * R), F32),
-            pltpu.VMEM((4 * R, 6 * R), BF),
-            pltpu.VMEM((4 * R, 2 * R), F32),
+            pltpu.VMEM((4 * R, 9 * R), BF),
+            pltpu.VMEM((4 * R, 3 * R), F32),
             pltpu.VMEM((2, 6 * R, 2 * R), BF),
             pltpu.VMEM((2, 2, 16, 32, 128), F32),
         ]
         + [pltpu.VMEM(*table_like) for table_like in TABLES]
-        + [pltpu.SemaphoreType.DMA((8,)), pltpu.SemaphoreType.DMA((4,))],
+        + [pltpu.SemaphoreType.DMA((9,)), pltpu.SemaphoreType.DMA((4,))],
         compiler_params=pltpu.CompilerParams(vmem_limit_bytes=60 << 20),
         name="convolve",
     )(moved, spec, turn, table)

time: 66.4 us -> 65.8 us (level)
  no operation moved by 1% of the time
where the time goes in v5:
time: 65.8 us; the launch traced here: 65.4 us
  starting transfers between devices  22.4 us (34%)
  waiting for transfers between devices  21.2 us (32%)
  Pallas kernels  18.4 us (28%)
  local copies, waits for them, and re-layouts  2.61 us (4%)
  between operations  0.83 us (1%)
    all_to_all x2, waiting for transfers between devices, exchange(): lax.all_to_all(blocks, ('seq', 'x_lo'), split_axis=0, concat_axis=0, tile...  16.1 us
    all_to_all x2, starting transfers between devices, exchange(): lax.all_to_all(blocks, ('seq', 'x_lo'), split_axis=0, concat_axis=0, tile...  12.9 us
    pallas_call x1, Pallas kernels, convolve(): pl.pallas_call(conv_kernel, in_specs=[HB] * 4, out_specs=HB, out_shape=ja...  7.76 us
    ppermute x3, starting transfers between devices, body(): lax.ppermute(pair, 'y', [(i, (i + away) % 4) for i in range(4)])  5.89 us
    ppermute x3, waiting for transfers between devices, body(): lax.ppermute(pair, 'y', [(i, (i + away) % 4) for i in range(4)])  5.05 us
    pallas_call x1, Pallas kernels, gate(): pl.pallas_call(gate_kernel, in_specs=[VM, HB, HB], out_specs=HB, out_shap...  3.39 us
    pallas_call x1, Pallas kernels, filter_spectrum(): pl.pallas_call(filter_kernel, in_specs=[SM] + [VM] * 4 + [HB] * 2, out_sp...  2.85 us
    unnamed x20, local copies, waits for them, and re-layouts  2.61 us
  transfers between devices with their start and end apart: 7, of which 4 were waited for; matrix products, arithmetic and copies ran while one was open for 0% of the time, Pallas kernels for 12%

profile of v5, /device:TPU:0, one launch (start us, length us, event | category | flops | bytes accessed | tf_op | source)
XLA Modules:
  0.0 65.4 jit_solution(10557865752211896768)
XLA Ops:
  0.0 1.6 %collective-permute-start.1 = (f32[4,8192]{1,0:T(4,128)}, f32[4,8192]{1,0:T(4,128)S(1)}, u32[]{:S(2)}, u32[]{:S(2)}) collective-permute-start(f32[4,8192]{1,0:T(4,128)} %mine_ref.1), channel_id=1, source_target_pairs={{0,16},{16,0},{1,17},{17,1},{2,18},{18,2},{3,19},{19,3},{4,20},{20... | collective-permute-start | bytes 393224 | tf_op jit(solution)/shard_map/ppermute | solution.py:618
  2.2 0.0 copy-start.5
  2.2 3.4 %gate.1 = f32[2304,128]{1,0:T(8,128)} custom-call(s32[1]{0:T(128)S(6)} %copy.8.length_hbm.length_ref, f32[3,3,64]{2,1,0:T(4,128)} %taps_hbm.1, f32[1,3,64,4096]{3,2,1,0:T(8,128)} %features_ref.3), custom_call_target="tpu_custom_call" | custom-call | flops 1048576 | bytes 12582912 | tf_op jit(solution)/shard_map/gate/pallas_call | solution.py:235
  5.6 0.0 copy-start.1
  5.6 0.0 copy-start.3
  5.7 0.0 copy-start.8
  5.7 0.0 collective-permute-done.1.other_ref
  5.7 8.3 %all-to-all-start = ((f32[32,72,128]{2,1,0:T(8,128)}), f32[32,72,128]{2,1,0:T(8,128)}, u32[]{:S(2)}, u32[]{:S(2)}) async-start(f32[32,72,128]{2,1,0:T(8,128)} %bitcast.4), calls=%async_computation | async-start | bytes 2359296 | tf_op jit(solution)/shard_map/all_to_all | solution.py:611
  13.9 0.0 copy-done.5
  14.0 0.1 pair_up.1.p0
  14.0 1.6 %collective-permute-start.2 = (f32[2,2,32,256]{3,2,1,0:T(8,128)S(1)}, f32[2,2,32,256]{3,2,1,0:T(8,128)S(1)}, u32[]{:S(2)}, u32[]{:S(2)}) collective-permute-start(f32[2,2,32,256]{3,2,1,0:T(8,128)S(1)} %pair_up.1.p0), channel_id=1, source_target_pairs={{0,32},{32,64},{64,96},{96,0},{1,33},{33,65},{65,97},{97,1},{2,34}... | collective-permute-start | bytes 393224 | tf_op jit(solution)/shard_map/ppermute | solution.py:624
  15.7 2.9 %collective-permute-start.3 = (f32[2,2,32,256]{3,2,1,0:T(8,128)S(1)}, f32[2,2,32,256]{3,2,1,0:T(8,128)S(1)}, u32[]{:S(2)}, u32[]{:S(2)}) collective-permute-start(f32[2,2,32,256]{3,2,1,0:T(8,128)S(1)} %pair_up.1.p0), channel_id=1, source_target_pairs={{0,64},{32,96},{64,0},{96,32},{1,65},{33,97},{65,1},{97,33},{2,66}... | collective-permute-start | bytes 393224 | tf_op jit(solution)/shard_map/ppermute | solution.py:624
  18.6 1.3 %collective-permute-start.4 = (f32[2,2,32,256]{3,2,1,0:T(8,128)S(1)}, f32[2,2,32,256]{3,2,1,0:T(8,128)S(1)}, u32[]{:S(2)}, u32[]{:S(2)}) collective-permute-start(f32[2,2,32,256]{3,2,1,0:T(8,128)S(1)} %pair_up.1.p0), channel_id=1, source_target_pairs={{0,96},{32,0},{64,32},{96,64},{1,97},{33,1},{65,33},{97,65},{2,98}... | collective-permute-start | bytes 393224 | tf_op jit(solution)/shard_map/ppermute | solution.py:624
  19.9 1.1 %collective-permute-done.2.p1 = f32[2,2,32,256]{3,2,1,0:T(8,128)S(1)} collective-permute-done((f32[2,2,32,256]{3,2,1,0:T(8,128)S(1)}, f32[2,2,32,256]{3,2,1,0:T(8,128)S(1)}, u32[]{:S(2)}, u32[]{:S(2)}) %collective-permute-start.2) | collective-permute-done | bytes 131104 | tf_op jit(solution)/shard_map/ppermute | solution.py:624
  21.0 4.0 %collective-permute-done.3.p2 = f32[2,2,32,256]{3,2,1,0:T(8,128)S(1)} collective-permute-done((f32[2,2,32,256]{3,2,1,0:T(8,128)S(1)}, f32[2,2,32,256]{3,2,1,0:T(8,128)S(1)}, u32[]{:S(2)}, u32[]{:S(2)}) %collective-permute-start.3) | collective-permute-done | bytes 131104 | tf_op jit(solution)/shard_map/ppermute | solution.py:624
  25.0 0.0 collective-permute-done.4.p3
  25.0 0.0 copy-done.1
  25.0 0.0 copy-done.3
  25.0 0.0 copy-done.8
  25.0 2.9 %filter_spectrum.1.spec_hbm = f32[2,2,256,256]{3,2,1,0:T(8,128)S(1)} custom-call(f32[4]{0:T(128)S(1)} %copy-done.8, f32[2,2,32,256]{3,2,1,0:T(8,128)S(1)} %pair_up.1.p0, f32[2,2,32,256]{3,2,1,0:T(8,128)S(1)} %collective-permute-done.2.p1, f32[2,2,32,256]{3,2,1,0:T(8,128)S(1)} %collective-permute-done.3.p2, f32[2,2,32,256]{3,2,1,0:T(8,128)S(1)} %collective-permute-done.4.p3, ...), custom_call_target="tpu_custom_call" | custom-call | tf_op jit(solution)/shard_map/filter_spectrum/pallas_call | solution.py:330
  27.9 0.0 copy-start.2
  27.9 1.0 %copy-done.2 = f32[2,2,256,256]{3,2,1,0:T(8,128)} copy-done((f32[2,2,256,256]{3,2,1,0:T(8,128)}, f32[2,2,256,256]{3,2,1,0:T(8,128)S(1)}, u32[]{:S(2)}) %copy-start.2) | copy-done | bytes 1048600
  28.8 4.0 %all-to-all-done.moved_hbm = f32[32,72,128]{2,1,0:T(8,128)} async-done(((f32[32,72,128]{2,1,0:T(8,128)}), f32[32,72,128]{2,1,0:T(8,128)}, u32[]{:S(2)}, u32[]{:S(2)}) %all-to-all-start) | async-done | bytes 1179680 | tf_op jit(solution)/shard_map/all_to_all | solution.py:611
  32.9 0.0 copy-start
  32.9 7.8 %convolve.1 = f32[32,64,128]{2,1,0:T(8,128)} custom-call(f32[32,72,128]{2,1,0:T(8,128)} %all-to-all-done.moved_hbm, f32[2,2,256,256]{3,2,1,0:T(8,128)} %copy-done.2, f32[2,256,256]{2,1,0:T(8,128)} %constant.5.clone.turn_hbm, bf16[1792,512]{1,0:T(8,128)(2,1)} %constant.4.clone.table_hbm), custom_call_target="tpu_custom_call" | custom-call | tf_op jit(solution)/shard_map/convolve/pallas_call | solution.py:474
  40.6 0.0 copy-start.7
  40.6 4.7 %all-to-all-start.1 = ((f32[32,64,128]{2,1,0:T(8,128)}), f32[32,64,128]{2,1,0:T(8,128)}, u32[]{:S(2)}, u32[]{:S(2)}) async-start(f32[32,64,128]{2,1,0:T(8,128)} %convolve.1), calls=%async_computation.1 | async-start | bytes 2097152 | tf_op jit(solution)/shard_map/all_to_all | solution.py:611
  45.3 0.0 copy-done
  45.4 2.0 %collective-permute-start = (f32[64,128]{1,0:T(8,128)S(1)}, f32[64,128]{1,0:T(8,128)S(1)}, u32[]{:S(2)}, u32[]{:S(2)}) collective-permute-start(f32[64,128]{1,0:T(8,128)S(1)} %slice_bitcast_fusion), channel_id=1, source_target_pairs={{0,1},{1,2},{2,3},{3,4},{4,5},{5,6},{6,7},{7,8},{8,9},{9,10},{10,1... | collective-permute-start | bytes 98312 | tf_op jit(solution)/shard_map/ppermute | solution.py:629
  47.4 0.0 copy-done.7
  47.4 1.7 %query.1 = (f32[64,4096]{1,0:T(8,128)S(1)}, f32[64,256]{1,0:T(8,128)S(1)}) custom-call(s32[1]{0:T(128)S(6)} %copy.8.length_hbm.length_ref, f32[3,3,64]{2,1,0:T(4,128)S(1)} %copy-done.7, f32[1,3,64,4096]{3,2,1,0:T(8,128)S(1)} %copy-done), custom_call_target="tpu_custom_call" | custom-call | tf_op jit(solution)/shard_map/query/pallas_call | solution.py:525
  49.1 0.0 copy-start.4
  49.1 1.0 %copy-done.4 = f32[64,4096]{1,0:T(8,128)} copy-done((f32[64,4096]{1,0:T(8,128)}, f32[64,4096]{1,0:T(8,128)S(1)}, u32[]{:S(2)}) %copy-start.4) | copy-done | bytes 1048600
  50.1 0.0 copy-start.6
  50.1 0.6 copy-done.6
  50.7 0.0 collective-permute-done.tail_hbm
  50.7 0.0 copy-start.9
  50.7 12.1 %all-to-all-done.1 = f32[32,64,128]{2,1,0:T(8,128)} async-done(((f32[32,64,128]{2,1,0:T(8,128)}), f32[32,64,128]{2,1,0:T(8,128)}, u32[]{:S(2)}, u32[]{:S(2)}) %all-to-all-start.1) | async-done | bytes 1048608 | tf_op jit(solution)/shard_map/all_to_all | solution.py:611
  62.8 0.0 copy-done.9
  62.8 2.6 %mix.1 = f32[1,64,4096]{2,1,0:T(8,128)} custom-call(f32[64,4096]{1,0:T(8,128)} %copy-done.4, f32[64,256]{1,0:T(8,128)} %copy-done.6, f32[64,128]{1,0:T(8,128)} %copy-done.9, f32[2048,128]{1,0:T(8,128)} %bitcast.2.back_hbm), custom_call_target="tpu_custom_call" | custom-call | tf_op jit(solution)/shard_map/mix/pallas_call | solution.py:592
  (1 shorter events, 0.0 us)
Async XLA Ops:
  0.0 5.7 %collective-permute-start.1 = (f32[4,8192]{1,0:T(4,128)}, f32[4,8192]{1,0:T(4,128)S(1)}, u32[]{:S(2)}, u32[]{:S(2)}) collective-permute-start(f32[4,8192]{1,0:T(4,128)} %mine_ref.1), channel_id=1, source_target_pairs={{0,16},{16,0},{1,17},{17,1},{2,18},{18,2},{3,19},{19,3},{4,20},{20... | collective-permute-start | bytes 393224 | tf_op jit(solution)/shard_map/ppermute | solution.py:618
  2.2 11.7 %copy-start.5 = (f32[4,8192]{1,0:T(4,128)S(1)}, f32[4,8192]{1,0:T(4,128)}, u32[]{:S(2)}) copy-start(f32[4,8192]{1,0:T(4,128)} %mine_ref.1) | copy-start | bytes 393220
  5.6 19.4 %copy-start.1 = (bf16[1792,512]{1,0:T(8,128)(2,1)S(1)}, bf16[1792,512]{1,0:T(8,128)(2,1)}, u32[]{:S(2)}) copy-start(bf16[1792,512]{1,0:T(8,128)(2,1)} %constant.4.clone.table_hbm) | copy-start | bytes 5505028
  5.6 19.4 %copy-start.3 = (f32[2,256,256]{2,1,0:T(8,128)S(1)}, f32[2,256,256]{2,1,0:T(8,128)}, u32[]{:S(2)}) copy-start(f32[2,256,256]{2,1,0:T(8,128)} %constant.5.clone.turn_hbm) | copy-start | bytes 1572868
  5.7 19.3 %copy-start.8 = (f32[4]{0:T(128)S(1)}, f32[4]{0:T(128)}, u32[]{:S(2)}) copy-start(f32[4]{0:T(128)} %skip_ref.1) | copy-start | bytes 52
  5.7 27.2 %all-to-all-start = ((f32[32,72,128]{2,1,0:T(8,128)}), f32[32,72,128]{2,1,0:T(8,128)}, u32[]{:S(2)}, u32[]{:S(2)}) async-start(f32[32,72,128]{2,1,0:T(8,128)} %bitcast.4), calls=%async_computation | async-start | bytes 2359296 | tf_op jit(solution)/shard_map/all_to_all | solution.py:611
  14.0 7.0 %collective-permute-start.2 = (f32[2,2,32,256]{3,2,1,0:T(8,128)S(1)}, f32[2,2,32,256]{3,2,1,0:T(8,128)S(1)}, u32[]{:S(2)}, u32[]{:S(2)}) collective-permute-start(f32[2,2,32,256]{3,2,1,0:T(8,128)S(1)} %pair_up.1.p0), channel_id=1, source_target_pairs={{0,32},{32,64},{64,96},{96,0},{1,33},{33,65},{65,97},{97,1},{2,34}... | collective-permute-start | bytes 393224 | tf_op jit(solution)/shard_map/ppermute | solution.py:624
  15.7 9.3 %collective-permute-start.3 = (f32[2,2,32,256]{3,2,1,0:T(8,128)S(1)}, f32[2,2,32,256]{3,2,1,0:T(8,128)S(1)}, u32[]{:S(2)}, u32[]{:S(2)}) collective-permute-start(f32[2,2,32,256]{3,2,1,0:T(8,128)S(1)} %pair_up.1.p0), channel_id=1, source_target_pairs={{0,64},{32,96},{64,0},{96,32},{1,65},{33,97},{65,1},{97,33},{2,66}... | collective-permute-start | bytes 393224 | tf_op jit(solution)/shard_map/ppermute | solution.py:624
  18.6 6.4 %collective-permute-start.4 = (f32[2,2,32,256]{3,2,1,0:T(8,128)S(1)}, f32[2,2,32,256]{3,2,1,0:T(8,128)S(1)}, u32[]{:S(2)}, u32[]{:S(2)}) collective-permute-start(f32[2,2,32,256]{3,2,1,0:T(8,128)S(1)} %pair_up.1.p0), channel_id=1, source_target_pairs={{0,96},{32,0},{64,32},{96,64},{1,97},{33,1},{65,33},{97,65},{2,98}... | collective-permute-start | bytes 393224 | tf_op jit(solution)/shard_map/ppermute | solution.py:624
  27.9 1.0 %copy-start.2 = (f32[2,2,256,256]{3,2,1,0:T(8,128)}, f32[2,2,256,256]{3,2,1,0:T(8,128)S(1)}, u32[]{:S(2)}) copy-start(f32[2,2,256,256]{3,2,1,0:T(8,128)S(1)} %filter_spectrum.1.spec_hbm) | copy-start | bytes 3145732
  32.9 12.5 %copy-start = (f32[1,3,64,4096]{3,2,1,0:T(8,128)S(1)}, f32[1,3,64,4096]{3,2,1,0:T(8,128)}, u32[]{:S(2)}) copy-start(f32[1,3,64,4096]{3,2,1,0:T(8,128)} %features_ref.3) | copy-start | bytes 9437188
  40.6 6.7 %copy-start.7 = (f32[3,3,64]{2,1,0:T(4,128)S(1)}, f32[3,3,64]{2,1,0:T(4,128)}, u32[]{:S(2)}) copy-start(f32[3,3,64]{2,1,0:T(4,128)} %taps_hbm.1) | copy-start | bytes 6916
  40.6 22.2 %all-to-all-start.1 = ((f32[32,64,128]{2,1,0:T(8,128)}), f32[32,64,128]{2,1,0:T(8,128)}, u32[]{:S(2)}, u32[]{:S(2)}) async-start(f32[32,64,128]{2,1,0:T(8,128)} %convolve.1), calls=%async_computation.1 | async-start | bytes 2097152 | tf_op jit(solution)/shard_map/all_to_all | solution.py:611
  45.4 5.4 %collective-permute-start = (f32[64,128]{1,0:T(8,128)S(1)}, f32[64,128]{1,0:T(8,128)S(1)}, u32[]{:S(2)}, u32[]{:S(2)}) collective-permute-start(f32[64,128]{1,0:T(8,128)S(1)} %slice_bitcast_fusion), channel_id=1, source_target_pairs={{0,1},{1,2},{2,3},{3,4},{4,5},{5,6},{6,7},{7,8},{8,9},{9,10},{10,1... | collective-permute-start | bytes 98312 | tf_op jit(solution)/shard_map/ppermute | solution.py:629
  49.1 1.0 %copy-start.4 = (f32[64,4096]{1,0:T(8,128)}, f32[64,4096]{1,0:T(8,128)S(1)}, u32[]{:S(2)}) copy-start(f32[64,4096]{1,0:T(8,128)S(1)} %get-tuple-element.9.query_hbm) | copy-start | bytes 3145732
  50.1 0.6 copy-start.6
  50.7 12.1 %copy-start.9 = (f32[64,128]{1,0:T(8,128)}, f32[64,128]{1,0:T(8,128)S(1)}, u32[]{:S(2)}) copy-start(f32[64,128]{1,0:T(8,128)S(1)} %collective-permute-done.tail_hbm) | copy-start | bytes 98308

commit v6 on v5

--- a/solution.py
+++ b/solution.py
@@ -374,8 +374,8 @@
         pltpu.make_async_copy(moved_hbm.at[:, rows, :], moved_ref.at[:, rows, :], sem.at[i])
         for i, rows in enumerate((slice(0, cut), slice(cut, 2 * SPAN)))
     ]
+    outer_copies = start(load_outer(table_hbm, outer_ref, sem.at[2]))
     start(moved_copies[0:1])
-    outer_copies = start(load_outer(table_hbm, outer_ref, sem.at[2]))
     turn_copies = start([pltpu.make_async_copy(turn_hbm, turn_ref, sem.at[3])])
     start(moved_copies[1:2])
     inner_copies = start(load_inner(table_hbm, inner_ref, sem.at[4:6]))
@@ -494,7 +494,7 @@
     )(moved, spec, turn, table)
 
 
-def query_kernel(length_hbm, taps_ref, features_ref, out_ref, edge_ref, length_ref, column_ref, sem):
+def query_kernel(length_hbm, taps_ref, features_ref, out_ref, length_ref, column_ref, sem):
     group, width = out_ref.shape
 
     @pl.when(pl.program_id(0) == 0)
@@ -514,9 +514,6 @@
         two = jnp.where(lane < 2, 0.0, pltpu.roll(here, 2, 1))
         value = t0 * here + t1 * one + t2 * two
         out_ref[sub * 8 : sub * 8 + 8, :] = jnp.where(lane < limit, value, 0.0)
-        here = slice(sub * 8, sub * 8 + 8)
-        edge_ref[here, 0:128] = jnp.where((near < 1) & (near < limit), t1, 0.0)
-        edge_ref[here, 128:256] = jnp.where((near < 2) & (near < limit), t2, 0.0)
 
 
 def query(lengths, short_filter, features):
@@ -526,85 +523,64 @@
         query_kernel,
         grid=(channels // group,),
         in_specs=[HB, VM, pl.BlockSpec((None, None, group, width), lambda i: (0, 0, i, 0))],
-        out_specs=[
-            pl.BlockSpec((group, width), lambda i: (i, 0)),
-            pl.BlockSpec((group, 256), lambda i: (i, 0)),
-        ],
-        out_shape=[
-            jax.ShapeDtypeStruct((channels, width), F32),
-            jax.ShapeDtypeStruct((channels, 256), F32),
-        ],
+        out_specs=pl.BlockSpec((None, group, width), lambda i: (0, i, 0)),
+        out_shape=jax.ShapeDtypeStruct((1, channels, width), F32),
         scratch_shapes=[
             pltpu.SMEM((1,), jnp.int32),
             pltpu.VMEM((channels, 128), F32),
             pltpu.SemaphoreType.DMA,
         ],
-        compiler_params=pltpu.CompilerParams(vmem_limit_bytes=12 << 20),
+        compiler_params=pltpu.CompilerParams(vmem_limit_bytes=60 << 20),
         name="query",
     )(lengths, short_filter, features)
 
 
-def mix_kernel(
-    query_hbm, edge_hbm, tail_hbm, back_hbm, out_hbm, query_ref, edge_ref, tail_ref, back_ref, out_ref, sem
-):
-    channels, width = out_ref.shape
+def mix_kernel(length_ref, tail_ref, query_hbm, back_ref, out_hbm, query_ref, sem):
+    channels, width = query_ref.shape
     parts = 4
     group = channels // parts
-    small = start(
-        [
-            pltpu.make_async_copy(edge_hbm, edge_ref, sem.at[3, 0]),
-            pltpu.make_async_copy(tail_hbm, tail_ref, sem.at[3, 1]),
-        ]
-    )
     loads = []
     for part in range(parts):
-        rows, there = pl.ds(group * part, group), pl.ds(32 * group * part, 32 * group)
-        loads.append(
-            start(
-                [
-                    pltpu.make_async_copy(query_hbm.at[rows, :], query_ref.at[rows, :], sem.at[0, part]),
-                    pltpu.make_async_copy(back_hbm.at[there, :], back_ref.at[there, :], sem.at[1, part]),
-                ]
-            )
-        )
-    finish(small)
+        rows = pl.ds(group * part, group)
+        loads += start([pltpu.make_async_copy(query_hbm.at[0, rows, :], query_ref.at[rows, :], sem.at[0, part])])
+    limit = length_ref[0] - lax.axis_index("seq") * width
+    near = lax.broadcasted_iota(jnp.int32, (8, 128), 1)
     sends = []
     for part in range(parts):
-        finish(loads[part])
+        finish(loads[part : part + 1])
         for sub in range(group // 8):
             channel = part * group + sub * 8
             here = slice(channel, channel + 8)
             tail = tail_ref[here, :]
-            mend = pltpu.roll(tail, 1, 1) * edge_ref[here, 0:128] + pltpu.roll(tail, 2, 1) * edge_ref[here, 128:256]
+            mend = jnp.where(near < 1, tail[:, 0:1], jnp.where(near < 2, tail[:, 1:2], 0.0))
+            mend = jnp.where(near < limit, mend, 0.0)
             for tile in range(width // 128):
                 row = channel * 32 + (tile % 2) * 16 + tile // 2
                 lanes = slice(tile * 128, tile * 128 + 128)
                 value = query_ref[here, lanes]
                 if tile == 0:
                     value = value + mend
-                out_ref[here, lanes] = value * back_ref[pl.ds(row, 8, stride=32), :]
+                query_ref[here, lanes] = value * back_ref[pl.ds(row, 8, stride=32), :]
         rows = pl.ds(group * part, group)
-        sends += start([pltpu.make_async_copy(out_ref.at[rows, :], out_hbm.at[0, rows, :], sem.at[2, part])])
+        sends += start([pltpu.make_async_copy(query_ref.at[rows, :], out_hbm.at[0, rows, :], sem.at[1, part])])
     finish(sends)
 
 
-def mix(query, edge, tail, returned):
+def mix(lengths, tail, query, returned):
+    _, channels, width = query.shape
     return pl.pallas_call(
         mix_kernel,
-        in_specs=[HB] * 4,
+        in_specs=[SM, VM, HB, VM],
         out_specs=HB,
-        out_shape=jax.ShapeDtypeStruct((1,) + query.shape, F32),
+        out_shape=jax.ShapeDtypeStruct(query.shape, F32),
+        input_output_aliases={2: 0},
         scratch_shapes=[
-            pltpu.VMEM(query.shape, F32),
-            pltpu.VMEM(edge.shape, F32),
-            pltpu.VMEM(tail.shape, F32),
-            pltpu.VMEM(returned.shape, F32),
-            pltpu.VMEM(query.shape, F32),
-            pltpu.SemaphoreType.DMA((4, 4)),
+            pltpu.VMEM((channels, width), F32),
+            pltpu.SemaphoreType.DMA((2, 4)),
         ],
-        compiler_params=pltpu.CompilerParams(vmem_limit_bytes=60 << 20),
+        compiler_params=pltpu.CompilerParams(vmem_limit_bytes=12 << 20),
         name="mix",
-    )(query, edge, tail, returned)
+    )(lengths, tail, query, returned)
 
 
 def exchange(blocks):
@@ -626,9 +602,12 @@
     spec = filter_spectrum(skip_gain, parts, table, turn)
     convolved = convolve(moved, spec, turn, table)
     returned = exchange(convolved)
-    tail = lax.ppermute(features[0, 0, :, seq_dev - 128 :], "seq", [(i, i + 1) for i in range(n_seq - 1)])
-    gates, edge = query(lengths, short_filter, features)
-    return mix(gates, edge, tail, returned.reshape(2 * n_seq * 64, 128))
+    far, last = features[0, 0, :, seq_dev - 2], features[0, 0, :, seq_dev - 1]
+    one, two = short_filter[0, 1], short_filter[0, 2]
+    over = jnp.stack([one * last + two * far, two * last], axis=1)
+    tail = lax.ppermute(over, "seq", [(i, i + 1) for i in range(n_seq - 1)])
+    gates = query(lengths, short_filter, features)
+    return mix(lengths, tail, gates, returned.reshape(2 * n_seq * 64, 128))
 
 
 def solution(mesh):

time: 65.8 us -> 65.3 us (level)
  waiting for transfers between devices: 21.2 us -> 18 us
  Pallas kernels: 18.4 us -> 20.8 us
  other arithmetic: 0 us -> 0.78 us
    all_to_all x2, waiting for transfers between devices: 16.1 us -> 12.9 us  [exchange(): lax.all_to_all(blocks, ('seq', 'x_lo'), split_axis=0, concat_axis=0, tile...]
    pallas_call x1, Pallas kernels: 1.72 us -> 4.49 us  [query(): pl.pallas_call(query_kernel, grid=(channels // group,), in_specs=[HB, VM,...]
    unnamed x20 -> x10, local copies, waits for them, and re-layouts: 2.61 us -> 0.99 us
    slice x0 -> x1, local copies, waits for them, and re-layouts: none -> 1.02 us  [body(): far, last = (features[0, 0, :, seq_dev - 2], features[0, 0, :, seq_dev - 1])]
    add x0 -> x1, other arithmetic: none -> 0.77 us  [body(): over = jnp.stack([one * last + two * far, two * last], axis=1)]
  transfers between devices with their start and end apart: 7 -> 7, of which waited for: 4 -> 4; matrix products, arithmetic and copies ran while one was open for 0% -> 3% of each run, Pallas kernels for 12% -> 17%
where the time goes in v6:
time: 65.3 us; the launch traced here: 64.7 us
  starting transfers between devices  22.3 us (34%)
  Pallas kernels  20.8 us (32%)
  waiting for transfers between devices  18 us (28%)
  local copies, waits for them, and re-layouts  2.11 us (3%)
  between operations  0.8 us (1%)
  other arithmetic  0.78 us (1%)
    all_to_all x2, waiting for transfers between devices, exchange(): lax.all_to_all(blocks, ('seq', 'x_lo'), split_axis=0, concat_axis=0, tile...  12.9 us
    all_to_all x2, starting transfers between devices, exchange(): lax.all_to_all(blocks, ('seq', 'x_lo'), split_axis=0, concat_axis=0, tile...  12.6 us
    pallas_call x1, Pallas kernels, convolve(): pl.pallas_call(conv_kernel, in_specs=[HB] * 4, out_specs=HB, out_shape=ja...  7.59 us
    ppermute x3, starting transfers between devices, body(): lax.ppermute(pair, 'y', [(i, (i + away) % 4) for i in range(4)])  5.89 us
    ppermute x3, waiting for transfers between devices, body(): lax.ppermute(pair, 'y', [(i, (i + away) % 4) for i in range(4)])  5.05 us
    pallas_call x1, Pallas kernels, query(): pl.pallas_call(query_kernel, grid=(channels // group,), in_specs=[HB, VM,...  4.49 us
    pallas_call x1, Pallas kernels, gate(): pl.pallas_call(gate_kernel, in_specs=[VM, HB, HB], out_specs=HB, out_shap...  3.39 us
    pallas_call x1, Pallas kernels, filter_spectrum(): pl.pallas_call(filter_kernel, in_specs=[SM] + [VM] * 4 + [HB] * 2, out_sp...  2.85 us
  transfers between devices with their start and end apart: 7, of which 4 were waited for; matrix products, arithmetic and copies ran while one was open for 3% of the time, Pallas kernels for 17%

profile of v6, /device:TPU:0, one launch (start us, length us, event | category | flops | bytes accessed | tf_op | source)
XLA Modules:
  0.0 64.7 jit_solution(7932012765073505451)
XLA Ops:
  0.0 1.6 %collective-permute-start.1 = (f32[4,8192]{1,0:T(4,128)}, f32[4,8192]{1,0:T(4,128)S(1)}, u32[]{:S(2)}, u32[]{:S(2)}) collective-permute-start(f32[4,8192]{1,0:T(4,128)} %mine_ref.1), channel_id=1, source_target_pairs={{0,16},{16,0},{1,17},{17,1},{2,18},{18,2},{3,19},{19,3},{4,20},{20... | collective-permute-start | bytes 393224 | tf_op jit(solution)/shard_map/ppermute | solution.py:594
  2.2 0.0 copy-start.3
  2.2 3.4 %gate.1 = f32[2304,128]{1,0:T(8,128)} custom-call(s32[1]{0:T(128)S(6)} %copy.23.length_hbm.length_ref, f32[3,3,64]{2,1,0:T(4,128)} %taps_hbm.1, f32[1,3,64,4096]{3,2,1,0:T(8,128)} %features_ref.3), custom_call_target="tpu_custom_call" | custom-call | flops 1048576 | bytes 12582912 | tf_op jit(solution)/shard_map/gate/pallas_call | solution.py:235
  5.6 0.0 copy-start
  5.6 0.0 copy-start.2
  5.7 0.0 copy-start.4
  5.7 0.0 collective-permute-done.1.other_ref
  5.7 8.3 %all-to-all-start = ((f32[32,72,128]{2,1,0:T(8,128)}), f32[32,72,128]{2,1,0:T(8,128)}, u32[]{:S(2)}, u32[]{:S(2)}) async-start(f32[32,72,128]{2,1,0:T(8,128)} %bitcast.17), calls=%async_computation | async-start | bytes 2359296 | tf_op jit(solution)/shard_map/all_to_all | solution.py:587
  13.9 0.0 copy-done.3
  14.0 0.1 pair_up.1.p0
  14.0 1.6 %collective-permute-start.2 = (f32[2,2,32,256]{3,2,1,0:T(8,128)S(1)}, f32[2,2,32,256]{3,2,1,0:T(8,128)S(1)}, u32[]{:S(2)}, u32[]{:S(2)}) collective-permute-start(f32[2,2,32,256]{3,2,1,0:T(8,128)S(1)} %pair_up.1.p0), channel_id=1, source_target_pairs={{0,32},{32,64},{64,96},{96,0},{1,33},{33,65},{65,97},{97,1},{2,34}... | collective-permute-start | bytes 393224 | tf_op jit(solution)/shard_map/ppermute | solution.py:600
  15.7 2.9 %collective-permute-start.3 = (f32[2,2,32,256]{3,2,1,0:T(8,128)S(1)}, f32[2,2,32,256]{3,2,1,0:T(8,128)S(1)}, u32[]{:S(2)}, u32[]{:S(2)}) collective-permute-start(f32[2,2,32,256]{3,2,1,0:T(8,128)S(1)} %pair_up.1.p0), channel_id=1, source_target_pairs={{0,64},{32,96},{64,0},{96,32},{1,65},{33,97},{65,1},{97,33},{2,66}... | collective-permute-start | bytes 393224 | tf_op jit(solution)/shard_map/ppermute | solution.py:600
  18.6 1.3 %collective-permute-start.4 = (f32[2,2,32,256]{3,2,1,0:T(8,128)S(1)}, f32[2,2,32,256]{3,2,1,0:T(8,128)S(1)}, u32[]{:S(2)}, u32[]{:S(2)}) collective-permute-start(f32[2,2,32,256]{3,2,1,0:T(8,128)S(1)} %pair_up.1.p0), channel_id=1, source_target_pairs={{0,96},{32,0},{64,32},{96,64},{1,97},{33,1},{65,33},{97,65},{2,98}... | collective-permute-start | bytes 393224 | tf_op jit(solution)/shard_map/ppermute | solution.py:600
  19.9 1.1 %collective-permute-done.2.p1 = f32[2,2,32,256]{3,2,1,0:T(8,128)S(1)} collective-permute-done((f32[2,2,32,256]{3,2,1,0:T(8,128)S(1)}, f32[2,2,32,256]{3,2,1,0:T(8,128)S(1)}, u32[]{:S(2)}, u32[]{:S(2)}) %collective-permute-start.2) | collective-permute-done | bytes 131104 | tf_op jit(solution)/shard_map/ppermute | solution.py:600
  21.0 4.0 %collective-permute-done.3.p2 = f32[2,2,32,256]{3,2,1,0:T(8,128)S(1)} collective-permute-done((f32[2,2,32,256]{3,2,1,0:T(8,128)S(1)}, f32[2,2,32,256]{3,2,1,0:T(8,128)S(1)}, u32[]{:S(2)}, u32[]{:S(2)}) %collective-permute-start.3) | collective-permute-done | bytes 131104 | tf_op jit(solution)/shard_map/ppermute | solution.py:600
  25.0 0.0 collective-permute-done.4.p3
  25.0 0.0 copy-done
  25.0 0.0 copy-done.2
  25.0 0.0 copy-done.4
  25.0 2.9 %filter_spectrum.1.spec_hbm = f32[2,2,256,256]{3,2,1,0:T(8,128)S(1)} custom-call(f32[4]{0:T(128)S(1)} %copy-done.4, f32[2,2,32,256]{3,2,1,0:T(8,128)S(1)} %pair_up.1.p0, f32[2,2,32,256]{3,2,1,0:T(8,128)S(1)} %collective-permute-done.2.p1, f32[2,2,32,256]{3,2,1,0:T(8,128)S(1)} %collective-permute-done.3.p2, f32[2,2,32,256]{3,2,1,0:T(8,128)S(1)} %collective-permute-done.4.p3, ...), custom_call_target="tpu_custom_call" | custom-call | tf_op jit(solution)/shard_map/filter_spectrum/pallas_call | solution.py:330
  27.9 0.0 copy-start.1
  27.9 1.0 %copy-done.1 = f32[2,2,256,256]{3,2,1,0:T(8,128)} copy-done((f32[2,2,256,256]{3,2,1,0:T(8,128)}, f32[2,2,256,256]{3,2,1,0:T(8,128)S(1)}, u32[]{:S(2)}) %copy-start.1) | copy-done | bytes 1048600
  28.8 4.0 %all-to-all-done.moved_hbm = f32[32,72,128]{2,1,0:T(8,128)} async-done(((f32[32,72,128]{2,1,0:T(8,128)}), f32[32,72,128]{2,1,0:T(8,128)}, u32[]{:S(2)}, u32[]{:S(2)}) %all-to-all-start) | async-done | bytes 1179680 | tf_op jit(solution)/shard_map/all_to_all | solution.py:587
  32.9 7.6 %convolve.1 = f32[32,64,128]{2,1,0:T(8,128)} custom-call(f32[32,72,128]{2,1,0:T(8,128)} %all-to-all-done.moved_hbm, f32[2,2,256,256]{3,2,1,0:T(8,128)} %copy-done.1, f32[2,256,256]{2,1,0:T(8,128)} %constant.5.clone.turn_hbm, bf16[1792,512]{1,0:T(8,128)(2,1)} %constant.4.clone.table_hbm), custom_call_target="tpu_custom_call" | custom-call | tf_op jit(solution)/shard_map/convolve/pallas_call | solution.py:474
  40.5 4.4 %all-to-all-start.1 = ((f32[32,64,128]{2,1,0:T(8,128)}), f32[32,64,128]{2,1,0:T(8,128)S(1)}, u32[]{:S(2)}, u32[]{:S(2)}) async-start(f32[32,64,128]{2,1,0:T(8,128)} %convolve.1), calls=%async_computation.1 | async-start | bytes 2097152 | tf_op jit(solution)/shard_map/all_to_all | solution.py:587
  44.8 1.0 %slice_reduce_fusion = (f32[64]{0:T(128)S(1)}, f32[64]{0:T(128)S(1)}) fusion(f32[1,3,64,4096]{3,2,1,0:T(8,128)} %features_ref.3), kind=kLoop, calls=%fused_computation | loop fusion | bytes 1024 | tf_op jit(solution)/shard_map/slice | solution.py:605
  45.9 0.8 %fusion = (f32[64,1]{0,1:T(1,128)S(1)}, f32[64,1]{0,1:T(1,128)S(1)}) fusion(f32[64]{0:T(128)S(1)} %get-tuple-element.9, f32[64]{0:T(128)S(1)} %get-tuple-element.10, f32[3,3,64]{2,1,0:T(4,128)} %taps_hbm.1), kind=kLoop, calls=%fused_computation.4 | loop fusion | flops 256 | bytes 1536 | tf_op jit(solution)/shard_map/add | solution.py:607
  46.7 0.1 copy.21
  46.8 2.2 %collective-permute-start = (f32[64,2]{1,0:T(8,128)S(1)}, f32[64,2]{1,0:T(8,128)S(1)}, u32[]{:S(2)}, u32[]{:S(2)}) collective-permute-start(f32[64,2]{1,0:T(8,128)S(1)} %copy.21), channel_id=1, source_target_pairs={{0,1},{1,2},{2,3},{3,4},{4,5},{5,6},{6,7},{7,8},{8,9},{9,10},{10,1... | collective-permute-start | bytes 1544 | tf_op jit(solution)/shard_map/ppermute | solution.py:608
  48.9 4.5 %query.1.query_hbm = f32[1,64,4096]{2,1,0:T(8,128)} custom-call(s32[1]{0:T(128)S(6)} %copy.23.length_hbm.length_ref, f32[3,3,64]{2,1,0:T(4,128)} %taps_hbm.1, f32[1,3,64,4096]{3,2,1,0:T(8,128)} %features_ref.3), custom_call_target="tpu_custom_call" | custom-call | tf_op jit(solution)/shard_map/query/pallas_call | solution.py:522
  53.4 0.0 collective-permute-done.tail_ref
  53.4 8.9 %all-to-all-done.1 = f32[32,64,128]{2,1,0:T(8,128)S(1)} async-done(((f32[32,64,128]{2,1,0:T(8,128)}), f32[32,64,128]{2,1,0:T(8,128)S(1)}, u32[]{:S(2)}, u32[]{:S(2)}) %all-to-all-start.1) | async-done | bytes 1048608 | tf_op jit(solution)/shard_map/all_to_all | solution.py:587
  62.4 2.4 %mix.1 = f32[1,64,4096]{2,1,0:T(8,128)} custom-call(s32[1]{0:T(128)S(6)} %copy.23.length_hbm.length_ref, f32[64,2]{1,0:T(8,128)S(1)} %collective-permute-done.tail_ref, f32[1,64,4096]{2,1,0:T(8,128)} %query.1.query_hbm, f32[2048,128]{1,0:T(8,128)S(1)} %bitcast.16), custom_call_target="tpu_custom_call", output_to_operand_aliasing={{}: (2, {})} | custom-call | tf_op jit(solution)/shard_map/mix/pallas_call | solution.py:571
  (1 shorter events, 0.0 us)
Async XLA Ops:
  0.0 5.7 %collective-permute-start.1 = (f32[4,8192]{1,0:T(4,128)}, f32[4,8192]{1,0:T(4,128)S(1)}, u32[]{:S(2)}, u32[]{:S(2)}) collective-permute-start(f32[4,8192]{1,0:T(4,128)} %mine_ref.1), channel_id=1, source_target_pairs={{0,16},{16,0},{1,17},{17,1},{2,18},{18,2},{3,19},{19,3},{4,20},{20... | collective-permute-start | bytes 393224 | tf_op jit(solution)/shard_map/ppermute | solution.py:594
  2.2 11.7 %copy-start.3 = (f32[4,8192]{1,0:T(4,128)S(1)}, f32[4,8192]{1,0:T(4,128)}, u32[]{:S(2)}) copy-start(f32[4,8192]{1,0:T(4,128)} %mine_ref.1) | copy-start | bytes 393220
  5.6 19.4 %copy-start = (bf16[1792,512]{1,0:T(8,128)(2,1)S(1)}, bf16[1792,512]{1,0:T(8,128)(2,1)}, u32[]{:S(2)}) copy-start(bf16[1792,512]{1,0:T(8,128)(2,1)} %constant.4.clone.table_hbm) | copy-start | bytes 5505028
  5.6 19.4 %copy-start.2 = (f32[2,256,256]{2,1,0:T(8,128)S(1)}, f32[2,256,256]{2,1,0:T(8,128)}, u32[]{:S(2)}) copy-start(f32[2,256,256]{2,1,0:T(8,128)} %constant.5.clone.turn_hbm) | copy-start | bytes 1572868
  5.7 19.3 %copy-start.4 = (f32[4]{0:T(128)S(1)}, f32[4]{0:T(128)}, u32[]{:S(2)}) copy-start(f32[4]{0:T(128)} %skip_ref.1) | copy-start | bytes 52
  5.7 27.2 %all-to-all-start = ((f32[32,72,128]{2,1,0:T(8,128)}), f32[32,72,128]{2,1,0:T(8,128)}, u32[]{:S(2)}, u32[]{:S(2)}) async-start(f32[32,72,128]{2,1,0:T(8,128)} %bitcast.17), calls=%async_computation | async-start | bytes 2359296 | tf_op jit(solution)/shard_map/all_to_all | solution.py:587
  14.0 7.0 %collective-permute-start.2 = (f32[2,2,32,256]{3,2,1,0:T(8,128)S(1)}, f32[2,2,32,256]{3,2,1,0:T(8,128)S(1)}, u32[]{:S(2)}, u32[]{:S(2)}) collective-permute-start(f32[2,2,32,256]{3,2,1,0:T(8,128)S(1)} %pair_up.1.p0), channel_id=1, source_target_pairs={{0,32},{32,64},{64,96},{96,0},{1,33},{33,65},{65,97},{97,1},{2,34}... | collective-permute-start | bytes 393224 | tf_op jit(solution)/shard_map/ppermute | solution.py:600
  15.7 9.3 %collective-permute-start.3 = (f32[2,2,32,256]{3,2,1,0:T(8,128)S(1)}, f32[2,2,32,256]{3,2,1,0:T(8,128)S(1)}, u32[]{:S(2)}, u32[]{:S(2)}) collective-permute-start(f32[2,2,32,256]{3,2,1,0:T(8,128)S(1)} %pair_up.1.p0), channel_id=1, source_target_pairs={{0,64},{32,96},{64,0},{96,32},{1,65},{33,97},{65,1},{97,33},{2,66}... | collective-permute-start | bytes 393224 | tf_op jit(solution)/shard_map/ppermute | solution.py:600
  18.6 6.4 %collective-permute-start.4 = (f32[2,2,32,256]{3,2,1,0:T(8,128)S(1)}, f32[2,2,32,256]{3,2,1,0:T(8,128)S(1)}, u32[]{:S(2)}, u32[]{:S(2)}) collective-permute-start(f32[2,2,32,256]{3,2,1,0:T(8,128)S(1)} %pair_up.1.p0), channel_id=1, source_target_pairs={{0,96},{32,0},{64,32},{96,64},{1,97},{33,1},{65,33},{97,65},{2,98}... | collective-permute-start | bytes 393224 | tf_op jit(solution)/shard_map/ppermute | solution.py:600
  27.9 1.0 %copy-start.1 = (f32[2,2,256,256]{3,2,1,0:T(8,128)}, f32[2,2,256,256]{3,2,1,0:T(8,128)S(1)}, u32[]{:S(2)}) copy-start(f32[2,2,256,256]{3,2,1,0:T(8,128)S(1)} %filter_spectrum.1.spec_hbm) | copy-start | bytes 3145732
  40.5 21.9 %all-to-all-start.1 = ((f32[32,64,128]{2,1,0:T(8,128)}), f32[32,64,128]{2,1,0:T(8,128)S(1)}, u32[]{:S(2)}, u32[]{:S(2)}) async-start(f32[32,64,128]{2,1,0:T(8,128)} %convolve.1), calls=%async_computation.1 | async-start | bytes 2097152 | tf_op jit(solution)/shard_map/all_to_all | solution.py:587
  46.8 6.7 %collective-permute-start = (f32[64,2]{1,0:T(8,128)S(1)}, f32[64,2]{1,0:T(8,128)S(1)}, u32[]{:S(2)}, u32[]{:S(2)}) collective-permute-start(f32[64,2]{1,0:T(8,128)S(1)} %copy.21), channel_id=1, source_target_pairs={{0,1},{1,2},{2,3},{3,4},{4,5},{5,6},{6,7},{7,8},{8,9},{9,10},{10,1... | collective-permute-start | bytes 1544 | tf_op jit(solution)/shard_map/ppermute | solution.py:608
